TPU v7x, 128 devices: a whole 4x4x4 slice. The times are simulated.
128 devices in a mesh: fsdp: 16 (over x_lo, y, core), tp: 8 (over x_hi, z).
Axes of the slice: x: 4 (x_hi: 2, x_lo: 2; x = x_hi * 2 + x_lo), y: 4, z: 4, core: 2. Of those that a mesh axis runs over, the one named last changes fastest.
Arguments:
- tokens: bfloat16 [16384, 2048], P(('fsdp', 'tp')), may hold values from -6 to 6
- grad_out: bfloat16 [16384, 2048], P(('fsdp', 'tp')), may hold values from -6 to 6
- adapter_ids: int32 [16], P('fsdp'), may hold values from 0 to 7
- first_gain: float32 [2048], replicated, may hold values from 0.1 to 1.9
- first_shift: float32 [2048], replicated, may hold values from -4 to 4
- joined_weight: bfloat16 [2048, 6144], P('fsdp', 'tp'), may hold values from -0.125 to 0.125
- joined_bias: float32 [6144], P('tp'), may hold values from -4 to 4
- dense_weight: bfloat16 [2048, 2048], P('tp', 'fsdp'), may hold values from -0.5 to 0.5
- dense_bias: float32 [2048], replicated, may hold values from -4 to 4
- second_gain: float32 [2048], replicated, may hold values from 0.1 to 1.9
- second_shift: float32 [2048], replicated, may hold values from -4 to 4
- up_weight: bfloat16 [2048, 8192], P('fsdp', 'tp'), may hold values from -0.125 to 0.125
- up_bias: float32 [8192], P('tp'), may hold values from -6 to 6
- down_weight: bfloat16 [8192, 2048], P('tp', 'fsdp'), may hold values from -0.125 to 0.125
- down_bias: float32 [2048], replicated, may hold values from -4 to 4
- joined_adapt_in: bfloat16 [8, 2048, 16], replicated, may hold values from -0.125 to 0.125
- joined_adapt_out: bfloat16 [8, 16, 6144], P(None, None, 'tp'), may hold values from -2 to 2
- dense_adapt_in: bfloat16 [8, 2048, 16], P(None, 'tp'), may hold values from -0.5 to 0.5
- dense_adapt_out: bfloat16 [8, 16, 2048], replicated, may hold values from -2 to 2
- up_adapt_in: bfloat16 [8, 2048, 16], replicated, may hold values from -0.125 to 0.125
- up_adapt_out: bfloat16 [8, 16, 8192], P(None, None, 'tp'), may hold values from -2 to 2
- down_adapt_in: bfloat16 [8, 8192, 16], P(None, 'tp'), may hold values from -0.125 to 0.125
- down_adapt_out: bfloat16 [8, 16, 2048], replicated, may hold values from -2 to 2
Outputs:
- layer_out: bfloat16 [16384, 2048], P(('fsdp', 'tp'))
- grad_tokens: float32 [16384, 2048], P(('fsdp', 'tp'))
- grad_joined_in: float32 [8, 2048, 16], replicated
- grad_joined_out: float32 [8, 16, 6144], P(None, None, 'tp')
- grad_dense_in: float32 [8, 2048, 16], P(None, 'tp')
- grad_dense_out: float32 [8, 16, 2048], replicated
- grad_up_in: float32 [8, 2048, 16], replicated
- grad_up_out: float32 [8, 16, 8192], P(None, None, 'tp')
- grad_down_in: float32 [8, 8192, 16], P(None, 'tp')
- grad_down_out: float32 [8, 16, 2048], replicated
All inputs are finite; a program needn't handle non-finite values.
Results may differ from a plain program's by a relative error of at most 0.02.
Values may be sent and summed in bfloat16 or wider, within the bound.
A program may use at most 128 MiB of HBM per device.

v0:
```python
import jax
import jax.numpy as jnp
from jax import lax
from jax.sharding import PartitionSpec as P

HEADS = 32
HEAD_DIM = 64


EPSILON = 1e-05
MASKED = -1e30
HIGHEST = lax.Precision.HIGHEST


def split_up(value, dim, size):
    before, after = (value.shape[:dim], value.shape[dim + 1 :])
    return jnp.moveaxis(value.reshape(*before, size, -1, *after), dim, 0)


def sum_at_owner(value, axis, dim):
    blocks = split_up(value, dim, lax.axis_size(axis))
    arrived = lax.all_to_all(blocks, axis, split_axis=0, concat_axis=0, tiled=True)
    return arrived.astype(jnp.float32).sum(axis=0)


def together(arrays, axis):
    ends = [0]
    for a in arrays:
        ends.append(ends[-1] + a.size)
    so_far = lax.psum(jnp.concatenate([a.ravel() for a in arrays]), axis)
    return tuple((so_far[b:e].reshape(a.shape) for a, b, e in zip(arrays, ends, ends[1:])))


def layer_norm(rows_in, gain, shift):
    row_mean = jnp.mean(rows_in, axis=-1, keepdims=True)
    centered = rows_in - row_mean
    variance = jnp.mean(centered * centered, axis=-1, keepdims=True)
    return centered * lax.rsqrt(variance + EPSILON) * gain + shift


def exact_gelu(values_in):
    return jax.nn.gelu(values_in, approximate=False)


def choose(onehot, tensor_in):
    return jnp.einsum(
        "sa,a...->s...", onehot, tensor_in, preferred_element_type=jnp.float32
    ).astype(jnp.bfloat16)


def spread(onehot, grads_in):
    return jnp.einsum("sa,s...->a...", onehot, grads_in, precision=HIGHEST)


def seq_dot(left_side, right_side):
    return jnp.einsum("slk,skn->sln", left_side, right_side, preferred_element_type=jnp.float32)


def seq_dot_back(left_side, right_side):
    return jnp.einsum("sln,skn->slk", left_side, right_side, preferred_element_type=jnp.float32)


def seq_outer(left_side, right_side):
    return jnp.einsum("slk,sln->skn", left_side, right_side, preferred_element_type=jnp.float32)


def dot_back(left_side, right_side):
    return lax.dot_general(
        left_side, right_side, (((1,), (1,)), ((), ())), preferred_element_type=jnp.float32
    )


def widen_rows(low_rows):
    seq_total = low_rows.shape[0]
    identity = jnp.eye(seq_total, dtype=low_rows.dtype)
    widened = jnp.einsum("slr,st->sltr", low_rows, identity)
    return widened.reshape(seq_total * low_rows.shape[1], seq_total * low_rows.shape[2])


def block_scores(queries, keys_all, slopes, offset, block_rows):
    length = keys_all.shape[0]
    row_ids = offset + jnp.arange(block_rows)
    distance = (row_ids[:, None] - jnp.arange(length)[None, :]).astype(jnp.float32)
    query_block = lax.dynamic_slice_in_dim(queries, offset, block_rows, 0)
    raw_scores = jnp.einsum(
        "qhe,khe->hqk", query_block, keys_all, preferred_element_type=jnp.float32
    )
    scaled = (raw_scores - slopes[:, None, None] * distance[None]) * 0.125
    return (jnp.where(distance[None] >= 0, scaled, MASKED), query_block)


def attend(queries, keys_all, values_all, slopes, block_rows):
    length = queries.shape[0]

    def one_block(block_index):
        scores, _ = block_scores(queries, keys_all, slopes, block_index * block_rows, block_rows)
        row_max = jnp.max(scores, axis=-1, keepdims=True)
        exp_scores = jnp.exp(scores - row_max)
        row_sum = jnp.sum(exp_scores, axis=-1, keepdims=True)
        attn_probs = (exp_scores / row_sum).astype(jnp.bfloat16)
        context = jnp.einsum(
            "hqk,khe->qhe", attn_probs, values_all, preferred_element_type=jnp.float32
        )
        return (context.astype(jnp.bfloat16), (row_max + jnp.log(row_sum))[..., 0])

    context, log_sums = lax.map(one_block, jnp.arange(length // block_rows))
    return (context.reshape(queries.shape), log_sums)


def attend_back(queries, keys_all, values_all, grad_context, log_sums, slopes, block_rows):
    length = queries.shape[0]

    def one_block(running, block_index):
        grad_keys, grad_values = running
        offset = block_index * block_rows
        scores, query_block = block_scores(queries, keys_all, slopes, offset, block_rows)
        grad_block = lax.dynamic_slice_in_dim(grad_context, offset, block_rows, 0)
        attn_probs = jnp.exp(scores - log_sums[block_index][:, :, None])
        grad_probs = jnp.einsum(
            "qhe,khe->hqk", grad_block, values_all, preferred_element_type=jnp.float32
        )
        row_dot = jnp.sum(attn_probs * grad_probs, axis=-1, keepdims=True)
        grad_scores = (attn_probs * (grad_probs - row_dot)).astype(jnp.bfloat16)
        grad_queries = (
            jnp.einsum("hqk,khe->qhe", grad_scores, keys_all, preferred_element_type=jnp.float32)
            * 0.125
        )
        grad_keys = (
            grad_keys
            + jnp.einsum(
                "hqk,qhe->khe", grad_scores, query_block, preferred_element_type=jnp.float32
            )
            * 0.125
        )
        grad_values = grad_values + jnp.einsum(
            "hqk,qhe->khe",
            attn_probs.astype(jnp.bfloat16),
            grad_block,
            preferred_element_type=jnp.float32,
        )
        return ((grad_keys, grad_values), grad_queries)

    zeros_kv = jnp.zeros(keys_all.shape, jnp.float32)
    (grad_keys, grad_values), grad_queries = lax.scan(
        one_block, (zeros_kv, zeros_kv), jnp.arange(length // block_rows)
    )
    return (grad_queries.reshape(queries.shape), grad_keys, grad_values)


def local(
    tokens,
    grad_out,
    adapter_ids,
    first_gain,
    first_shift,
    joined_weight,
    joined_bias,
    dense_weight,
    dense_bias,
    second_gain,
    second_shift,
    up_weight,
    up_bias,
    down_weight,
    down_bias,
    joined_adapt_in,
    joined_adapt_out,
    dense_adapt_in,
    dense_adapt_out,
    up_adapt_in,
    up_adapt_out,
    down_adapt_in,
    down_adapt_out,
):
    local_rows = tokens.shape[0]
    model_width = tokens.shape[1]
    seq_total = adapter_ids.shape[0]
    group_rows = local_rows * lax.axis_size("tp")
    length = group_rows // seq_total
    block_rows = min(512, length)
    set_count = joined_adapt_in.shape[0]
    low_rank = joined_adapt_in.shape[2]
    joined_width = joined_bias.shape[0]
    hidden_width = up_bias.shape[0]
    local_heads = joined_width // (3 * HEAD_DIM)
    head_cols = local_heads * HEAD_DIM
    head_ids = lax.axis_index("tp") * local_heads + jnp.arange(local_heads)
    slopes = jnp.exp2(-8.0 * (head_ids + 1).astype(jnp.float32) / HEADS)
    matches = adapter_ids[:, None] == jnp.arange(set_count)[None, :]
    onehot_low = matches.astype(jnp.bfloat16)
    onehot_high = matches.astype(jnp.float32)
    pick_joined_in = choose(onehot_low, joined_adapt_in)
    pick_joined_out = choose(onehot_low, joined_adapt_out)
    pick_dense_in = choose(onehot_low, dense_adapt_in)
    pick_dense_out = choose(onehot_low, dense_adapt_out)
    pick_up_in = choose(onehot_low, up_adapt_in)
    pick_up_out = choose(onehot_low, up_adapt_out)
    pick_down_in = choose(onehot_low, down_adapt_in)
    pick_down_out = choose(onehot_low, down_adapt_out)
    residual_in = tokens.astype(jnp.float32)
    normed_one = layer_norm(residual_in, first_gain, first_shift).astype(jnp.bfloat16)
    gathered_one = lax.all_gather(normed_one, "tp", axis=0, tiled=True)
    w_joined, w_dense = (
        lax.all_gather(joined_weight, "fsdp", axis=0, tiled=True),
        lax.all_gather(dense_weight, "fsdp", axis=1, tiled=True),
    )
    seq_one = gathered_one.reshape(seq_total, length, model_width)
    low_joined = seq_dot(seq_one, pick_joined_in).astype(jnp.bfloat16)
    joined_cols = jnp.dot(gathered_one, w_joined, preferred_element_type=jnp.float32).reshape(
        seq_total, length, joined_width
    )
    joined_cols = (joined_cols + seq_dot(low_joined, pick_joined_out) + joined_bias).astype(
        jnp.bfloat16
    )
    joined_heads = joined_cols.reshape(seq_total, length, local_heads, 3, HEAD_DIM)
    sequence = 0
    context, log_sums = attend(
        joined_heads[sequence, :, :, 0, :],
        joined_heads[sequence, :, :, 1, :],
        joined_heads[sequence, :, :, 2, :],
        slopes,
        block_rows,
    )
    contexts = [context]
    log_list = [log_sums]
    seq_context = jnp.stack(contexts).reshape(seq_total, length, head_cols)
    context_rows = seq_context.reshape(group_rows, head_cols)
    low_dense = seq_dot(seq_context, pick_dense_in).astype(jnp.bfloat16)
    wide_dense = widen_rows(low_dense)
    stack_dense = pick_dense_out.reshape(seq_total * low_rank, model_width)
    rows_low = wide_dense
    attn_sum = sum_at_owner(
        (
            jnp.dot(context_rows, w_dense, preferred_element_type=jnp.float32)
            + jnp.dot(rows_low, stack_dense, preferred_element_type=jnp.float32)
        ).astype(jnp.bfloat16),
        "tp",
        0,
    )
    residual_mid = residual_in + attn_sum + dense_bias
    normed_two = layer_norm(residual_mid, second_gain, second_shift).astype(jnp.bfloat16)
    gathered_two = lax.all_gather(normed_two, "tp", axis=0, tiled=True)
    w_up, w_down = (
        lax.all_gather(up_weight, "fsdp", axis=0, tiled=True),
        lax.all_gather(down_weight, "fsdp", axis=1, tiled=True),
    )
    seq_two = gathered_two.reshape(seq_total, length, model_width)
    low_up = seq_dot(seq_two, pick_up_in).astype(jnp.bfloat16)
    pre_act = (
        jnp.dot(gathered_two, w_up, preferred_element_type=jnp.float32)
        + seq_dot(low_up, pick_up_out).reshape(group_rows, hidden_width)
        + up_bias
    )
    activated = exact_gelu(pre_act).astype(jnp.bfloat16)
    seq_act = activated.reshape(seq_total, length, hidden_width)
    low_down = seq_dot(seq_act, pick_down_in).astype(jnp.bfloat16)
    wide_down = widen_rows(low_down)
    stack_down = pick_down_out.reshape(seq_total * low_rank, model_width)
    rows_low = wide_down
    mlp_sum = sum_at_owner(
        (
            jnp.dot(activated, w_down, preferred_element_type=jnp.float32)
            + jnp.dot(rows_low, stack_down, preferred_element_type=jnp.float32)
        ).astype(jnp.bfloat16),
        "tp",
        0,
    )
    layer_out = (residual_mid + mlp_sum + down_bias).astype(jnp.bfloat16)
    grad_mlp = lax.all_gather(grad_out, "tp", axis=0, tiled=True)
    back_up, back_down = (w_up, w_down)
    seq_grad_mlp = grad_mlp.reshape(seq_total, length, model_width)
    grad_low_down = seq_dot_back(seq_grad_mlp, pick_down_out).astype(jnp.bfloat16)
    term_down_out = seq_outer(low_down, seq_grad_mlp)
    term_down_in = seq_outer(seq_act, grad_low_down)
    grad_act = dot_back(grad_mlp, back_down) + seq_dot_back(grad_low_down, pick_down_in).reshape(
        group_rows, hidden_width
    )
    _, gelu_pull = jax.vjp(exact_gelu, pre_act)
    grad_pre = gelu_pull(grad_act)[0].astype(jnp.bfloat16)
    seq_grad_pre = grad_pre.reshape(seq_total, length, hidden_width)
    grad_low_up = seq_dot_back(seq_grad_pre, pick_up_out).astype(jnp.bfloat16)
    term_up_out = seq_outer(low_up, seq_grad_pre)
    term_up_in = seq_outer(seq_two, grad_low_up)
    wide_up = widen_rows(grad_low_up)
    stack_up = jnp.swapaxes(pick_up_in, 1, 2).reshape(seq_total * low_rank, model_width)
    rows_grad = grad_pre
    rows_low = wide_up
    grad_norm_two = sum_at_owner(
        (
            dot_back(rows_grad, back_up)
            + jnp.dot(rows_low, stack_up, preferred_element_type=jnp.float32)
        ).astype(jnp.bfloat16),
        "tp",
        0,
    )
    _, norm_pull_two = jax.vjp(
        lambda rows_in: layer_norm(rows_in, second_gain, second_shift), residual_mid
    )
    grad_mid = grad_out.astype(jnp.float32) + norm_pull_two(grad_norm_two)[0]
    grad_attn = lax.all_gather(grad_mid.astype(jnp.bfloat16), "tp", axis=0, tiled=True)
    back_joined, back_dense = (w_joined, w_dense)
    seq_grad_attn = grad_attn.reshape(seq_total, length, model_width)
    grad_low_dense = seq_dot_back(seq_grad_attn, pick_dense_out).astype(jnp.bfloat16)
    term_dense_out = seq_outer(low_dense, seq_grad_attn)
    term_dense_in = seq_outer(seq_context, grad_low_dense)
    grad_context = dot_back(grad_attn, back_dense) + seq_dot_back(
        grad_low_dense, pick_dense_in
    ).reshape(group_rows, head_cols)
    grad_context = grad_context.astype(jnp.bfloat16).reshape(
        seq_total, length, local_heads, HEAD_DIM
    )
    sequence = 0
    grad_query, grad_key, grad_value = attend_back(
        joined_heads[sequence, :, :, 0, :],
        joined_heads[sequence, :, :, 1, :],
        joined_heads[sequence, :, :, 2, :],
        grad_context[sequence],
        log_list[sequence],
        slopes,
        block_rows,
    )
    grad_parts = [jnp.stack((grad_query, grad_key, grad_value), axis=2)]
    grad_joined = (
        jnp.stack(grad_parts).astype(jnp.bfloat16).reshape(seq_total, length, joined_width)
    )
    grad_low_joined = seq_dot_back(grad_joined, pick_joined_out).astype(jnp.bfloat16)
    term_joined_out = seq_outer(low_joined, grad_joined)
    term_joined_in = seq_outer(seq_one, grad_low_joined)
    grad_joined_rows = grad_joined.reshape(group_rows, joined_width)
    wide_joined = widen_rows(grad_low_joined)
    stack_joined = jnp.swapaxes(pick_joined_in, 1, 2).reshape(seq_total * low_rank, model_width)
    rows_grad = grad_joined_rows
    rows_low = wide_joined
    grad_norm_one = sum_at_owner(
        (
            dot_back(rows_grad, back_joined)
            + jnp.dot(rows_low, stack_joined, preferred_element_type=jnp.float32)
        ).astype(jnp.bfloat16),
        "tp",
        0,
    )
    _, norm_pull_one = jax.vjp(
        lambda rows_in: layer_norm(rows_in, first_gain, first_shift), residual_in
    )
    grad_tokens = grad_mid + norm_pull_one(grad_norm_one)[0]
    wide_sums = tuple(
        (
            part.astype(jnp.float32)
            for part in together(
                (
                    spread(onehot_high, term_joined_out).astype(jnp.bfloat16),
                    spread(onehot_high, term_dense_in).astype(jnp.bfloat16),
                    spread(onehot_high, term_up_out).astype(jnp.bfloat16),
                    spread(onehot_high, term_down_in).astype(jnp.bfloat16),
                ),
                "fsdp",
            )
        )
    )
    both_sums = lax.psum(
        (
            spread(onehot_high, term_joined_in),
            spread(onehot_high, term_dense_out),
            spread(onehot_high, term_up_in),
            spread(onehot_high, term_down_out),
        ),
        ("fsdp", "tp"),
    )
    return (
        layer_out,
        grad_tokens,
        both_sums[0],
        wide_sums[0],
        wide_sums[1],
        both_sums[1],
        both_sums[2],
        wide_sums[2],
        wide_sums[3],
        both_sums[3],
    )


def solution(mesh):
    return jax.shard_map(
        local,
        mesh=mesh,
        in_specs=(
            P(("fsdp", "tp"), None),
            P(("fsdp", "tp"), None),
            P("fsdp"),
            P(),
            P(),
            P("fsdp", "tp"),
            P("tp"),
            P("tp", "fsdp"),
            P(),
            P(),
            P(),
            P("fsdp", "tp"),
            P("tp"),
            P("tp", "fsdp"),
            P(),
            P(),
            P(None, None, "tp"),
            P(None, "tp", None),
            P(),
            P(),
            P(None, None, "tp"),
            P(None, "tp", None),
            P(),
        ),
        out_specs=(
            P(("fsdp", "tp"), None),
            P(("fsdp", "tp"), None),
            P(),
            P(None, None, "tp"),
            P(None, "tp", None),
            P(),
            P(),
            P(None, None, "tp"),
            P(None, "tp", None),
            P(),
        ),
        check_vma=False,
    )
```

profile of v0, /device:TPU:1, one launch (start us, length us, event | category | flops | bytes accessed | tf_op | source)
XLA Modules:
  0.0 977.7 jit_solution(4659292120763606901)
XLA Ops:
  19.2 68.6 %all-gather.9.cloned.1.call-done = bf16[1024,2048]{1,0:T(8,128)(2,1)} async-done(((bf16[128,2048]{1,0:T(8,128)(2,1)}), bf16[1024,2048]{1,0:T(8,128)(2,1)}) %all-gather.9.cloned.1.call-update) | async-done | bytes 4194320 | tf_op jit(solution)/shard_map/all_gather | solution.py:202
  87.8 3.4 convolution_convert_fusion.5
  91.2 32.7 %all-gather.11.cloned.1.call-done = bf16[2048,768]{1,0:T(8,128)(2,1)} async-done(((bf16[128,768]{1,0:T(8,128)(2,1)}), bf16[2048,768]{1,0:T(8,128)(2,1)}) %all-gather.11.cloned.1.call-update) | async-done | bytes 3145744 | tf_op jit(solution)/shard_map/all_gather | solution.py:204
  123.9 6.4 fusion.96
  131.2 22.1 %while.28 = (s32[]{:T(128)}, bf16[2,512,4,64]{1,3,2,0:T(8,128)(2,1)S(1)}, f32[2,4,512]{2,1,0:T(4,128)S(1)}, s32[2]{0:T(128)S(1)}, bf16[1024,4,64]{0,2,1:T(8,128)...) while((s32[]{:T(128)}, ...), condition=%wide.region_5.6_spmd.clone, body=%wide.region_2.5_spmd.clone.sunk | while | flops 577370624 | bytes 37297388 | solution.py:106
  133.2 2.7 fusion.187
  135.9 2.9 fusion.188
  138.8 3.4 fusion.189
  144.2 2.7 fusion.187
  146.9 2.9 fusion.188
  149.9 3.4 fusion.189
  154.2 5.4 all-gather.13.cloned.1.call-done
  163.4 62.2 %all_to_all.20 = bf16[8,128,2048]{2,1,0:T(8,128)(2,1)S(1)} all-to-all(bf16[8,128,2048]{2,1,0:T(8,128)(2,1)S(1)} %bitcast.233), channel_id=1, replica_groups=mesh['fsdp'=16,'tp'=8] {'tp'}, dimensions={0} | all-to-all | bytes 8388608 | tf_op jit(solution)/shard_map/all_to_all | solution.py:22
  232.0 33.0 %all-gather.21.cloned.1.call-done = bf16[1024,2048]{1,0:T(8,128)(2,1)} async-done(((bf16[128,2048]{1,0:T(8,128)(2,1)}), bf16[1024,2048]{1,0:T(8,128)(2,1)}) %all-gather.21.cloned.1.call-update) | async-done | bytes 4194320 | tf_op jit(solution)/shard_map/all_gather | solution.py:269
  265.0 3.4 convolution_convert_fusion.3
  268.3 41.9 %all-gather.19.cloned.1.call-done = bf16[1024,2048]{1,0:T(8,128)(2,1)} async-done(((bf16[1024,128]{1,0:T(8,128)(2,1)}), bf16[1024,2048]{1,0:T(8,128)(2,1)}) %all-gather.19.cloned.1.call-update) | async-done | bytes 4194320 | tf_op jit(solution)/shard_map/all_gather | solution.py:245
  310.2 10.0 %fusion.100 = f32[1024,1024]{1,0:T(8,128)} fusion(bf16[1024,2048]{1,0:T(8,128)(2,1)} %all-gather.21.cloned.1.call-done, bf16[1024,2048]{1,0:T(8,128)(2,1)} %all-gather.19.cloned.1.call-done), kind=kOutput, calls=%fused_computation.187 | convolution fusion | flops 4294967296 | bytes 12582912 | tf_op jit(solution)/shard_map/dot_general | solution.py:68
  320.2 63.6 %all-gather.15.cloned.1.call-done = bf16[1024,2048]{1,0:T(8,128)(2,1)} async-done(((bf16[128,2048]{1,0:T(8,128)(2,1)}), bf16[1024,2048]{1,0:T(8,128)(2,1)}) %all-gather.15.cloned.1.call-update) | async-done | bytes 4194320 | tf_op jit(solution)/shard_map/all_gather | solution.py:242
  383.9 3.4 convolution_convert_fusion.4
  387.2 34.3 %all-gather.17.cloned.1.call-done = bf16[2048,1024]{1,0:T(8,128)(2,1)} async-done(((bf16[128,1024]{1,0:T(8,128)(2,1)}), bf16[2048,1024]{1,0:T(8,128)(2,1)}) %all-gather.17.cloned.1.call-update) | async-done | bytes 4194320 | tf_op jit(solution)/shard_map/all_gather | solution.py:244
  421.5 7.9 fusion.98
  429.5 11.2 %multiply_convert_fusion.2 = (bf16[1024,1024]{1,0:T(8,128)(2,1)}, f32[1024,1024]{1,0:T(8,128)S(1)}, f32[1024,1024]{1,0:T(8,128)S(1)}) fusion(f32[1024]{0:T(1024)S(1)} %copy-done.56, f32[1024,1024]{1,0:T(8,128)S(1)} %fusion.98, bf16[1024,16]{0,1:T(8,128)(2,1)S(1)} %convolution_convert_fusion.4, bf16[1,16,1024]{2,0,1:T(2,128)(2,1)S(1)} %fusion.66), kind=kOutput, calls=%fused_computation.60 | convolution fusion | flops 103809024 | bytes 14749696 | tf_op jit(solution)/shard_map/slk,skn->sln/dot_general | solution.py:56
  443.6 4.6 fusion.101
  448.2 3.3 add_convert_fusion.1
  451.5 6.5 all-to-all-start.2
  460.2 6.9 fusion.99
  467.2 3.4 add_convert_fusion.2
  470.5 36.2 %all-to-all-done.2 = bf16[8,128,2048]{2,1,0:T(8,128)(2,1)} async-done(((bf16[8,128,2048]{2,1,0:T(8,128)(2,1)}), bf16[8,128,2048]{2,1,0:T(8,128)(2,1)}, u32[]{:S(2)}, u32[]{:S(2)}) %all-to-all-start.2) | async-done | bytes 4194336 | tf_op jit(solution)/shard_map/all_to_all | solution.py:22
  506.8 5.1 all-to-all-start.1
  511.9 3.0 convert_reduce_fusion.1
  515.2 45.4 %all-to-all-done.1 = bf16[8,128,2048]{2,1,0:T(8,128)(2,1)} async-done(((bf16[8,128,2048]{2,1,0:T(8,128)(2,1)}), bf16[8,128,2048]{2,1,0:T(8,128)(2,1)}, u32[]{:S(2)}, u32[]{:S(2)}) %all-to-all-start.1) | async-done | bytes 4194336 | tf_op jit(solution)/shard_map/all_to_all | solution.py:22
  560.6 3.0 convert_reduce_fusion.2
  573.9 3.0 reshape.539
  576.9 3.7 fusion.109
  581.9 55.0 %all-gather.23.cloned.1.call-done = bf16[1024,2048]{1,0:T(8,128)(2,1)} async-done(((bf16[128,2048]{1,0:T(8,128)(2,1)}), bf16[1024,2048]{1,0:T(8,128)(2,1)}) %all-gather.23.cloned.1.call-update) | async-done | bytes 4194320 | tf_op jit(solution)/shard_map/all_gather | solution.py:300
  636.9 3.5 convolution_convert_fusion.1
  643.7 29.9 %while.29 = (s32[]{:T(128)}, f32[1024,4,64]{0,2,1:T(8,128)S(1)}, f32[1024,4,64]{0,2,1:T(8,128)S(1)}, bf16[2,512,4,64]{1,3,2,0:T(8,128)(2,1)}, s32[2]{0:T(128)S(1...) while((s32[]{:T(128)}, f32[1024,4,64]{0,2,1:T(8,128)S(1)}, ...), condition=%wide.region_15.16_spmd.clone, body=%wide.region_13.15_spmd.clone.sunk | while | flops 1369307648 | bytes 81836928 | solution.py:144
  650.3 3.9 multiply_reduce_fusion.4
  665.0 3.9 multiply_reduce_fusion.4
  679.0 5.4 fusion.103
  684.5 3.2 add_convert_fusion
  687.7 4.6 all-to-all-start.3
  692.3 3.0 fusion.110
  699.3 101.2 %all-reduce.4.cloned.1.call-done = bf16[393216]{0:T(1024)(128)(2,1)} async-done(((bf16[393216]{0:T(1024)(128)(2,1)}), bf16[393216]{0:T(1024)(128)(2,1)}) %all-reduce.4.cloned.1.call-update) | async-done | bytes 786448 | tf_op jit(solution)/shard_map/psum | solution.py:30
  806.4 2.9 reshape.543
  809.3 3.6 copy.47
  812.9 3.1 convert_reduce_fusion
  818.3 145.4 %all-reduce.6.cloned.1.call-done = (f32[8,2048,16]{1,2,0:T(8,128)}, f32[8,16,2048]{2,1,0:T(8,128)}, f32[8,2048,16]{1,2,0:T(8,128)}, f32[8,16,2048]{2,1,0:T(8,128)}) async-done(((f32[8,2048,16]{1,2,0:T(8,128)}, f32[8,16,2048]{2,1,0:T(8,128)}, f32[8,2048,16]{1,2,0:T(8,128)}, f32[8,16,2048]{2,1,0:T(8,128)}), (f32[8,2048,16]{1,2,0:T(8,128)}, f32[8,16,2048]{2,1,0:T(8,128)}, f32[8,2048,16]{1,2,0:T(8,128)}, ...) | async-done | bytes 4194320 | tf_op jit(solution)/shard_map/psum | solution.py:360
  (263 shorter events, 86.1 us)
Async XLA Ops:
  7.2 10.6 %copy-start = (bf16[8,2048,16]{1,2,0:T(8,128)(2,1)S(1)}, bf16[8,2048,16]{1,2,0:T(8,128)(2,1)}, u32[]{:S(2)}) copy-start(bf16[8,2048,16]{1,2,0:T(8,128)(2,1)} %param.42) | copy-start | bytes 1572868
  7.2 11.3 %copy-start.38 = (bf16[8,16,768]{2,1,0:T(8,128)(2,1)S(1)}, bf16[8,16,768]{2,1,0:T(8,128)(2,1)}, u32[]{:S(2)}) copy-start(bf16[8,16,768]{2,1,0:T(8,128)(2,1)} %param.43) | copy-start | bytes 589828
  7.2 11.5 %copy-start.24 = (bf16[8,16,2048]{2,1,0:T(8,128)(2,1)S(1)}, bf16[8,16,2048]{2,1,0:T(8,128)(2,1)}, u32[]{:S(2)}) copy-start(bf16[8,16,2048]{2,1,0:T(8,128)(2,1)} %param.45) | copy-start | bytes 1572868
  7.2 80.6 %all-gather.9.cloned.1.call-start = ((), (), s32[]{:S(2)}) async-start(), calls=%async_computation.4 | async-start | bytes 4718592 | tf_op jit(solution)/shard_map/all_gather | solution.py:202
  13.3 110.7 %all-gather.11.cloned.1.call-start = ((), (), s32[]{:S(2)}) async-start(), calls=%async_computation.5 | async-start | bytes 3342336 | tf_op jit(solution)/shard_map/all_gather | solution.py:204
  14.0 145.6 %all-gather.13.cloned.1.call-start = ((), (), s32[]{:S(2)}) async-start(), calls=%async_computation.6 | async-start | bytes 1114112 | tf_op jit(solution)/shard_map/all_gather | solution.py:205
  14.7 250.2 %all-gather.21.cloned.1.call-start = ((), (), s32[]{:S(2)}) async-start(), calls=%async_computation.10 | async-start | bytes 4718592 | tf_op jit(solution)/shard_map/all_gather | solution.py:269
  15.3 294.9 %all-gather.19.cloned.1.call-start = ((), (), s32[]{:S(2)}) async-start(), calls=%async_computation.9 | async-start | bytes 4456448 | tf_op jit(solution)/shard_map/all_gather | solution.py:245
  15.9 367.9 %all-gather.15.cloned.1.call-start = ((), (), s32[]{:S(2)}) async-start(), calls=%async_computation.7 | async-start | bytes 4718592 | tf_op jit(solution)/shard_map/all_gather | solution.py:242
  18.5 72.6 %copy-start.14 = (bf16[1,2048,16]{2,1,0:T(8,128)(2,1)}, bf16[1,2048,16]{2,1,0:T(8,128)(2,1)S(1)}, u32[]{:S(2)}) copy-start(bf16[1,2048,16]{2,1,0:T(8,128)(2,1)S(1)} %copy.49) | copy-start | bytes 196612
  18.7 111.6 %copy-start.36 = (bf16[1,16,768]{2,0,1:T(2,128)(2,1)}, bf16[1,16,768]{2,0,1:T(2,128)(2,1)S(1)}, u32[]{:S(2)}) copy-start(bf16[1,16,768]{2,0,1:T(2,128)(2,1)S(1)} %fusion.68) | copy-start | bytes 73732
  19.2 142.9 %copy-start.28 = (bf16[1,16,2048]{2,0,1:T(2,128)(2,1)}, bf16[1,16,2048]{2,0,1:T(2,128)(2,1)S(1)}, u32[]{:S(2)}) copy-start(bf16[1,16,2048]{2,0,1:T(2,128)(2,1)S(1)} %fusion.60) | copy-start | bytes 196612
  91.1 39.2 %copy-start.30 = (bf16[1024,16]{0,1:T(8,128)(2,1)}, bf16[1024,16]{0,1:T(8,128)(2,1)S(1)}, u32[]{:S(2)}) copy-start(bf16[1024,16]{0,1:T(8,128)(2,1)S(1)} %convolution_convert_fusion.5) | copy-start | bytes 98308
  91.1 39.2 %copy-start.50 = (f32[768]{0:T(1024)S(1)}, f32[768]{0:T(1024)}, u32[]{:S(2)}) copy-start(f32[768]{0:T(1024)} %param.33) | copy-start | bytes 9220
  153.3 8.8 copy-start.8
  153.9 8.2 copy-start.11
  154.2 8.0 copy-start.32
  226.7 3.6 copy-start.35
  228.3 193.3 %all-gather.17.cloned.1.call-start = ((), (), s32[]{:S(2)}) async-start(), calls=%async_computation.8 | async-start | bytes 4456448 | tf_op jit(solution)/shard_map/all_gather | solution.py:244
  387.2 42.3 %copy-start.56 = (f32[1024]{0:T(1024)S(1)}, f32[1024]{0:T(1024)}, u32[]{:S(2)}) copy-start(f32[1024]{0:T(1024)} %param.39) | copy-start | bytes 12292
  429.5 11.2 %copy-start.57 = (f32[1024,1024]{1,0:T(8,128)S(1)}, f32[1024,1024]{1,0:T(8,128)}, u32[]{:S(2)}) copy-start(f32[1024,1024]{1,0:T(8,128)} %fusion.100) | copy-start | bytes 12582916
  442.9 5.2 copy-start.13
  451.5 55.3 %all-to-all-start.2 = ((bf16[8,128,2048]{2,1,0:T(8,128)(2,1)}), bf16[8,128,2048]{2,1,0:T(8,128)(2,1)}, u32[]{:S(2)}, u32[]{:S(2)}) async-start(bf16[8,128,2048]{2,1,0:T(8,128)(2,1)} %bitcast.232), calls=%async_computation.2 | async-start | bytes 8388608 | tf_op jit(solution)/shard_map/all_to_all | solution.py:22
  506.8 53.8 %all-to-all-start.1 = ((bf16[8,128,2048]{2,1,0:T(8,128)(2,1)}), bf16[8,128,2048]{2,1,0:T(8,128)(2,1)}, u32[]{:S(2)}, u32[]{:S(2)}) async-start(bf16[8,128,2048]{2,1,0:T(8,128)(2,1)} %bitcast.231), calls=%async_computation.1 | async-start | bytes 8388608 | tf_op jit(solution)/shard_map/all_to_all | solution.py:22
  511.8 125.0 %all-gather.23.cloned.1.call-start = ((), (), s32[]{:S(2)}) async-start(), calls=%async_computation.11 | async-start | bytes 4718592 | tf_op jit(solution)/shard_map/all_gather | solution.py:300
  514.9 48.7 %copy-start.47 = (f32[2048]{0:T(1024)S(1)}, f32[2048]{0:T(1024)}, u32[]{:S(2)}) copy-start(f32[2048]{0:T(1024)} %param.41) | copy-start | bytes 24580
  560.6 5.2 copy-start.16
  566.8 233.7 %all-reduce.4.cloned.1.call-start = ((), (), s32[]{:S(2)}) async-start(), calls=%async_computation.12 | async-start | bytes 1572864 | tf_op jit(solution)/shard_map/psum | solution.py:30
  566.9 5.2 copy-start.41
  576.9 3.7 copy-start.2
  636.9 3.5 copy-start.12
  636.9 4.5 copy-start.5
  636.9 4.5 copy-start.18
  679.0 5.4 copy-start.15
  687.7 125.2 %all-to-all-start.3 = ((bf16[8,128,2048]{2,1,0:T(8,128)(2,1)}), bf16[8,128,2048]{2,1,0:T(8,128)(2,1)}, u32[]{:S(2)}, u32[]{:S(2)}) async-start(bf16[8,128,2048]{2,1,0:T(8,128)(2,1)} %bitcast.230), calls=%async_computation.3 | async-start | bytes 8388608 | tf_op jit(solution)/shard_map/all_to_all | solution.py:22
  692.3 4.7 copy-start.33
  692.3 271.4 %all-reduce.6.cloned.1.call-start = ((), (), s32[]{:S(2)}) async-start(), calls=%async_computation.13 | async-start | bytes 8388608 | tf_op jit(solution)/shard_map/psum | solution.py:360
  692.3 4.7 copy-start.6
  809.3 6.7 copy-start.4
  809.3 6.7 copy-start.39
  809.3 6.7 copy-start.44
  812.9 3.5 copy-start.49
  812.9 3.9 copy-start.10
  812.9 3.9 copy-start.17
  812.9 3.9 copy-start.52
  963.7 4.7 copy-start.20
  963.7 5.7 copy-start.19
  963.7 6.7 copy-start.1
  (26 other events, 41.1 us)
Sparse Core Ops, SparseCore 0:
  13.4 74.3 all-gather.8
  89.5 34.3 all-gather.10
  125.5 33.9 all-gather.12
  161.8 103.1 all-gather.20
  266.4 43.7 all-gather.18
  313.0 70.7 all-gather.14
  385.6 35.9 all-gather.16
  566.9 69.9 all-gather.22
  679.1 121.3 all-reduce.3
  807.4 156.1 all-reduce.5
where the time goes:
time: 982 us; the launch traced here: 978 us
  waiting for transfers between devices  666 us (68%)
  matrix products  139 us (14%)
  blocking collectives  62.2 us (6%)
  other arithmetic  40.9 us (4%)
  local copies, waits for them, and re-layouts  29.7 us (3%)
  starting transfers between devices  16.5 us (2%)
  between operations  16.2 us (2%)
    psum x1, waiting for transfers between devices, local(): lax.psum((spread(onehot_high, term_joined_in), spread(onehot_high, term_d...  145 us
    psum x1, waiting for transfers between devices, together(): so_far = lax.psum(jnp.concatenate([a.ravel() for a in arrays]), axis)  101 us
    all_to_all x3, waiting for transfers between devices, sum_at_owner(): lax.all_to_all(blocks, axis, split_axis=0, concat_axis=0, tiled=True)  81.6 us
    all_gather x1, waiting for transfers between devices, local(): gathered_one = lax.all_gather(normed_one, 'tp', axis=0, tiled=True)  68.6 us
    all_gather x1, waiting for transfers between devices, local(): gathered_two = lax.all_gather(normed_two, 'tp', axis=0, tiled=True)  63.6 us
    all_to_all x1, blocking collectives, sum_at_owner(): lax.all_to_all(blocks, axis, split_axis=0, concat_axis=0, tiled=True)  62.2 us
    all_gather x1, waiting for transfers between devices, local(): lax.all_gather(grad_mid.astype(jnp.bfloat16), 'tp', axis=0, tiled=True)  55 us
    all_gather x1, waiting for transfers between devices, local(): lax.all_gather(down_weight, 'fsdp', axis=1, tiled=True)  41.9 us
  transfers between devices with their start and end apart: 13, of which 12 were waited for; matrix products, arithmetic and copies ran while one was open for 13% of the time, Pallas kernels for 0%

commit v1 on v0

v1 whole, which is shorter than its diff:
```python
import functools

import jax
import jax.numpy as jnp
import numpy as np
from jax import lax
from jax.experimental import pallas as pl
from jax.experimental.pallas import tpu as pltpu
from jax.sharding import Mesh
from jax.sharding import PartitionSpec as P

HEADS = 32
HEAD_DIM = 64
EPSILON = 1e-05
MASKED = -1e30
AXES = ("xl", "y", "c", "xh", "z")
FSDP = ("xl", "y", "c")
TP = ("xh", "z")
PLANE = ("xl", "y", "xh")
MESH_ID = pl.DeviceIdType.MESH
ANY = pl.ANY
VMEM = pltpu.VMEM
F32 = jnp.float32
BF16 = jnp.bfloat16


def remote(src, dst, sems, index, device):
    send, recv = sems
    return pltpu.make_async_remote_copy(
        src_ref=src, dst_ref=dst, send_sem=send.at[index], recv_sem=recv.at[index],
        device_id=device, device_id_type=MESH_ID)


def places():
    return tuple(lax.axis_index(a) for a in AXES)


def meet(peers):
    barrier = pltpu.get_barrier_semaphore()
    for p in peers:
        pl.semaphore_signal(barrier, inc=1, device_id=p, device_id_type=MESH_ID)
    pl.semaphore_wait(barrier, len(peers))


def ring_peers():
    _, _, c, _, z = places()
    return [{"z": lax.rem(z + 1, 4)}, {"z": lax.rem(z + 3, 4)}, {"c": 1 - c}]


def plane_peers():
    xl, y, c, xh, _ = places()
    peers = []
    for d in range(1, 4):
        for core in (0, 1):
            peers.append({"y": lax.rem(y + d, 4), "c": core})
            x = lax.rem(xh * 2 + xl + d, 4)
            peers.append({"xh": x // 2, "xl": lax.rem(x, 2), "c": core})
    return peers


class GroupGather:
    sub = 4

    def __init__(self, src, dst, local_sem, sems):
        self.src, self.dst, self.local_sem, self.sems = src, dst, local_sem, sems
        _, _, self.c, _, self.z = places()
        self.up, self.down, self.other = ring_peers()
        self.rows = src.shape[0]

    @staticmethod
    def semaphores():
        return [pltpu.SemaphoreType.DMA((1,)), pltpu.SemaphoreType.DMA((8, GroupGather.sub)),
                pltpu.SemaphoreType.DMA((8, GroupGather.sub))]

    def at(self, core, z, j=None):
        first = (core * 4 + z) * self.rows
        if j is None:
            return self.dst.at[pl.ds(pl.multiple_of(first, 128), self.rows)]
        step = self.rows // self.sub
        return self.dst.at[pl.ds(pl.multiple_of(first + j * step, step), step)]

    def start(self):
        c, z = self.c, self.z
        step = self.rows // self.sub
        self.own = pltpu.make_async_copy(self.src, self.at(c, z), self.local_sem.at[0])
        self.own.start()
        self.ups, self.downs = {}, {}
        for j in range(self.sub):
            k = self.sub - 1 - j
            self.ups[j] = remote(self.src.at[pl.ds(j * step, step)], self.at(c, z, j), self.sems, (0, j), self.up)
            self.ups[j].start()
            self.downs[k] = remote(self.src.at[pl.ds(k * step, step)], self.at(c, z, k), self.sems, (1, k), self.down)
            self.downs[k].start()
        self.shared = [remote(self.src, self.at(c, z), self.sems, (2, 0), self.other)]
        self.shared[0].start()
        self.forward = []

    def share(self, z, j, kind):
        block = self.at(self.c, z, j)
        copy = remote(block, block, self.sems, (kind, j), self.other)
        copy.start()
        self.shared.append(copy)

    def near(self, j):
        c, z = self.c, self.z
        above, below = lax.rem(z + 1, 4), lax.rem(z + 3, 4)
        half = self.sub // 2
        self.ups[j].wait_recv()
        if j < half:
            block = self.at(c, below, j)
            copy = remote(block, block, self.sems, (3, j), self.up)
            copy.start()
            self.forward.append((j, copy))
        k = self.sub - 1 - j
        self.downs[k].wait_recv()
        if k >= half:
            block = self.at(c, above, k)
            copy = remote(block, block, self.sems, (4, k), self.down)
            copy.start()
            self.forward.append((k, copy))
        self.share(below, j, 5)
        self.share(above, k, 6)

    def far(self):
        opposite = lax.rem(self.z + 2, 4)
        for j, copy in self.forward:
            copy.wait_recv()
            self.share(opposite, j, 7)

    def finish(self):
        self.own.wait()
        for copy in (*self.ups.values(), *self.downs.values()):
            copy.wait_send()
        for _, copy in self.forward:
            copy.wait_send()
        for copy in self.shared:
            copy.wait()


class PlaneGather:
    def __init__(self, src, dst, by_rows, local_sem, sems):
        self.src, self.dst, self.by_rows, self.local_sem, self.sems = src, dst, by_rows, local_sem, sems
        self.xl, self.y, self.c, self.xh, _ = places()
        self.x = self.xh * 2 + self.xl
        self.home = 1 - (self.xh - self.c) * (self.xh - self.c)

    @staticmethod
    def semaphores():
        return [pltpu.SemaphoreType.DMA((1,)), pltpu.SemaphoreType.DMA((22,)), pltpu.SemaphoreType.DMA((16,))]

    def slot(self, xl, y, core):
        k = (xl * 4 + y) * 2 + core
        if self.by_rows:
            return k, self.dst.at[pl.ds(pl.multiple_of(k * 128, 128), 128)]
        return k, self.dst.at[:, pl.ds(pl.multiple_of(k * 128, 128), 128)]

    def send(self, src, where, n, device):
        k, dst = where
        send, recv = self.sems
        return pltpu.make_async_remote_copy(
            src_ref=src, dst_ref=dst, send_sem=send.at[n], recv_sem=recv.at[k],
            device_id=device, device_id_type=MESH_ID)

    def arrived(self, where):
        self.send(where[1], where, 0, {"c": 1 - self.c}).wait_recv()

    def chip_x(self, d, core):
        x = lax.rem(self.x + d, 4)
        return {"xh": x // 2, "xl": lax.rem(x, 2), "c": core}

    def chip_y(self, d, core):
        return {"y": lax.rem(self.y + d, 4), "c": core}

    def first(self, act):
        own = self.slot(self.xl, self.y, self.c)

        @pl.when(self.c == 0)
        def _():
            for d in (1, 3, 2):
                act(self.send(self.src, own, d, self.chip_x(d, self.xh)))

        @pl.when(self.c == 1)
        def _():
            for d in (1, 3, 2):
                act(self.send(self.src, own, d, self.chip_y(d, self.xh)))

        @pl.when(self.home == 0)
        def _():
            act(self.send(self.src, own, 0, {"c": 1 - self.c}))

    def start(self):
        @pl.when(self.home == 1)
        def _():
            pltpu.make_async_copy(self.src, self.slot(self.xl, self.y, self.c)[1], self.local_sem.at[0]).start()

        self.first(lambda copy: copy.start())

        @pl.when(self.home == 1)
        def _():
            pltpu.make_async_copy(self.src, self.slot(self.xl, self.y, self.c)[1], self.local_sem.at[0]).wait()

    def columns(self):
        one = self.home * self.xl
        return one, 1 - one

    def rows_step(self, n, act):
        where = self.slot(self.columns()[n], self.y, 0)
        for d in (1, 3, 2):
            act(self.send(where[1], where, 4 + n * 3 + d - 1, self.chip_y(d, self.c)))

    def columns_step(self, n, act):
        where = self.slot(self.xl, lax.rem(self.y + n, 4), 1)

        @pl.when(self.home == 1)
        def _():
            for d in (1, 3, 2):
                act(self.send(where[1], where, 10 + n * 3 + d - 1, self.chip_x(d, self.c)))

    def step(self, n):
        if n < 2:
            where = self.slot(self.columns()[n], self.y, 0)
            if n == 0:
                @pl.when(self.home * (1 - self.c) == 0)
                def _():
                    self.arrived(where)
            else:
                self.arrived(where)
            self.rows_step(n, lambda copy: copy.start())
        else:
            where = self.slot(self.xl, lax.rem(self.y + n - 2, 4), 1)
            here = self.home * (1 - self.c) if n == 2 else self.home

            @pl.when(here == 1)
            def _():
                self.arrived(where)

            self.columns_step(n - 2, lambda copy: copy.start())

    def finish(self):
        for xl in (0, 1):
            for d in (1, 2, 3):
                self.arrived(self.slot(xl, lax.rem(self.y + d, 4), 0))
        one, two = self.columns()
        for y in range(4):
            self.arrived(self.slot(two, y, 1))

        @pl.when(self.home == 0)
        def _():
            for y in range(4):
                self.arrived(self.slot(one, y, 1))

        self.first(lambda copy: copy.wait_send())
        for n in (0, 1):
            self.rows_step(n, lambda copy: copy.wait_send())
        for n in range(4):
            self.columns_step(n, lambda copy: copy.wait_send())


class GroupSum:
    def __init__(self, parts, near, sent, half, full, sems):
        self.parts, self.near, self.sent, self.half, self.full, self.sems = parts, near, sent, half, full, sems
        _, _, self.c, _, self.z = places()
        self.up, self.down, self.other = ring_peers()
        self.order = [lax.rem(self.z + d, 4) for d in (2, 1, 3, 0)]

    @staticmethod
    def scratch(rows, width):
        return [VMEM((4, rows, width), BF16), VMEM((3, rows, width), BF16), VMEM((2, rows // 2, width), BF16),
                VMEM((2, rows, width), BF16), pltpu.SemaphoreType.DMA((10,)), pltpu.SemaphoreType.DMA((10,))]

    def part(self, core, i):
        return self.parts.at[core * 4 + self.order[i]]

    def give(self, i):
        remote(self.part(1 - self.c, i), self.near.at[i], self.sems, (i,), self.other).start()

    def pair(self, i, rows=slice(None)):
        return self.part(self.c, i)[rows].astype(F32) + self.near[i, rows].astype(F32)

    def got(self, i):
        remote(self.near.at[i], self.near.at[i], self.sems, (i,), self.other).wait_recv()

    def piece(self, name):
        h = self.half.shape[1]
        low, high = pl.ds(0, h), pl.ds(h, h)
        n = ("far_up", "far_down", "up_high", "down_low", "up_low", "down_high").index(name)
        src = (self.sent.at[0, low], self.sent.at[0, high], self.sent.at[1, high], self.sent.at[2, low],
               self.sent.at[1, low], self.sent.at[2, high])[n]
        dst = (self.half.at[0], self.half.at[1], self.full.at[0, high], self.full.at[1, low],
               self.full.at[0, low], self.full.at[1, high])[n]
        return remote(src, dst, self.sems, (4 + n,), (self.up, self.down)[n % 2])

    def far(self):
        self.got(0)
        self.sent[0] = self.pair(0).astype(BF16)
        self.piece("far_up").start()
        self.piece("far_down").start()

    def near_first(self):
        h = self.half.shape[1]
        self.got(1)
        self.sent[1, pl.ds(h, h)] = self.pair(1, pl.ds(h, h)).astype(BF16)
        self.piece("up_high").start()
        self.got(2)
        self.sent[2, pl.ds(0, h)] = self.pair(2, pl.ds(0, h)).astype(BF16)
        self.piece("down_low").start()

    def near_second(self):
        h = self.half.shape[1]
        self.piece("far_up").wait_recv()
        self.sent[1, pl.ds(0, h)] = (self.pair(1, pl.ds(0, h)) + self.half[0].astype(F32)).astype(BF16)
        self.piece("up_low").start()
        self.piece("far_down").wait_recv()
        self.sent[2, pl.ds(h, h)] = (self.pair(2, pl.ds(h, h)) + self.half[1].astype(F32)).astype(BF16)
        self.piece("down_high").start()

    def total(self):
        self.got(3)
        for name in ("up_high", "down_low", "up_low", "down_high"):
            self.piece(name).wait_recv()
        return self.pair(3) + self.full[0].astype(F32) + self.full[1].astype(F32)

    def finish(self):
        for name in ("far_up", "far_down", "up_high", "down_low", "up_low", "down_high"):
            self.piece(name).wait_send()
        for i in range(4):
            remote(self.part(1 - self.c, i), self.near.at[i], self.sems, (i,), self.other).wait_send()


def params(cid, mib):
    return pltpu.CompilerParams(collective_id=cid, has_side_effects=True, vmem_limit_bytes=mib << 20)


def gather_kernel(count, by_rows, with_group, *refs):
    refs = list(refs)
    take = lambda n: [refs.pop(0) for _ in range(n)]
    x_ref = take(1)[0] if with_group else None
    shards = take(count)
    o_ref = take(1)[0] if with_group else None
    wholes = take(count)
    peers = plane_peers() + ring_peers()
    meet(peers)
    if with_group:
        local, send, recv = take(3)
        group = GroupGather(x_ref, o_ref, local, (send, recv))
        group.start()
    planes = []
    for i in range(count):
        local, send, recv = take(3)
        planes.append(PlaneGather(shards[i], wholes[i], by_rows[i], local, (send, recv)))
        planes[-1].start()
    if with_group:
        for j in range(2):
            group.near(j)
    for w in planes:
        for n in range(6):
            w.step(n)
    if with_group:
        for j in range(2, group.sub):
            group.near(j)
        group.far()
        group.finish()
    for w in planes:
        w.finish()


def gathers(cid, shards, by_rows, x=None):
    group = x is not None
    count = len(shards)
    outs = []
    if group:
        outs.append(jax.ShapeDtypeStruct((x.shape[0] * 8, x.shape[1]), x.dtype))
    for w, rows in zip(shards, by_rows):
        shape = (2048, w.shape[1]) if rows else (w.shape[0], 2048)
        outs.append(jax.ShapeDtypeStruct(shape, w.dtype))
    g = [pl.BlockSpec(memory_space=VMEM)] if group else []
    anys = [pl.BlockSpec(memory_space=ANY)] * count
    return pl.pallas_call(
        functools.partial(gather_kernel, count, tuple(by_rows), group), out_shape=outs,
        in_specs=g + anys, out_specs=g + anys,
        scratch_shapes=(GroupGather.semaphores() if group else []) + PlaneGather.semaphores() * count,
        compiler_params=params(cid, 16), name=f"gathers_{cid}")(*([x] if group else []), *shards)


def sum_kernel(p_ref, o_ref, near, sent, half, full, send, recv):
    meet(ring_peers())
    s = GroupSum(p_ref, near, sent, half, full, (send, recv))
    for i in range(4):
        s.give(i)
    s.far()
    s.near_first()
    s.near_second()
    o_ref[...] = s.total()
    s.finish()


def group_sum(parts, cid):
    rows, width = parts.shape[0] // 8, parts.shape[1]
    return pl.pallas_call(
        sum_kernel, out_shape=jax.ShapeDtypeStruct((rows, width), F32),
        in_specs=[pl.BlockSpec(memory_space=VMEM)], out_specs=pl.BlockSpec(memory_space=VMEM),
        scratch_shapes=GroupSum.scratch(rows, width), compiler_params=params(cid, 24),
        name=f"group_sum_{cid}")(parts.reshape(8, rows, width))


def ag_kernel(x_ref, o_ref, local_sem, send, recv):
    meet(ring_peers())
    g = GroupGather(x_ref, o_ref, local_sem, (send, recv))
    g.start()
    for j in range(g.sub):
        g.near(j)
    g.far()
    g.finish()


def group_gather(x, cid):
    return pl.pallas_call(
        ag_kernel, out_shape=jax.ShapeDtypeStruct((x.shape[0] * 8, x.shape[1]), x.dtype),
        in_specs=[pl.BlockSpec(memory_space=VMEM)], out_specs=pl.BlockSpec(memory_space=VMEM),
        scratch_shapes=GroupGather.semaphores(), compiler_params=params(cid, 16), name=f"group_gather_{cid}")(x)


SWAP = ((0, 0), (1, 2), (2, 1), (3, 3))


def swap(a):
    return lax.ppermute(a, ("c", "xh"), SWAP)


def layer_norm(rows_in, gain, shift):
    row_mean = jnp.mean(rows_in, axis=-1, keepdims=True)
    centered = rows_in - row_mean
    variance = jnp.mean(centered * centered, axis=-1, keepdims=True)
    return centered * lax.rsqrt(variance + EPSILON) * gain + shift


def norm_back(rows_in, gain, grad):
    row_mean = jnp.mean(rows_in, axis=-1, keepdims=True)
    centered = rows_in - row_mean
    inverse = lax.rsqrt(jnp.mean(centered * centered, axis=-1, keepdims=True) + EPSILON)
    n = centered * inverse
    e = gain * grad
    return (e - jnp.mean(e, axis=-1, keepdims=True) - n * jnp.mean(e * n, axis=-1, keepdims=True)) * inverse


def dot(a, b, dims=((1,), (0,))):
    return lax.dot_general(a, b, (dims, ((), ())), preferred_element_type=F32)


def dot_t(a, b):
    return dot(a, b, ((1,), (1,)))


def dot_o(a, b):
    return dot(a, b, ((0,), (0,)))


def exact_gelu(v):
    return jax.nn.gelu(v, approximate=False)


def scores_of(q, k, slope):
    n = q.shape[0]
    distance = (jnp.arange(n)[:, None] - jnp.arange(n)[None, :]).astype(F32)
    s = (dot_t(q, k) - slope * distance) * 0.125
    return jnp.where(distance >= 0, s, MASKED)


def attend(heads, slopes):
    outs, logs = [], []
    for h in range(4):
        q, k, v = (heads[:, h, i] for i in range(3))
        s = scores_of(q, k, slopes[h])
        top = jnp.max(s, axis=-1, keepdims=True)
        e = jnp.exp(s - top)
        total = jnp.sum(e, axis=-1, keepdims=True)
        outs.append(dot((e / total).astype(BF16), v).astype(BF16))
        logs.append(top + jnp.log(total))
    return jnp.concatenate(outs, axis=1), logs


def attend_back(heads, logs, grad, slopes):
    outs = []
    for h in range(4):
        q, k, v = (heads[:, h, i] for i in range(3))
        g = grad[:, h * 64:(h + 1) * 64]
        p = jnp.exp(scores_of(q, k, slopes[h]) - logs[h])
        dp = dot_t(g, v)
        ds = (p * (dp - jnp.sum(p * dp, axis=-1, keepdims=True))).astype(BF16)
        outs.append(jnp.stack((dot(ds, k) * 0.125, dot_o(ds, q) * 0.125, dot_o(p.astype(BF16), g)), axis=1))
    return jnp.stack(outs, axis=1).astype(BF16).reshape(grad.shape[0], 768)


def local(tokens, grad_out, adapter_ids, first_gain, first_shift, joined_weight, joined_bias, dense_weight,
          dense_bias, second_gain, second_shift, up_weight, up_bias, down_weight, down_bias, joined_adapt_in,
          joined_adapt_out, dense_adapt_in, dense_adapt_out, up_adapt_in, up_adapt_out, down_adapt_in,
          down_adapt_out):
    c, xh, z = lax.axis_index("c"), lax.axis_index("xh"), lax.axis_index("z")
    group = c * 4 + z
    own_id = adapter_ids[0]
    picked = [lax.dynamic_index_in_dim(a, own_id, 0, keepdims=False) for a in
              (joined_adapt_out, dense_adapt_in, up_adapt_out, down_adapt_in)]
    flat = swap(jnp.concatenate([a.ravel() for a in picked]))
    biases = swap(jnp.concatenate([joined_bias, up_bias]))
    set_id = swap(adapter_ids)
    pick_joined_out = flat[:12288].reshape(16, 768)
    pick_dense_in = flat[12288:16384].reshape(256, 16)
    pick_up_out = flat[16384:32768].reshape(16, 1024)
    pick_down_in = flat[32768:].reshape(1024, 16)
    b_joined, b_up = biases[:768], biases[768:]
    pick_joined_in, pick_dense_out, pick_up_in, pick_down_out = [
        lax.dynamic_index_in_dim(a, set_id[0], 0, keepdims=False) for a in
        (joined_adapt_in, dense_adapt_out, up_adapt_in, down_adapt_out)]
    slopes = jnp.exp2(-8.0 * (group * 4 + jnp.arange(4) + 1).astype(F32) / HEADS)
    tokens = swap(tokens)
    grad_out = swap(grad_out)
    residual_in = tokens.astype(F32)
    x1 = layer_norm(residual_in, first_gain, first_shift).astype(BF16)
    x1_all, w_joined = gathers(1, [joined_weight], [True], x1)
    low_joined = dot(x1_all, pick_joined_in).astype(BF16)
    joined = (dot(x1_all, w_joined) + dot(low_joined, pick_joined_out) + b_joined).astype(BF16)
    go_all, w_dense, w_up = gathers(2, [dense_weight, up_weight], [False, True], grad_out)
    heads = joined.reshape(1024, 4, 3, 64)
    context, logs = attend(heads, slopes)
    low_dense = dot(context, pick_dense_in).astype(BF16)
    attn = (dot(context, w_dense) + dot(low_dense, pick_dense_out)).astype(BF16)
    mid = residual_in + group_sum(attn, 3) + dense_bias
    x2 = layer_norm(mid, second_gain, second_shift).astype(BF16)
    x2_all, w_down = gathers(4, [down_weight], [False], x2)
    low_up = dot(x2_all, pick_up_in).astype(BF16)
    pre = dot(x2_all, w_up) + dot(low_up, pick_up_out) + b_up
    act = exact_gelu(pre).astype(BF16)
    low_down = dot(act, pick_down_in).astype(BF16)
    mlp = (dot(act, w_down) + dot(low_down, pick_down_out)).astype(BF16)
    layer_out = swap((mid + group_sum(mlp, 5) + down_bias).astype(BF16))
    grad_low_down = dot_t(go_all, pick_down_out).astype(BF16)
    grad_act = dot_t(go_all, w_down) + dot_t(grad_low_down, pick_down_in)
    grad_pre = jax.vjp(exact_gelu, pre)[1](grad_act)[0].astype(BF16)
    grad_low_up = dot_t(grad_pre, pick_up_out).astype(BF16)
    part_two = (dot_t(grad_pre, w_up) + dot_t(grad_low_up, pick_up_in)).astype(BF16)
    grad_mid = grad_out.astype(F32) + norm_back(mid, second_gain, group_sum(part_two, 6))
    ga_all = group_gather(grad_mid.astype(BF16), 7)
    grad_low_dense = dot_t(ga_all, pick_dense_out).astype(BF16)
    grad_context = (dot_t(ga_all, w_dense) + dot_t(grad_low_dense, pick_dense_in)).astype(BF16)
    grad_joined = attend_back(heads, logs, grad_context, slopes)
    grad_low_joined = dot_t(grad_joined, pick_joined_out).astype(BF16)
    part_one = (dot_t(grad_joined, w_joined) + dot_t(grad_low_joined, pick_joined_in)).astype(BF16)
    grad_tokens = swap(grad_mid + norm_back(residual_in, first_gain, group_sum(part_one, 8)))

    lows = jnp.concatenate([grad_low_joined, low_dense, grad_low_up, low_down], axis=1)
    lows = lax.psum(lows.astype(F32), ("c", "z")).astype(BF16)
    cols = [lax.dynamic_slice_in_dim(a, group * 256, 256, 1) for a in (x1_all, ga_all, x2_all, go_all)]
    halves = jnp.concatenate([dot_o(lows[:, i * 16:(i + 1) * 16], cols[i]) for i in range(4)], axis=1)
    wide = jnp.concatenate([dot_o(low_joined, grad_joined), dot_o(grad_low_dense, context), dot_o(low_up, grad_pre),
                            dot_o(grad_low_down, act)], axis=1)
    mine = jnp.concatenate([wide, halves], axis=1).astype(BF16)
    every = lax.all_gather(mine, PLANE, axis=0, tiled=False)
    ids = lax.all_gather(set_id, PLANE, axis=0, tiled=True)
    onehot = (jnp.arange(8)[:, None] == ids[None, :]).astype(BF16)
    sums = lax.dot_general(onehot, every, (((1,), (0,)), ((), ())), preferred_element_type=F32)
    split = swap(sums[:, :, :3072].astype(BF16)).astype(F32)
    whole = lax.all_gather(sums[:, :, 3072:].astype(BF16), ("c", "z"), axis=0, tiled=False).astype(F32)
    whole = whole.reshape(8, 8, 16, 4, 256)
    per = [whole[:, :, :, i].transpose(1, 2, 0, 3).reshape(8, 16, 2048) for i in range(4)]
    turn = lambda a: jnp.swapaxes(a, 1, 2)
    return (layer_out, grad_tokens, turn(per[0]), split[:, :, :768], turn(split[:, :, 768:1024]), per[1],
            turn(per[2]), split[:, :, 1024:2048], turn(split[:, :, 2048:3072]), per[3])


def solution(mesh):
    fine = Mesh(mesh.devices.reshape(2, 4, 2, 2, 4), AXES)
    rows, cols = P(FSDP, TP), P(TP, FSDP)
    tok = P((*FSDP, *TP), None)
    last, middle, one = P(None, None, TP), P(None, TP, None), P(TP)
    return jax.shard_map(
        local, mesh=fine,
        in_specs=(tok, tok, P(FSDP), P(), P(), rows, one, cols, P(), P(), P(), rows, one, cols, P(), P(), last,
                  middle, P(), P(), last, middle, P()),
        out_specs=(tok, tok, P(), last, middle, P(), P(), last, middle, P()), check_vma=False)
```

time: 982 us -> 596 us (0.61)
  waiting for transfers between devices: 666 us -> 79.1 us
  Pallas kernels: 0 us -> 248 us
  other arithmetic: 40.9 us -> 15.9 us
  blocking collectives: 62.2 us -> 38 us
  starting transfers between devices: 16.5 us -> 32.1 us
  matrix products: 139 us -> 127 us
    all_gather x8 -> x2, waiting for transfers between devices: 335 us -> 57.1 us  [the longest x1 57.1 us: local(): every = lax.all_gather(mine, PLANE, axis=0, tiled=False)]
    pallas_call x0 -> x8, Pallas kernels: none -> 248 us  [the longest x3 115 us: gathers(): pl.pallas_call(functools.partial(gather_kernel, count, tuple(by_rows), gr...]
    psum x2 -> x0, waiting for transfers between devices: 247 us -> none  [the longest x1 145 us: local(): lax.psum((spread(onehot_high, term_joined_in), spread(onehot_high, term_d...]
    all_to_all x3 -> x0, waiting for transfers between devices: 81.6 us -> none  [sum_at_owner(): lax.all_to_all(blocks, axis, split_axis=0, concat_axis=0, tiled=True)]
    all_to_all x1 -> x0, blocking collectives: 62.2 us -> none  [sum_at_owner(): lax.all_to_all(blocks, axis, split_axis=0, concat_axis=0, tiled=True)]
    ppermute x0 -> x8, starting transfers between devices: none -> 32 us  [swap(): return lax.ppermute(a, ('c', 'xh'), SWAP)]
    psum x0 -> x1, blocking collectives: none -> 26.5 us  [local(): lows = lax.psum(lows.astype(F32), ('c', 'z')).astype(BF16)]
    ppermute x0 -> x8, waiting for transfers between devices: none -> 22 us  [swap(): return lax.ppermute(a, ('c', 'xh'), SWAP)]
  transfers between devices with their start and end apart: 13 -> 10, of which waited for: 12 -> 3; matrix products, arithmetic and copies ran while one was open for 13% -> 8% of each run, Pallas kernels for 0% -> 12%
where the time goes in v1:
time: 596 us; the launch traced here: 592 us
  Pallas kernels  248 us (42%)
  matrix products  127 us (21%)
  waiting for transfers between devices  79.1 us (13%)
  blocking collectives  38 us (6%)
  local copies, waits for them, and re-layouts  33.2 us (6%)
  starting transfers between devices  32.1 us (5%)
  between operations  18 us (3%)
  other arithmetic  15.9 us (3%)
    dot_general x56, matrix products, dot(): return lax.dot_general(a, b, (dims, ((), ())), preferred_element_type=F32)  123 us
    pallas_call x3, Pallas kernels, gathers(): pl.pallas_call(functools.partial(gather_kernel, count, tuple(by_rows), gr...  115 us
    pallas_call x4, Pallas kernels, group_sum(): pl.pallas_call(sum_kernel, out_shape=jax.ShapeDtypeStruct((rows, width),...  111 us
    all_gather x1, waiting for transfers between devices, local(): every = lax.all_gather(mine, PLANE, axis=0, tiled=False)  57.1 us
    ppermute x8, starting transfers between devices, swap(): return lax.ppermute(a, ('c', 'xh'), SWAP)  32 us
    psum x1, blocking collectives, local(): lows = lax.psum(lows.astype(F32), ('c', 'z')).astype(BF16)  26.5 us
    pallas_call x1, Pallas kernels, group_gather(): pl.pallas_call(ag_kernel, out_shape=jax.ShapeDtypeStruct((x.shape[0] * 8,...  22.8 us
    ppermute x8, waiting for transfers between devices, swap(): return lax.ppermute(a, ('c', 'xh'), SWAP)  22 us
  transfers between devices with their start and end apart: 10, of which 3 were waited for; matrix products, arithmetic and copies ran while one was open for 8% of the time, Pallas kernels for 12%

profile of v1, /device:TPU:1, one launch (start us, length us, event | category | flops | bytes accessed | tf_op | source)
XLA Modules:
  0.0 591.7 jit_solution(4878429790256113121)
XLA Ops:
  7.2 6.2 %collective-permute-start.1 = (s32[1]{0:T(128)}, s32[1]{0:T(128)}, u32[]{:S(2)}, u32[]{:S(2)}) collective-permute-start(s32[1]{0:T(128)} %param.25), channel_id=1, source_target_pairs={{0,0},{4,8},{8,4},{12,12},{1,1},{5,9},{9,5},{13,13},{2,2},{6,10},{... | collective-permute-start | bytes 20 | tf_op jit(solution)/shard_map/ppermute | solution.py:427
  14.1 1.9 collective-permute-start.3
  20.4 5.1 collective-permute-start.2
  25.5 1.9 collective-permute-start
  27.4 5.1 collective-permute-start.4
  35.6 2.1 collective-permute-done
  40.0 32.9 %gathers_1.1 = (bf16[1024,2048]{1,0:T(8,128)(2,1)S(1)}, bf16[2048,768]{1,0:T(8,128)(2,1)S(1)}) custom-call(bf16[128,2048]{1,0:T(8,128)(2,1)S(1)} %fusion.98.refs_0_, bf16[128,768]{1,0:T(8,128)(2,1)S(1)} %copy-done.8), custom_call_target="tpu_custom_call" | custom-call | tf_op jit(solution)/shard_map/gathers_1/pallas_call | solution.py:378
  73.0 2.1 convolution_convert_fusion.8
  75.9 3.5 add_convert_fusion.5
  79.4 2.2 fusion.164
  83.6 2.2 fusion.165
  87.7 2.8 fusion.166
  92.4 2.2 fusion.167
  96.8 5.4 fusion.127
  102.2 43.7 %gathers_2.1 = (bf16[1024,2048]{1,0:T(8,128)(2,1)S(1)}, bf16[256,2048]{1,0:T(8,128)(2,1)S(1)}, bf16[2048,1024]{1,0:T(8,128)(2,1)S(1)}) custom-call(bf16[128,2048]{1,0:T(8,128)(2,1)S(1)} %collective-permute-done.4.refs_0_, bf16[256,128]{1,0:T(8,128)(2,1)S(1)} %copy-done.9, bf16[128,1024]{1,0:T(8,128)(2,1)S(1)} %copy-done.7), custom_call_target="tpu_custom_call" | custom-call | tf_op jit(solution)/shard_map/gathers_2/pallas_call | solution.py:378
  146.0 6.2 %add_convert_fusion.3 = bf16[1024,2048]{1,0:T(8,128)(2,1)S(1)} fusion(f32[1024,2048]{1,0:T(8,128)} %fusion.127, bf16[256,2048]{1,0:T(8,128)(2,1)S(1)} %get-tuple-element.19, bf16[1024,64]{0,1:T(8,128)(2,1)S(1)} %fusion.57, bf16[1024,64]{0,1:T(8,128)(2,1)S(1)} %fusion.58, bf16[1024,64]{0,1:T(8,128)(2,1)S(1)} %fusion.59, bf16[1024,64]{0,1:T(8,128)(2,1)S(1)} %fusion.60), kind=kOutput, calls=%fused_computation.3 | convolution fusion | flops 1080033280 | bytes 14155776 | tf_op jit(solution)/shard_map/dot_general | solution.py:447
  152.2 23.0 %group_sum_3.1 = f32[128,2048]{1,0:T(8,128)S(1)} custom-call(bf16[8,128,2048]{2,1,0:T(8,128)(2,1)S(1)} %bitcast.263), custom_call_target="tpu_custom_call" | custom-call | tf_op jit(solution)/shard_map/group_sum_3/pallas_call | solution.py:399
  177.0 2.7 fusion.172
  179.9 38.1 %gathers_4.1 = (bf16[1024,2048]{1,0:T(8,128)(2,1)S(1)}, bf16[1024,2048]{1,0:T(8,128)(2,1)S(1)}) custom-call(bf16[128,2048]{1,0:T(8,128)(2,1)S(1)} %add_convert_fusion.7.refs_0_, bf16[1024,128]{1,0:T(8,128)(2,1)S(1)} %copy-done.6), custom_call_target="tpu_custom_call" | custom-call | tf_op jit(solution)/shard_map/gathers_4/pallas_call | solution.py:378
  218.0 2.1 convolution_convert_fusion.7
  220.2 2.8 fusion.169
  223.0 16.8 %multiply_convert_fusion.4 = (bf16[1024,1024]{0,1:T(8,128)(2,1)S(1)}, f32[1024,1024]{0,1:T(8,128)}, f32[1024,1024]{0,1:T(8,128)}) fusion(f32[1024]{0:T(1024)S(1)} %slice.238, f32[1024,1024]{0,1:T(8,128)} %fusion.169, bf16[1024,2048]{1,0:T(8,128)(2,1)S(1)} %get-tuple-element.20, bf16[2048,1024]{1,0:T(8,128)(2,1)S(1)} %get-tuple-element.21), kind=kOutput, calls=%fused_computation.20 | convolution fusion | flops 4365221888 | bytes 23072768 | tf_op jit(solution)/shard_map/dot_general | solution.py:447
  240.3 9.1 %fusion.170 = f32[1024,2048]{1,0:T(8,128)} fusion(bf16[1024,1024]{0,1:T(8,128)(2,1)S(1)} %get-tuple-element.60, bf16[1024,2048]{1,0:T(8,128)(2,1)} %copy-done.10), kind=kOutput, calls=%fused_computation.272 | convolution fusion | flops 4294967296 | bytes 14680064 | tf_op jit(solution)/shard_map/dot_general | solution.py:447
  249.4 8.9 %add_convert_fusion.4 = bf16[1024,1024]{0,1:T(8,128)(2,1)S(1)} fusion(f32[1024,1024]{0,1:T(8,128)} %get-tuple-element.61, f32[1024,1024]{0,1:T(8,128)} %fusion.172, f32[1024,1024]{0,1:T(8,128)} %get-tuple-element.83, bf16[1024,2048]{1,0:T(8,128)(2,1)S(1)} %get-tuple-element.23, bf16[1024,2048]{1,0:T(8,128)(2,1)S(1)} %copy-done.11), kind=kOutput, calls=%fused_computation.19 | convolution fusion | flops 4310695936 | bytes 23068672 | tf_op jit(solution)/shard_map/dot_general | solution.py:447
  258.7 5.0 add_convert_fusion.2
  263.7 23.5 %group_sum_5.1 = f32[128,2048]{1,0:T(8,128)S(1)} custom-call(bf16[8,128,2048]{2,1,0:T(8,128)(2,1)S(1)} %bitcast.265), custom_call_target="tpu_custom_call" | custom-call | tf_op jit(solution)/shard_map/group_sum_5/pallas_call | solution.py:399
  287.2 5.5 fusion.123
  292.8 7.2 %add_convert_fusion.1 = bf16[1024,2048]{1,0:T(8,128)(2,1)S(1)} fusion(f32[1024,2048]{1,0:T(8,128)} %fusion.123, bf16[1024,1024]{0,1:T(8,128)(2,1)S(1)} %copy-done.22, bf16[2048,1024]{1,0:T(8,128)(2,1)S(1)} %get-tuple-element.21), kind=kOutput, calls=%fused_computation.1 | convolution fusion | flops 4299161600 | bytes 18874368 | tf_op jit(solution)/shard_map/dot_general | solution.py:447
  300.0 23.5 %group_sum_6.1 = f32[128,2048]{1,0:T(8,128)S(1)} custom-call(bf16[8,128,2048]{2,1,0:T(8,128)(2,1)S(1)} %bitcast.266), custom_call_target="tpu_custom_call" | custom-call | tf_op jit(solution)/shard_map/group_sum_6/pallas_call | solution.py:399
  323.9 1.8 fusion.158
  325.7 22.8 %group_gather_7.1 = bf16[1024,2048]{1,0:T(8,128)(2,1)S(1)} custom-call(bf16[128,2048]{1,0:T(8,128)(2,1)S(1)} %get-tuple-element.58.x_ref), custom_call_target="tpu_custom_call" | custom-call | tf_op jit(solution)/shard_map/group_gather_7/pallas_call | solution.py:417
  348.6 2.1 convolution_convert_fusion.5
  376.0 26.5 %all-reduce.2 = bf16[1024,64]{0,1:T(8,128)(2,1)S(1)} all-reduce(f32[1024,64]{0,1:T(8,128)S(1)} %maximum_convert_fusion), channel_id=1, replica_groups=mesh['xl'=2,'y'=4,'c'=2,'xh'=2,'z'=4] {'c','z'}, use_global_device_ids=true, to_apply=%region_20.21 | all-reduce | flops 65536 | bytes 393216 | tf_op jit(solution)/shard_map/psum | solution.py:551
  410.1 11.5 %all-reduce = s32[16]{0:T(128)S(1)} all-reduce(s32[16]{0:T(128)S(1)} %dynamic-update-slice), channel_id=1, replica_groups=mesh['xl'=2,'y'=4,'c'=2,'xh'=2,'z'=4] {'xl','y','xh'}, use_global_device_ids=true, to_apply=%add | all-reduce | flops 16 | bytes 128
  421.6 57.1 %all-gather.4.cloned.1.call-done = bf16[16,16,4096]{2,1,0:T(8,128)(2,1)} async-done(((bf16[1,16,4096]{2,1,0:T(8,128)(2,1)}), bf16[16,16,4096]{2,1,0:T(8,128)(2,1)}) %all-gather.4.cloned.1.call-update) | async-done | bytes 2097168 | tf_op jit(solution)/shard_map/all_gather | solution.py:557
  478.7 3.9 convolution_convert_fusion
  484.3 5.4 fusion.171
  489.7 2.1 add_convert_fusion
  491.9 40.5 %group_sum_8.1 = f32[128,2048]{1,0:T(8,128)S(1)} custom-call(bf16[8,128,2048]{2,1,0:T(8,128)(2,1)S(1)} %bitcast.264), custom_call_target="tpu_custom_call" | custom-call | tf_op jit(solution)/shard_map/group_sum_8/pallas_call | solution.py:399
  533.3 4.4 collective-permute-start.6
  537.8 2.7 collective-permute-start.7
  540.5 4.6 collective-permute-start.5
  545.1 19.9 %collective-permute-done.5 = bf16[128,2048]{1,0:T(8,128)(2,1)S(1)} collective-permute-done((bf16[128,2048]{1,0:T(8,128)(2,1)S(1)}, bf16[128,2048]{1,0:T(8,128)(2,1)S(1)}, u32[]{:S(2)}, u32[]{:S(2)}) %collective-permute-start.5) | collective-permute-done | bytes 524320 | tf_op jit(solution)/shard_map/ppermute | solution.py:427
  569.2 2.1 convert.114
  571.3 1.8 slice_bitcast_fusion
  574.6 1.6 copy.70
  577.3 1.6 copy.69
  582.3 2.3 copy.97
  (227 shorter events, 65.2 us)
Async XLA Ops:
  7.2 168.6 %copy-start = (bf16[8,16,2048]{2,1,0:T(8,128)(2,1)S(1)}, bf16[8,16,2048]{2,1,0:T(8,128)(2,1)}, u32[]{:S(2)}) copy-start(bf16[8,16,2048]{2,1,0:T(8,128)(2,1)} %param.45) | copy-start | bytes 1572868
  7.2 32.8 %copy-start.8 = (bf16[128,768]{1,0:T(8,128)(2,1)S(1)}, bf16[128,768]{1,0:T(8,128)(2,1)}, u32[]{:S(2)}) copy-start(bf16[128,768]{1,0:T(8,128)(2,1)} %refs_1_.3) | copy-start | bytes 589828
  7.2 471.5 %all-gather.4.cloned.1.call-start = ((), (), s32[]{:S(2)}) async-start(), calls=%async_computation | async-start | bytes 2228224 | tf_op jit(solution)/shard_map/all_gather | solution.py:557
  7.2 26.0 %collective-permute-start.1 = (s32[1]{0:T(128)}, s32[1]{0:T(128)}, u32[]{:S(2)}, u32[]{:S(2)}) collective-permute-start(s32[1]{0:T(128)} %param.25), channel_id=1, source_target_pairs={{0,0},{4,8},{8,4},{12,12},{1,1},{5,9},{9,5},{13,13},{2,2},{6,10},{... | collective-permute-start | bytes 20 | tf_op jit(solution)/shard_map/ppermute | solution.py:427
  14.1 21.0 %collective-permute-start.3 = (f32[1792]{0:T(1024)S(1)}, f32[1792]{0:T(1024)S(1)}, u32[]{:S(2)}, u32[]{:S(2)}) collective-permute-start(f32[1792]{0:T(1024)S(1)} %pad_maximum_fusion.3), channel_id=1, source_target_pairs={{0,0},{4,8},{8,4},{12,12},{1,1},{5,9},{9,5},{13,13},{2,2},{6,10},{... | collective-permute-start | bytes 21512 | tf_op jit(solution)/shard_map/ppermute | solution.py:427
  20.4 14.8 %collective-permute-start.2 = (bf16[49152]{0:T(1024)(128)(2,1)S(1)}, bf16[49152]{0:T(1024)(128)(2,1)S(1)}, u32[]{:S(2)}, u32[]{:S(2)}) collective-permute-start(bf16[49152]{0:T(1024)(128)(2,1)S(1)} %pad_maximum_fusion.2), channel_id=1, source_target_pairs={{0,0},{4,8},{8,4},{12,12},{1,1},{5,9},{9,5},{13,13},{2,2},{6,10},{... | collective-permute-start | bytes 294920 | tf_op jit(solution)/shard_map/ppermute | solution.py:427
  25.5 12.2 %collective-permute-start = (bf16[128,2048]{1,0:T(8,128)(2,1)}, bf16[128,2048]{1,0:T(8,128)(2,1)S(1)}, u32[]{:S(2)}, u32[]{:S(2)}) collective-permute-start(bf16[128,2048]{1,0:T(8,128)(2,1)} %param.23), channel_id=1, source_target_pairs={{0,0},{4,8},{8,4},{12,12},{1,1},{5,9},{9,5},{13,13},{2,2},{6,10},{... | collective-permute-start | bytes 1572872 | tf_op jit(solution)/shard_map/ppermute | solution.py:427
  27.4 74.8 %collective-permute-start.4 = (bf16[128,2048]{1,0:T(8,128)(2,1)}, bf16[128,2048]{1,0:T(8,128)(2,1)S(1)}, u32[]{:S(2)}, u32[]{:S(2)}) collective-permute-start(bf16[128,2048]{1,0:T(8,128)(2,1)} %param.24), channel_id=1, source_target_pairs={{0,0},{4,8},{8,4},{12,12},{1,1},{5,9},{9,5},{13,13},{2,2},{6,10},{... | collective-permute-start | bytes 1572872 | tf_op jit(solution)/shard_map/ppermute | solution.py:427
  35.2 39.9 %copy-start.32 = (bf16[16,768]{1,0:T(8,128)(2,1)}, bf16[16,768]{1,0:T(8,128)(2,1)S(1)}, u32[]{:S(2)}) copy-start(bf16[16,768]{1,0:T(8,128)(2,1)S(1)} %slice.179) | copy-start | bytes 73732
  73.0 2.8 copy-start.3
  73.0 2.9 copy-start.12
  75.1 4.3 copy-start.30
  79.4 15.9 %copy-start.26 = (bf16[1024,768]{0,1:T(8,128)(2,1)}, bf16[1024,768]{0,1:T(8,128)(2,1)S(1)}, u32[]{:S(2)}) copy-start(bf16[1024,768]{0,1:T(8,128)(2,1)S(1)} %add_convert_fusion.5) | copy-start | bytes 4718596
  87.7 58.3 %copy-start.35 = (bf16[1024,64]{0,1:T(8,128)(2,1)}, bf16[1024,64]{0,1:T(8,128)(2,1)S(1)}, u32[]{:S(2)}) copy-start(bf16[1024,64]{0,1:T(8,128)(2,1)S(1)} %fusion.58) | copy-start | bytes 393220
  90.4 2.0 copy-start.15
  92.4 53.5 %copy-start.37 = (bf16[1024,64]{0,1:T(8,128)(2,1)}, bf16[1024,64]{0,1:T(8,128)(2,1)S(1)}, u32[]{:S(2)}) copy-start(bf16[1024,64]{0,1:T(8,128)(2,1)S(1)} %fusion.59) | copy-start | bytes 393220
  94.6 2.0 copy-start.13
  96.6 49.4 %copy-start.39 = (bf16[1024,64]{0,1:T(8,128)(2,1)}, bf16[1024,64]{0,1:T(8,128)(2,1)S(1)}, u32[]{:S(2)}) copy-start(bf16[1024,64]{0,1:T(8,128)(2,1)S(1)} %fusion.60) | copy-start | bytes 393220
  96.8 5.4 copy-start.7
  96.8 5.4 copy-start.9
  145.9 103.5 %copy-start.4 = (bf16[1024,2048]{1,0:T(8,128)(2,1)}, bf16[1024,2048]{1,0:T(8,128)(2,1)S(1)}, u32[]{:S(2)}) copy-start(bf16[1024,2048]{1,0:T(8,128)(2,1)S(1)} %get-tuple-element.23) | copy-start | bytes 12582916
  152.2 23.0 %copy-start.45 = (f32[2048]{0:T(1024)S(1)}, f32[2048]{0:T(1024)}, u32[]{:S(2)}) copy-start(f32[2048]{0:T(1024)} %param.31) | copy-start | bytes 24580
  175.7 3.9 copy-start.41
  175.8 3.9 copy-start.46
  176.9 2.9 copy-start.6
  218.0 5.0 copy-start.10
  218.0 5.0 copy-start.5
  240.3 9.1 %copy-start.11 = (bf16[1024,2048]{1,0:T(8,128)(2,1)S(1)}, bf16[1024,2048]{1,0:T(8,128)(2,1)}, u32[]{:S(2)}) copy-start(bf16[1024,2048]{1,0:T(8,128)(2,1)} %copy-done.10) | copy-start | bytes 12582916
  258.3 5.4 copy-start.21
  287.2 5.5 copy-start.22
  300.0 23.9 %copy-start.47 = (f32[2048]{0:T(1024)S(1)}, f32[2048]{0:T(1024)}, u32[]{:S(2)}) copy-start(f32[2048]{0:T(1024)} %param.37) | copy-start | bytes 24580
  348.5 3.7 copy-start.2
  350.9 2.2 copy-start.20
  356.6 2.2 copy-start.18
  361.7 2.2 copy-start.16
  366.7 2.2 copy-start.14
  374.6 33.6 %copy-start.50 = (u32[128]{0:T(128)S(1)}, u32[128]{0:T(128)}, u32[]{:S(2)}) copy-start(u32[128]{0:T(128)} %constant.140) | copy-start | bytes 1540
  408.1 161.1 %all-gather.6.cloned.1.call-start = ((), (), s32[]{:S(2)}) async-start(), calls=%async_computation.1 | async-start | bytes 2359296 | tf_op jit(solution)/shard_map/all_gather | solution.py:562
  491.8 40.6 %copy-start.42 = (f32[2048]{0:T(1024)S(1)}, f32[2048]{0:T(1024)}, u32[]{:S(2)}) copy-start(f32[2048]{0:T(1024)} %param.26) | copy-start | bytes 24580
  491.8 40.6 %copy-start.44 = (f32[128]{0:T(128)S(1)}, f32[128]{0:T(128)}, u32[]{:S(2)}) copy-start(f32[128]{0:T(128)} %copy-done.43) | copy-start | bytes 1540
  491.8 40.6 %copy-start.49 = (f32[128]{0:T(128)S(1)}, f32[128]{0:T(128)}, u32[]{:S(2)}) copy-start(f32[128]{0:T(128)} %copy-done.48) | copy-start | bytes 1540
  491.8 40.9 %copy-start.25 = (f32[128,2048]{1,0:T(8,128)S(1)}, f32[128,2048]{1,0:T(8,128)}, u32[]{:S(2)}) copy-start(f32[128,2048]{1,0:T(8,128)} %get-tuple-element.59) | copy-start | bytes 3145732
  491.8 45.9 %copy-start.24 = (bf16[8,16,4096]{2,0,1:T(8,128)(2,1)S(1)}, bf16[8,16,4096]{2,0,1:T(8,128)(2,1)}, u32[]{:S(2)}) copy-start(bf16[8,16,4096]{2,0,1:T(8,128)(2,1)} %copy-done.23) | copy-start | bytes 3145732
  532.4 8.1 %copy-start.29 = (bf16[128,2048]{1,0:T(8,128)(2,1)S(1)}, bf16[128,2048]{1,0:T(8,128)(2,1)}, u32[]{:S(2)}) copy-start(bf16[128,2048]{1,0:T(8,128)(2,1)} %get-tuple-element.68) | copy-start | bytes 1572868
  533.3 31.7 %collective-permute-start.6 = (f32[128,2048]{1,0:T(8,128)S(1)}, f32[128,2048]{1,0:T(8,128)S(1)}, u32[]{:S(2)}, u32[]{:S(2)}) collective-permute-start(f32[128,2048]{1,0:T(8,128)S(1)} %fusion.102), channel_id=1, source_target_pairs={{0,0},{4,8},{8,4},{12,12},{1,1},{5,9},{9,5},{13,13},{2,2},{6,10},{... | collective-permute-start | bytes 3145736 | tf_op jit(solution)/shard_map/ppermute | solution.py:427
  537.8 27.2 %collective-permute-start.7 = (bf16[8,16,3072]{2,0,1:T(8,128)(2,1)S(1)}, bf16[8,16,3072]{2,0,1:T(8,128)(2,1)S(1)}, u32[]{:S(2)}, u32[]{:S(2)}) collective-permute-start(bf16[8,16,3072]{2,0,1:T(8,128)(2,1)S(1)} %slice.250), channel_id=1, source_target_pairs={{0,0},{4,8},{8,4},{12,12},{1,1},{5,9},{9,5},{13,13},{2,2},{6,10},{... | collective-permute-start | bytes 2359304 | tf_op jit(solution)/shard_map/ppermute | solution.py:427
  540.5 24.5 %collective-permute-start.5 = (bf16[128,2048]{1,0:T(8,128)(2,1)S(1)}, bf16[128,2048]{1,0:T(8,128)(2,1)S(1)}, u32[]{:S(2)}, u32[]{:S(2)}) collective-permute-start(bf16[128,2048]{1,0:T(8,128)(2,1)S(1)} %copy-done.29), channel_id=1, source_target_pairs={{0,0},{4,8},{8,4},{12,12},{1,1},{5,9},{9,5},{13,13},{2,2},{6,10},{... | collective-permute-start | bytes 1572872 | tf_op jit(solution)/shard_map/ppermute | solution.py:427
  578.9 5.7 copy-start.1
  (13 other events, 14.7 us)
Sparse Core Ops, SparseCore 0:
  408.2 70.4 all-gather.3
  484.4 39.9 all-gather.5

commit v2 on v1

v2 whole, which is shorter than its diff:
```python
import functools

import jax
import jax.numpy as jnp
from jax import lax
from jax.experimental import pallas as pl
from jax.experimental.pallas import tpu as pltpu
from jax.sharding import Mesh
from jax.sharding import PartitionSpec as P

HEADS = 32
EPSILON = 1e-05
MASKED = -1e30
AXES = ("xl", "y", "c", "xh", "z")
FSDP = ("xl", "y", "c")
TP = ("xh", "z")
PLANE = ("xl", "y", "xh")
MESH_ID = pl.DeviceIdType.MESH
ANY = pl.ANY
VMEM = pltpu.VMEM
DMA = pltpu.SemaphoreType.DMA
F32 = jnp.float32
BF16 = jnp.bfloat16
ORDER = (0, 3, 1, 2)
PICKS = dict(joined_in=(0, 2048), joined_out=(2048, 768), hot=(2816, 128), up_in=(2944, 2048), up_out=(4992, 1024),
             dense_in=(6016, 256), dense_out=(6272, 2048), down_in=(8320, 1024), down_out=(9344, 2048))
PICKED = 11392


def remote(src, dst, sems, index, device):
    send, recv = sems
    return pltpu.make_async_remote_copy(
        src_ref=src, dst_ref=dst, send_sem=send.at[index], recv_sem=recv.at[index],
        device_id=device, device_id_type=MESH_ID)


def places():
    return tuple(lax.axis_index(a) for a in AXES)


def at_home():
    _, _, c, xh, _ = places()
    return 1 - (xh - c) * (xh - c)


def meet(peers):
    barrier = pltpu.get_barrier_semaphore()
    for p in peers:
        pl.semaphore_signal(barrier, inc=1, device_id=p, device_id_type=MESH_ID)
    pl.semaphore_wait(barrier, len(peers))


def group_peer(n):
    _, _, c, _, z = places()
    return {"c": lax.rem(c + n // 4, 2), "z": lax.rem(z + n % 4, 4)}


def group_peers():
    return [group_peer(n) for n in range(1, 8)]


def diagonal():
    _, _, c, xh, _ = places()
    return {"c": 1 - c, "xh": 1 - xh}


def plane_peers():
    xl, y, c, xh, _ = places()
    peers = []
    for d in range(1, 4):
        for core in (0, 1):
            peers.append({"y": lax.rem(y + d, 4), "c": core})
            x = lax.rem(xh * 2 + xl + d, 4)
            peers.append({"xh": x // 2, "xl": lax.rem(x, 2), "c": core})
    return peers


def block(ref, n, size=128):
    return ref.at[pl.ds(pl.multiple_of(n * size, size), size)]


class GroupGather:
    SEMS = [DMA((8, 4)), DMA((8, 4))]

    def __init__(self, dst, send, recv):
        self.dst, self.sems = dst, (send, recv)
        _, _, self.c, _, self.z = places()
        self.up, self.down, self.other = group_peer(1), group_peer(3), group_peer(4)

    def at(self, core, z, j):
        return self.dst.at[pl.ds(pl.multiple_of((core * 4 + z) * 128 + j * 32, 32), 32)]

    def copy(self, z, j, kind, device):
        ref = self.at(self.c, z, j)
        return remote(ref, ref, self.sems, (kind, j), device)

    def put(self, j):
        self.copy(self.z, j, 0, self.up).start()
        self.copy(self.z, j, 1, self.down).start()
        self.copy(self.z, j, 2, self.other).start()

    def near(self, j):
        below, above = lax.rem(self.z + 3, 4), lax.rem(self.z + 1, 4)
        self.copy(below, j, 0, self.up).wait_recv()
        if j < 2:
            self.copy(below, j, 3, self.up).start()
        self.copy(below, j, 5, self.other).start()
        self.copy(above, j, 1, self.down).wait_recv()
        if j >= 2:
            self.copy(above, j, 4, self.down).start()
        self.copy(above, j, 6, self.other).start()

    def far(self, j):
        opposite = lax.rem(self.z + 2, 4)
        self.copy(opposite, j, 3 if j < 2 else 4, self.up).wait_recv()
        self.copy(opposite, j, 7, self.other).start()

    def shared(self, kind):
        for j in ORDER:
            self.copy(self.z, j, kind, self.other).wait_recv()

    def finish(self):
        for j in ORDER:
            for kind in (0, 1, 2, 3 if j < 2 else 4, 5, 6, 7):
                self.copy(self.z, j, kind, self.other).wait_send()


class LowGather:
    SEMS = [DMA((8,)), DMA((8,))]

    def __init__(self, dst, send, recv):
        self.dst, self.sems = dst, (send, recv)
        _, _, c, _, z = places()
        self.own = pl.ds(pl.multiple_of((c * 4 + z) * 128, 128), 128)

    def copies(self):
        ref = self.dst.at[:, self.own]
        return [remote(ref, ref, self.sems, (n,), group_peer(n)) for n in range(1, 8)]

    def start(self, value):
        self.dst[:, self.own] = value
        for copy in self.copies():
            copy.start()

    def wait(self):
        for copy in self.copies():
            copy.wait()


class LowSum:
    SEMS = [DMA((8,)), DMA((8,))]

    def __init__(self, src, got, send, recv):
        self.src, self.got, self.sems = src, got, (send, recv)
        _, _, self.c, _, self.z = places()

    def copies(self):
        out = []
        for n in range(1, 8):
            p = group_peer(n)
            cols = pl.ds(pl.multiple_of((p["c"] * 4 + p["z"]) * 128, 128), 128)
            out.append(remote(self.src.at[:, cols], self.got.at[n], self.sems, (n,), p))
        return out

    def start(self):
        for copy in self.copies():
            copy.start()

    def total(self):
        for copy in self.copies():
            copy.wait()
        own = pl.ds(pl.multiple_of((self.c * 4 + self.z) * 128, 128), 128)
        out = self.src[:, own].astype(F32)
        for n in range(1, 8):
            out = out + self.got[n].astype(F32)
        return out.astype(BF16)


class PlaneGather:
    SEMS = [DMA((1,)), DMA((22,)), DMA((16,))]

    def __init__(self, src, dst, by_rows, local_sem, send, recv):
        self.src, self.dst, self.by_rows, self.local_sem, self.sems = src, dst, by_rows, local_sem, (send, recv)
        self.xl, self.y, self.c, self.xh, _ = places()
        self.x = self.xh * 2 + self.xl
        self.home = at_home()

    def slot(self, xl, y, core):
        k = (xl * 4 + y) * 2 + core
        if self.by_rows:
            return k, block(self.dst, k)
        return k, self.dst.at[:, pl.ds(pl.multiple_of(k * 128, 128), 128)]

    def send(self, src, where, n, device):
        k, dst = where
        send, recv = self.sems
        return pltpu.make_async_remote_copy(
            src_ref=src, dst_ref=dst, send_sem=send.at[n], recv_sem=recv.at[k],
            device_id=device, device_id_type=MESH_ID)

    def arrived(self, where):
        self.send(where[1], where, 0, {"c": 1 - self.c}).wait_recv()

    def chip_x(self, d, core):
        x = lax.rem(self.x + d, 4)
        return {"xh": x // 2, "xl": lax.rem(x, 2), "c": core}

    def chip_y(self, d, core):
        return {"y": lax.rem(self.y + d, 4), "c": core}

    def first(self, act):
        own = self.slot(self.xl, self.y, self.c)

        @pl.when(self.c == 0)
        def _():
            for d in (1, 3, 2):
                act(self.send(self.src, own, d, self.chip_x(d, self.xh)))

        @pl.when(self.c == 1)
        def _():
            for d in (1, 3, 2):
                act(self.send(self.src, own, d, self.chip_y(d, self.xh)))

        @pl.when(self.home == 0)
        def _():
            act(self.send(self.src, own, 0, {"c": 1 - self.c}))

    def start(self):
        @pl.when(self.home == 1)
        def _():
            pltpu.make_async_copy(self.src, self.slot(self.xl, self.y, self.c)[1], self.local_sem.at[0]).start()

        self.first(lambda copy: copy.start())

    def columns(self):
        one = self.home * self.xl
        return one, 1 - one

    def rows_step(self, n, act):
        where = self.slot(self.columns()[n], self.y, 0)
        for d in (1, 3, 2):
            act(self.send(where[1], where, 4 + n * 3 + d - 1, self.chip_y(d, self.c)))

    def columns_step(self, n, act):
        where = self.slot(self.xl, lax.rem(self.y + n, 4), 1)

        @pl.when(self.home == 1)
        def _():
            for d in (1, 3, 2):
                act(self.send(where[1], where, 10 + n * 3 + d - 1, self.chip_x(d, self.c)))

    def step(self, n):
        if n == 0:
            @pl.when(self.home == 1)
            def _():
                pltpu.make_async_copy(self.src, self.slot(self.xl, self.y, self.c)[1], self.local_sem.at[0]).wait()
        if n < 2:
            where = self.slot(self.columns()[n], self.y, 0)
            if n == 0:
                @pl.when(self.home * (1 - self.c) == 0)
                def _():
                    self.arrived(where)
            else:
                self.arrived(where)
            self.rows_step(n, lambda copy: copy.start())
        else:
            where = self.slot(self.xl, lax.rem(self.y + n - 2, 4), 1)
            here = self.home * (1 - self.c) if n == 2 else self.home

            @pl.when(here == 1)
            def _():
                self.arrived(where)

            self.columns_step(n - 2, lambda copy: copy.start())

    def wait(self):
        for xl in (0, 1):
            for d in (1, 2, 3):
                self.arrived(self.slot(xl, lax.rem(self.y + d, 4), 0))
        one, two = self.columns()
        for y in range(4):
            self.arrived(self.slot(two, y, 1))

        @pl.when(self.home == 0)
        def _():
            for y in range(4):
                self.arrived(self.slot(one, y, 1))

    def finish(self):
        self.first(lambda copy: copy.wait_send())
        for n in (0, 1):
            self.rows_step(n, lambda copy: copy.wait_send())
        for n in range(4):
            self.columns_step(n, lambda copy: copy.wait_send())


class GroupSum:
    NAMES = ("far_up", "far_down", "up_high", "down_low", "up_low", "down_high")
    SCRATCH = [VMEM((1024, 2048), BF16), VMEM((4, 128, 2048), BF16), VMEM((3, 128, 2048), BF16),
               VMEM((2, 64, 2048), BF16), VMEM((2, 128, 2048), BF16), DMA((10,)), DMA((10,))]

    def __init__(self, parts, near, sent, half, full, send, recv):
        self.parts, self.near, self.sent, self.half, self.full, self.sems = parts, near, sent, half, full, (send, recv)
        _, _, self.c, _, self.z = places()
        self.up, self.down, self.other = group_peer(1), group_peer(3), group_peer(4)
        self.order = [lax.rem(self.z + d, 4) for d in (2, 1, 3, 0)]

    def part(self, core, i):
        return block(self.parts, core * 4 + self.order[i])

    def given(self, i):
        return remote(self.part(1 - self.c, i), self.near.at[i], self.sems, (i,), self.other)

    def give(self, i):
        self.given(i).start()

    def pair(self, i, rows=slice(None)):
        return self.part(self.c, i)[rows].astype(F32) + self.near[i, rows].astype(F32)

    def piece(self, name):
        low, high = pl.ds(0, 64), pl.ds(64, 64)
        n = self.NAMES.index(name)
        src = (self.sent.at[0, low], self.sent.at[0, high], self.sent.at[1, high], self.sent.at[2, low],
               self.sent.at[1, low], self.sent.at[2, high])[n]
        dst = (self.half.at[0], self.half.at[1], self.full.at[0, high], self.full.at[1, low],
               self.full.at[0, low], self.full.at[1, high])[n]
        return remote(src, dst, self.sems, (4 + n,), (self.up, self.down)[n % 2])

    def far(self):
        self.given(0).wait_recv()
        self.sent[0] = self.pair(0).astype(BF16)
        self.piece("far_up").start()
        self.piece("far_down").start()

    def near_up(self):
        self.given(1).wait_recv()
        self.sent[1, pl.ds(64, 64)] = self.pair(1, pl.ds(64, 64)).astype(BF16)
        self.piece("up_high").start()

    def near_down(self):
        self.given(2).wait_recv()
        self.sent[2, pl.ds(0, 64)] = self.pair(2, pl.ds(0, 64)).astype(BF16)
        self.piece("down_low").start()

    def pass_on(self):
        low, high = pl.ds(0, 64), pl.ds(64, 64)
        self.piece("far_up").wait_recv()
        self.sent[1, low] = (self.pair(1, low) + self.half[0].astype(F32)).astype(BF16)
        self.piece("up_low").start()
        self.piece("far_down").wait_recv()
        self.sent[2, high] = (self.pair(2, high) + self.half[1].astype(F32)).astype(BF16)
        self.piece("down_high").start()

    def arrive(self):
        self.given(3).wait_recv()
        for name in ("up_high", "down_low", "up_low", "down_high"):
            self.piece(name).wait_recv()

    def total(self, rows=slice(None)):
        return self.pair(3, rows) + self.full[0, rows].astype(F32) + self.full[1, rows].astype(F32)

    def finish(self):
        for name in self.NAMES:
            self.piece(name).wait_send()
        for i in range(4):
            self.given(i).wait_send()


def params(cid, mib):
    return pltpu.CompilerParams(collective_id=cid, has_side_effects=True, vmem_limit_bytes=mib << 20)


def plain(mib):
    return pltpu.CompilerParams(vmem_limit_bytes=mib << 20)


def shape(*dims, dtype=BF16):
    return jax.ShapeDtypeStruct(dims, dtype)


def specs(*spaces):
    return [pl.BlockSpec(memory_space=s) for s in spaces]


def layer_norm(rows_in, gain, shift):
    row_mean = jnp.mean(rows_in, axis=-1, keepdims=True)
    centered = rows_in - row_mean
    variance = jnp.mean(centered * centered, axis=-1, keepdims=True)
    return centered * lax.rsqrt(variance + EPSILON) * gain + shift


def norm_back(rows_in, gain, grad):
    row_mean = jnp.mean(rows_in, axis=-1, keepdims=True)
    centered = rows_in - row_mean
    inverse = lax.rsqrt(jnp.mean(centered * centered, axis=-1, keepdims=True) + EPSILON)
    n = centered * inverse
    e = gain * grad
    return (e - jnp.mean(e, axis=-1, keepdims=True) - n * jnp.mean(e * n, axis=-1, keepdims=True)) * inverse


def dot(a, b, dims=((1,), (0,))):
    return lax.dot_general(a, b, (dims, ((), ())), preferred_element_type=F32)


def dot_t(a, b):
    return dot(a, b, ((1,), (1,)))


def dot_o(a, b):
    return dot(a, b, ((0,), (0,)))


def tiles(count, size, body):
    def run(i, carry):
        body(pl.ds(pl.multiple_of(i * size, size), size))
        return carry

    lax.fori_loop(0, count, run, 0)


def split_refs(refs, *counts):
    refs, out = list(refs), []
    for n in counts:
        out.append(refs[:n])
        refs = refs[n:]
    return (*out, refs)


def pick(ref, name):
    first, n = PICKS[name]
    return ref[:, pl.ds(first, n)]


def row_pair(z):
    return (pl.ds(pl.multiple_of(z * 128, 128), 128), pl.ds(pl.multiple_of(512 + z * 128, 128), 128))


def take_pair(ref, z, cols=slice(None)):
    a, b = row_pair(z)
    return jnp.concatenate([ref[a, cols], ref[b, cols]], axis=0)


def put_pair(ref, z, value, cols=slice(None)):
    a, b = row_pair(z)
    ref[a, cols] = value[:128]
    ref[b, cols] = value[128:]


class Swap:
    def __init__(self, pairs, local, send, recv):
        self.pairs, self.local, self.sems, self.home = pairs, local, (send, recv), at_home()

    def near_copy(self, n):
        src, _, dst = self.pairs[n]
        return pltpu.make_async_copy(src, dst, self.local.at[n])

    def far_copy(self, n):
        src, dst, _ = self.pairs[n]
        return remote(src, dst, self.sems, (n,), diagonal())

    def start(self, n):
        @pl.when(self.home == 1)
        def _():
            self.near_copy(n).start()

        @pl.when(self.home == 0)
        def _():
            self.far_copy(n).start()

    def wait(self, n):
        @pl.when(self.home == 1)
        def _():
            self.near_copy(n).wait()

        @pl.when(self.home == 0)
        def _():
            self.far_copy(n).wait_recv()

    def finish(self):
        @pl.when(self.home == 0)
        def _():
            for n in range(len(self.pairs)):
                self.far_copy(n).wait_send()

    @staticmethod
    def sems(n):
        return [DMA((n,)), DMA((n,)), DMA((n,))]


ADAPTERS = ("joined_in", "joined_out", "dense_in", "dense_out", "up_in", "up_out", "down_in", "down_out")


def joined_kernel(*refs):
    (ids, tokens, gain, shift), adapters, (bj, bu, wj), outs, scratch = split_refs(refs, 4, 8, 3, 9)
    xs, x_all, pk, bias, qa, ka, va, wj_all, low = outs
    (mine, xbuf, wbuf, out_sem), sw_sems, g_sems, low_sems, p_sems = split_refs(scratch, 4, 3, 2, 2)
    _, _, c, _, z = places()
    own = c * 4 + z
    meet(plane_peers() + group_peers())
    sub = lambda ref, j: ref.at[pl.ds(j * 32, 32)]
    cut = 2944
    pairs = [(sub(tokens, j), sub(xs, j)) for j in range(4)]
    pairs += [(mine.at[:, :cut], pk.at[:, :cut]), (mine.at[:, cut:], pk.at[:, cut:]),
              (bj, bias.at[:, :768]), (bu, bias.at[:, 768:])]
    sw = Swap([(a, b, b) for a, b in pairs], *sw_sems)
    for j in ORDER:
        sw.start(j)
    plane = PlaneGather(wj, wbuf, True, *p_sems)
    plane.start()
    set_id = ids[0]
    for name, ref in zip(ADAPTERS, adapters):
        first, n = PICKS[name]
        mine[:, first:first + n] = ref[set_id]
    first, n = PICKS["hot"]
    mine[:, first:first + n] = jnp.where(lax.broadcasted_iota(jnp.int32, (16, 128), 0) == set_id, 1.0, 0.0).astype(BF16)
    for n in range(4, 8):
        sw.start(n)
    g = GroupGather(xbuf, *g_sems)
    lows = LowGather(low, *low_sems)
    for j in ORDER:
        sw.wait(j)
        x1 = layer_norm(xs[j * 32:(j + 1) * 32].astype(F32), gain[...], shift[...])
        xbuf[pl.ds(pl.multiple_of(own * 128 + j * 32, 32), 32)] = x1.astype(BF16)
        g.put(j)
    sw.wait(4)
    lows.start(dot_t(pick(pk, "joined_in"), block(xbuf, own)[...]).astype(BF16))
    g.near(0)
    plane.step(0)
    plane.step(1)
    g.near(3)
    for n in (2, 3):
        plane.step(n)
    g.near(1)
    for n in (4, 5):
        plane.step(n)
    g.near(2)
    for j in ORDER:
        g.far(j)
    for n in range(5, 8):
        sw.wait(n)
    for kind in (2, 5, 6, 7):
        g.shared(kind)
    x_out = pltpu.make_async_copy(xbuf, x_all, out_sem.at[0])
    x_out.start()
    plane.wait()
    w_out = pltpu.make_async_copy(wbuf, wj_all, out_sem.at[1])
    w_out.start()
    lows.wait()
    lane = lax.broadcasted_iota(jnp.int32, (256, 128), 1)
    row = lax.broadcasted_iota(jnp.int32, (256, 128), 0)

    def project(i, carry):
        rows = pl.ds(pl.multiple_of(i * 256, 256), 256)
        acc = dot(xbuf[rows], wbuf[...]) + dot_o(low[:, rows], pick(pk, "joined_out")) + bias[:, :768]
        b = acc.astype(BF16).astype(F32)
        position = (i * 256 + row).astype(F32) * 0.125
        ones = jnp.where(lane < 67, 1.0, 0.0)
        for h in range(4):
            slope = jnp.exp2((own * 4 + h + 1).astype(F32) * (-8.0 / HEADS) + jnp.zeros((1, 128), F32))
            line = position * slope
            high = line.astype(BF16).astype(F32)
            middle = (line - high).astype(BF16).astype(F32)
            lowest = line - high - middle
            tail = jnp.where(lane == 64, high, jnp.where(lane == 65, middle, jnp.where(lane == 66, lowest, jnp.where(
                lane < 70, 1.0, 0.0))))
            at = h * 192
            qa[h, rows] = jnp.where(lane < 64, b[:, at:at + 128] * 0.125, ones).astype(BF16)
            ka[h, rows] = jnp.where(lane < 64, b[:, at + 64:at + 192], tail).astype(BF16)
            v = jnp.concatenate([b[:, at + 128:at + 192], b[:, at:at + 64]], axis=1)
            va[h, rows] = jnp.where(lane < 64, v, ones).astype(BF16)
        return carry

    lax.fori_loop(0, 4, project, 0)
    x_out.wait()
    w_out.wait()
    g.finish()
    plane.finish()
    sw.finish()


def joined_call(ids, tokens, gain, shift, adapters, bj, bu, wj):
    outs = [shape(128, 2048), shape(1024, 2048), shape(16, PICKED), shape(1, 1792, dtype=F32)] + [
        shape(4, 1024, 128)] * 3 + [shape(2048, 768), shape(16, 1024)]
    return pl.pallas_call(
        joined_kernel, out_shape=outs,
        in_specs=specs(pltpu.SMEM, *[VMEM] * 13, ANY),
        out_specs=specs(VMEM, ANY, VMEM, VMEM, VMEM, VMEM, VMEM, ANY, VMEM),
        scratch_shapes=[VMEM((16, PICKED), BF16), VMEM((1024, 2048), BF16), VMEM((2048, 768), BF16), DMA((2,)),
                        *Swap.sems(8), *GroupGather.SEMS, *LowGather.SEMS, *PlaneGather.SEMS],
        compiler_params=params(1, 40), name="joined")(ids, tokens, gain, shift, *adapters, bj, bu, wj)


def attend_kernel(*refs):
    (qa, ka, va, pk, go, wd, wn), outs, scratch = split_refs(refs, 7, 7)
    qb, ctx, go_all, gos, wd_all, wn_all, low = outs
    (gbuf, c4, out_sem), sw_sems, g_sems, low_sems, d_sems, n_sems = split_refs(scratch, 3, 3, 2, 2, 3)
    _, _, c, _, z = places()
    own = c * 4 + z
    meet(plane_peers() + group_peers())
    there = (1 - c) * 4 + z
    piece = lambda who, j: gbuf.at[pl.ds(pl.multiple_of(who * 128 + j * 32, 32), 32)]
    sw = Swap([(go.at[pl.ds(j * 32, 32)], piece(there, j), piece(own, j)) for j in range(4)], *sw_sems)
    for j in ORDER:
        sw.start(j)
    dense = PlaneGather(wd, wd_all, False, *d_sems)
    down = PlaneGather(wn, wn_all, False, *n_sems)
    dense.start()
    down.start()
    g = GroupGather(gbuf, *g_sems)
    lows = LowGather(low, *low_sems)

    def begin():
        for j in ORDER:
            sw.wait(j)
            g.put(j)

    def low_start():
        gos[...] = block(gbuf, own)[...]
        lows.start(dot_t(pick(pk, "down_out"), block(gbuf, own)[...]).astype(BF16))

    hooks = [lambda: dense.step(0), begin, lambda: dense.step(1), low_start, lambda: down.step(0), lambda: down.step(1),
             lambda: dense.step(2), lambda: (dense.step(3), dense.step(4), dense.step(5)), lambda: g.near(0),
             lambda: down.step(2), lambda: g.near(3), lambda: down.step(3), lambda: g.near(1),
             lambda: down.step(4), lambda: g.near(2), lambda: down.step(5)]
    diagonal_mask = lax.broadcasted_iota(jnp.int32, (256, 256), 0) <= lax.broadcasted_iota(jnp.int32, (256, 256), 1)
    line = lax.broadcasted_iota(jnp.int32, (128, 256), 0)
    lane = lax.broadcasted_iota(jnp.int32, (256, 128), 1)

    def head(h, carry):
        for i in range(4):
            rows = pl.ds(i * 256, 256)
            q = qa[h, rows]
            last = jnp.where(diagonal_mask, dot_t(ka[h, rows], q), MASKED)
            top = jnp.max(last, axis=0, keepdims=True)
            if i:
                before = dot_t(ka[h, pl.ds(0, i * 256)], q)
                top = jnp.maximum(top, jnp.max(before, axis=0, keepdims=True))
            out = dot_o(va[h, rows], jnp.exp(last - top).astype(BF16))
            if i:
                out = out + dot_o(va[h, pl.ds(0, i * 256)], jnp.exp(before - top).astype(BF16))
            total = out[64:65]
            log = -(top + jnp.log(total))
            high = log.astype(BF16).astype(F32)
            middle = (log - high).astype(BF16).astype(F32)
            out = jnp.where(line == 67, high, jnp.where(line == 68, middle, jnp.where(
                line == 69, log - high - middle, out / total)))
            turned = out.T
            c4[h, rows] = turned.astype(BF16)
            qb[h, rows] = jnp.where(lane < 67, q.astype(F32), jnp.where(lane < 70, turned, 0.0)).astype(BF16)
            for k in range(4):
                @pl.when(h == k)
                def _(k=k, i=i):
                    hooks[k * 4 + i]()
        return carry

    lax.fori_loop(0, 4, head, 0)
    for h in (0, 2):
        ctx[:, h * 64:h * 64 + 128] = jnp.concatenate([c4[h, :, :64], c4[h + 1, :, :64]], axis=1)
    for j in ORDER:
        g.far(j)
    for kind in (2, 5, 6, 7):
        g.shared(kind)
    g_out = pltpu.make_async_copy(gbuf, go_all, out_sem.at[0])
    g_out.start()
    lows.wait()
    dense.wait()
    down.wait()
    g_out.wait()
    g.finish()
    dense.finish()
    down.finish()
    sw.finish()


def attend_call(qa, ka, va, pk, go, wd, wn):
    outs = [shape(4, 1024, 128), shape(1024, 256), shape(1024, 2048), shape(128, 2048), shape(256, 2048),
            shape(1024, 2048), shape(16, 1024)]
    return pl.pallas_call(
        attend_kernel, out_shape=outs, in_specs=specs(*[VMEM] * 4, ANY, ANY, ANY),
        out_specs=specs(VMEM, VMEM, ANY, VMEM, ANY, ANY, VMEM),
        scratch_shapes=[VMEM((1024, 2048), BF16), VMEM((4, 1024, 128), BF16), DMA((1,)), *Swap.sems(4),
                        *GroupGather.SEMS, *LowGather.SEMS, *PlaneGather.SEMS, *PlaneGather.SEMS],
        compiler_params=params(2, 40), name="attend")(qa, ka, va, pk, go, wd, wn)


ROOT_HALF = 0.7071067811865476
ROOT_TAU = 0.3989422804014327


def middle_kernel(*refs):
    (ctx, xs, pk, bias, lowg, gain, shift, dense_bias, wd, go, wn, wu), outs, scratch = split_refs(refs, 12, 7)
    mid, x_all, act, dpre, wu_all, low_u, low_d = outs
    (xbuf, ubuf, gbuf, nbuf, dbuf, dact, src, got, part_sem), s_refs, sems = split_refs(scratch, 9, 7)
    g_sems, l_sems, u_sems, t_sems, p_sems = split_refs(sems, 2, 2, 2, 2)
    _, _, c, _, z = places()
    own = c * 4 + z
    meet(plane_peers() + group_peers())
    loads = [pltpu.make_async_copy(a, b, part_sem.at[n]) for n, (a, b) in enumerate(((wd, dbuf), (go, gbuf), (wn, nbuf)))]
    for load in loads:
        load.start()
    plane = PlaneGather(wu, ubuf, True, *p_sems)
    plane.start()
    src[...] = dot_t(pick(pk, "dense_in"), ctx[...]).astype(BF16)
    total = LowSum(src, got, *l_sems)
    total.start()
    s = GroupSum(*s_refs)
    loads[0].wait()

    def part(i):
        put_pair(s.parts, s.order[i], dot(take_pair(ctx, s.order[i]), dbuf[...]).astype(BF16))
        s.give(i)

    part(0)
    part(1)
    s.far()
    plane.step(0)
    plane.step(1)
    part(2)
    s.near_up()
    part(3)
    s.near_down()
    plane.step(2)
    s.pass_on()
    plane.step(3)
    low_total = total.total()
    mid[...] = dot_o(low_total, pick(pk, "dense_out")) + dense_bias[...] + xs[...].astype(F32)
    loads[1].wait()
    loads[2].wait()

    def grad_act(rows):
        dact[rows] = dot_t(gbuf[rows], nbuf[...]) + dot_o(lowg[:, rows], pick(pk, "down_in"))

    tiles(2, 256, grad_act)
    plane.step(4)
    plane.step(5)
    tiles(2, 256, lambda rows: grad_act(pl.ds(pl.multiple_of(rows.start + 512, 256), 256)))
    s.arrive()
    g = GroupGather(xbuf, *g_sems)
    for j in ORDER:
        rows = slice(j * 32, (j + 1) * 32)
        mid[rows] = mid[rows] + s.total(rows)
        xbuf[pl.ds(pl.multiple_of(own * 128 + j * 32, 32), 32)] = layer_norm(mid[rows], gain[...], shift[...]).astype(BF16)
        g.put(j)
    lows = LowGather(low_u, *u_sems)
    lows.start(dot_t(pick(pk, "up_in"), block(xbuf, own)[...]).astype(BF16))
    sums = LowGather(low_d, *t_sems)
    sums.start(low_total)
    plane.wait()
    w_out = pltpu.make_async_copy(ubuf, wu_all, part_sem.at[0])
    w_out.start()
    lows.wait()

    def forward(at):
        x = take_pair(xbuf, at)
        lu = jnp.concatenate([low_u[:, rows] for rows in row_pair(at)], axis=1)

        def run(n, carry):
            cols = pl.ds(pl.multiple_of(n * 256, 256), 256)
            up = pk[:, pl.ds(pl.multiple_of(PICKS["up_out"][0] + n * 256, 128), 256)]
            b = bias[:, pl.ds(pl.multiple_of(768 + n * 256, 256), 256)]
            pre = dot(x, ubuf[:, cols]) + dot_o(lu, up) + b
            cdf = 0.5 * (1.0 + lax.erf(pre * ROOT_HALF))
            put_pair(act, at, (pre * cdf).astype(BF16), cols)
            slope = cdf + pre * (jnp.exp(-0.5 * pre * pre) * ROOT_TAU)
            put_pair(dpre, at, (take_pair(dact, at, cols) * slope).astype(BF16), cols)
            return carry

        lax.fori_loop(0, 4, run, 0)

    g.shared(2)
    forward(z)
    for j in ORDER:
        g.near(j)
    g.shared(5)
    forward(lax.rem(z + 3, 4))
    g.shared(6)
    forward(lax.rem(z + 1, 4))
    for j in ORDER:
        g.far(j)
    g.shared(7)
    x_out = pltpu.make_async_copy(xbuf, x_all, part_sem.at[1])
    x_out.start()
    forward(lax.rem(z + 2, 4))
    sums.wait()
    w_out.wait()
    x_out.wait()
    s.finish()
    g.finish()
    plane.finish()


def middle_call(*args):
    outs = [shape(128, 2048, dtype=F32), shape(1024, 2048), shape(1024, 1024), shape(1024, 1024), shape(2048, 1024),
            shape(16, 1024), shape(16, 1024)]
    return pl.pallas_call(
        middle_kernel, out_shape=outs, in_specs=specs(*[VMEM] * 8, *[ANY] * 4),
        out_specs=specs(VMEM, ANY, VMEM, VMEM, ANY, VMEM, VMEM),
        scratch_shapes=[VMEM((1024, 2048), BF16), VMEM((2048, 1024), BF16), VMEM((1024, 2048), BF16),
                        VMEM((1024, 2048), BF16), VMEM((256, 2048), BF16), VMEM((1024, 1024), F32),
                        VMEM((16, 1024), BF16), VMEM((8, 16, 128), BF16), DMA((3,)), *GroupSum.SCRATCH,
                        *GroupGather.SEMS, *LowSum.SEMS, *LowGather.SEMS, *LowGather.SEMS, *PlaneGather.SEMS],
        compiler_params=params(3, 56), name="middle")(*args)


def back_kernel(*refs):
    (dpre, act, mid, gos, pk, gain, wu, wn, wd), outs, scratch = split_refs(refs, 9, 7)
    dmid, ga_all, dctx, mlp, low_n, low_d, low_u = outs
    (xbuf, ubuf, nbuf, dbuf, src, got, part_sem), s_refs, sems = split_refs(scratch, 7, 7)
    g_sems, l_sems, d_sems, t_sems, _ = split_refs(sems, 2, 2, 2, 2)
    _, _, c, _, z = places()
    own = c * 4 + z
    meet(group_peers())
    loads = [pltpu.make_async_copy(a, b, part_sem.at[n]) for n, (a, b) in enumerate(((wu, ubuf), (wn, nbuf), (wd, dbuf)))]
    for load in loads:
        load.start()
    src[...] = dot_t(pick(pk, "up_out"), dpre[...]).astype(BF16)
    total = LowSum(src, got, *l_sems)
    total.start()
    s = GroupSum(*s_refs)
    loads[0].wait()

    def part(i):
        x = take_pair(dpre, s.order[i])

        def run(n, carry):
            cols = pl.ds(pl.multiple_of(n * 512, 512), 512)
            put_pair(s.parts, s.order[i], dot_t(x, ubuf[cols]).astype(BF16), cols)
            return carry

        lax.fori_loop(0, 4, run, 0)
        s.give(i)

    part(0)
    part(1)
    s.far()
    part(2)
    s.near_up()
    part(3)
    s.near_down()
    s.pass_on()
    low_total = total.total()
    dmid[...] = dot_o(low_total, pick(pk, "up_in"))
    loads[1].wait()

    def forward(rows):
        mlp[rows] = dot(act[rows], nbuf[...]).astype(BF16)

    tiles(4, 256, forward)
    low_n[...] = dot_t(pick(pk, "down_in"), act[...]).astype(BF16)
    s.arrive()
    g = GroupGather(xbuf, *g_sems)
    for j in ORDER:
        rows = slice(j * 32, (j + 1) * 32)
        dmid[rows] = gos[rows].astype(F32) + norm_back(mid[rows], gain[...], dmid[rows] + s.total(rows))
        xbuf[pl.ds(pl.multiple_of(own * 128 + j * 32, 32), 32)] = dmid[rows].astype(BF16)
        g.put(j)
    lows = LowGather(low_d, *d_sems)
    lows.start(dot_t(pick(pk, "dense_out"), block(xbuf, own)[...]).astype(BF16))
    sums = LowGather(low_u, *t_sems)
    sums.start(low_total)
    loads[2].wait()
    lows.wait()

    def context(at):
        ld = jnp.concatenate([low_d[:, rows] for rows in row_pair(at)], axis=1)
        value = dot_t(take_pair(xbuf, at), dbuf[...]) + dot_o(ld, pick(pk, "dense_in"))
        put_pair(dctx, at, value.astype(BF16))

    g.shared(2)
    context(z)
    for j in ORDER:
        g.near(j)
    g.shared(5)
    context(lax.rem(z + 3, 4))
    g.shared(6)
    context(lax.rem(z + 1, 4))
    for j in ORDER:
        g.far(j)
    g.shared(7)
    x_out = pltpu.make_async_copy(xbuf, ga_all, part_sem.at[1])
    x_out.start()
    context(lax.rem(z + 2, 4))
    sums.wait()
    x_out.wait()
    s.finish()
    g.finish()


def back_call(*args):
    outs = [shape(128, 2048, dtype=F32), shape(1024, 2048), shape(1024, 256), shape(1024, 2048), shape(16, 1024),
            shape(16, 1024), shape(16, 1024)]
    return pl.pallas_call(
        back_kernel, out_shape=outs, in_specs=specs(*[VMEM] * 6, *[ANY] * 3),
        out_specs=specs(VMEM, ANY, VMEM, VMEM, VMEM, VMEM, VMEM),
        scratch_shapes=[VMEM((1024, 2048), BF16), VMEM((2048, 1024), BF16), VMEM((1024, 2048), BF16),
                        VMEM((256, 2048), BF16), VMEM((16, 1024), BF16), VMEM((8, 16, 128), BF16), DMA((3,)),
                        *GroupSum.SCRATCH, *GroupGather.SEMS, *LowSum.SEMS, *LowGather.SEMS, *LowGather.SEMS],
        compiler_params=params(4, 56), name="back")(*args)


def attend_back_kernel(*refs):
    (qb, ka, va, ctx, dctx, mlp, low_n, mid, down_bias, pk), outs, scratch = split_refs(refs, 10, 3)
    dfused, layer, low_s = outs
    (g4, dq4, dk4, dv4, dk, dv, got), s_refs, (l_send, l_recv, t_send, t_recv) = split_refs(scratch, 7, 6)
    meet(group_peers())
    s = GroupSum(mlp, *s_refs)
    for i in range(4):
        s.give(i)
    total = LowSum(low_n, got, l_send, l_recv)
    total.start()
    lane = lax.broadcasted_iota(jnp.int32, (1024, 128), 1)
    for h in range(4):
        first = h // 2 * 128
        g = dctx[:, first:first + 128].astype(F32)
        f = ctx[:, first:first + 128].astype(F32)
        here = (lane // 64) == h % 2
        d = -jnp.sum(jnp.where(here, g * f, 0.0), axis=-1, keepdims=True)
        if h % 2:
            g = jnp.concatenate([g[:, 64:], g[:, :64]], axis=1)
        high = d.astype(BF16).astype(F32)
        middle = (d - high).astype(BF16).astype(F32)
        g4[h] = jnp.where(lane < 64, g, jnp.where(lane == 64, high, jnp.where(lane == 65, middle, jnp.where(
            lane == 66, d - high - middle, 0.0)))).astype(BF16)
    sums = LowGather(low_s, t_send, t_recv)

    def low_step():
        value = total.total()
        sums.start(value)
        layer[...] = (mid[...] + down_bias[...] + dot_o(value, pick(pk, "down_out"))).astype(BF16)

    hooks = {0: s.far, 1: s.near_up, 2: s.near_down, 5: low_step, 6: s.pass_on}
    diagonal_mask = lax.broadcasted_iota(jnp.int32, (256, 256), 0) <= lax.broadcasted_iota(jnp.int32, (256, 256), 1)

    def head(h, carry):
        dk[...] = jnp.zeros_like(dk)
        dv[...] = jnp.zeros_like(dv)
        for i in range(4):
            rows = pl.ds(i * 256, 256)
            q, g = qb[h, rows], g4[h, rows]

            def span(keys, mask):
                k = ka[h, keys]
                score = dot_t(k, q)
                if mask:
                    score = jnp.where(diagonal_mask, score, MASKED)
                p = jnp.exp(score)
                ds = (p * dot_t(va[h, keys], g)).astype(BF16)
                dk[keys] += dot(ds, q)
                dv[keys] += dot(p.astype(BF16), g)
                return dot_o(k, ds)

            dq = span(rows, True)
            if i:
                dq = dq + span(pl.ds(0, i * 256), False)
            dq4[h, rows] = (dq * 0.125).T.astype(BF16)
            for n, hook in hooks.items():
                if n % 4 == i:
                    @pl.when(h == n // 4)
                    def _(hook=hook):
                        hook()
        dk4[h] = dk[...].astype(BF16)
        dv4[h] = dv[...].astype(BF16)
        return carry

    lax.fori_loop(0, 4, head, 0)
    for h in (0, 2):
        dfused[:, h * 192:h * 192 + 384] = jnp.concatenate(
            [a[k, :, :64] for k in (h, h + 1) for a in (dq4, dk4, dv4)], axis=1)
    s.arrive()
    value = total_again(low_s, pk)
    layer[...] = (mid[...] + down_bias[...] + value + s.total()).astype(BF16)
    sums.wait()
    s.finish()


def total_again(low_s, pk):
    _, _, c, _, z = places()
    own = pl.ds(pl.multiple_of((c * 4 + z) * 128, 128), 128)
    return dot_o(low_s[:, own], pick(pk, "down_out"))


def attend_back_call(*args):
    outs = [shape(1024, 768), shape(128, 2048), shape(16, 1024)]
    return pl.pallas_call(
        attend_back_kernel, out_shape=outs, in_specs=specs(*[VMEM] * 10), out_specs=specs(*[VMEM] * 3),
        scratch_shapes=[VMEM((4, 1024, 128), BF16)] * 4 + [VMEM((1024, 128), F32)] * 2 + [
            VMEM((8, 16, 128), BF16)] + GroupSum.SCRATCH[1:] + LowSum.SEMS + LowGather.SEMS,
        compiler_params=params(5, 48), name="attend_back")(*args)


def last_kernel(*refs):
    (dfused, dmid, xs, layer, gain, pk, wj), outs, scratch = split_refs(refs, 7, 3)
    grad, out, low_s = outs
    (wbuf, mine, back, src, got, part_sem), s_refs, sems = split_refs(scratch, 6, 7)
    sw_sems, l_sems, t_sems, _ = split_refs(sems, 3, 2, 2)
    meet(group_peers() + [diagonal()])
    load = pltpu.make_async_copy(wj, wbuf, part_sem.at[0])
    load.start()
    sub = lambda ref, j: ref.at[pl.ds(j * 32, 32)]
    pairs = [(sub(mine, j), sub(back, j), sub(back, j)) for j in range(4)] + [(layer, out, out)]
    sw = Swap(pairs, *sw_sems)
    sw.start(4)
    src[...] = dot_t(pick(pk, "joined_out"), dfused[...]).astype(BF16)
    total = LowSum(src, got, *l_sems)
    total.start()
    s = GroupSum(*s_refs)
    load.wait()

    def part(i):
        x = take_pair(dfused, s.order[i])

        def run(n, carry):
            cols = pl.ds(pl.multiple_of(n * 512, 512), 512)
            put_pair(s.parts, s.order[i], dot_t(x, wbuf[cols]).astype(BF16), cols)
            return carry

        lax.fori_loop(0, 4, run, 0)
        s.give(i)

    part(0)
    part(1)
    s.far()
    part(2)
    s.near_up()
    part(3)
    s.near_down()
    s.pass_on()
    low_total = total.total()
    sums = LowGather(low_s, *t_sems)
    sums.start(low_total)
    grad[...] = dot_o(low_total, pick(pk, "joined_in"))
    s.arrive()
    for j in ORDER:
        rows = slice(j * 32, (j + 1) * 32)
        value = dmid[rows] + norm_back(xs[rows].astype(F32), gain[...], grad[rows] + s.total(rows))
        mine[rows] = value.astype(BF16)
        sw.start(j)
    for n in range(5):
        sw.wait(n)
    grad[...] = back[...].astype(F32)
    sums.wait()
    s.finish()
    sw.finish()


def last_call(*args):
    outs = [shape(128, 2048, dtype=F32), shape(128, 2048), shape(16, 1024)]
    return pl.pallas_call(
        last_kernel, out_shape=outs, in_specs=specs(*[VMEM] * 6, ANY), out_specs=specs(*[VMEM] * 3),
        scratch_shapes=[VMEM((2048, 768), BF16), VMEM((128, 2048), BF16), VMEM((128, 2048), BF16),
                        VMEM((16, 1024), BF16), VMEM((8, 16, 128), BF16), DMA((1,)), *GroupSum.SCRATCH,
                        *Swap.sems(5), *LowSum.SEMS, *LowGather.SEMS],
        compiler_params=params(6, 40), name="last")(*args)


SWAP = ((0, 0), (1, 2), (2, 1), (3, 3))


def finish(mine, hot):
    turn = lambda a: jnp.swapaxes(a, 1, 2)
    every = lax.all_gather(mine, PLANE, axis=0, tiled=False)
    onehot = lax.all_gather(hot[:, 0], PLANE, axis=1, tiled=False)
    sums = lax.dot_general(onehot, every, (((1,), (0,)), ((), ())), preferred_element_type=F32)
    split = lax.ppermute(sums[:, :, :3072].astype(BF16), ("c", "xh"), SWAP).astype(F32)
    whole = lax.all_gather(sums[:, :, 3072:].astype(BF16), ("c", "z"), axis=0, tiled=False).astype(F32)
    whole = whole.reshape(8, 8, 16, 4, 256)
    per = [whole[:, :, :, i].transpose(1, 2, 0, 3).reshape(8, 16, 2048) for i in range(4)]
    return (turn(per[0]), split[:, :, :768], turn(split[:, :, 768:1024]), per[1],
            turn(per[2]), split[:, :, 1024:2048], turn(split[:, :, 2048:3072]), per[3])


def local(tokens, grad_out, adapter_ids, first_gain, first_shift, joined_weight, joined_bias, dense_weight,
          dense_bias, second_gain, second_shift, up_weight, up_bias, down_weight, down_bias, joined_adapt_in,
          joined_adapt_out, dense_adapt_in, dense_adapt_out, up_adapt_in, up_adapt_out, down_adapt_in,
          down_adapt_out):
    c, xh, z = lax.axis_index("c"), lax.axis_index("xh"), lax.axis_index("z")
    group = c * 4 + z
    turn = lambda a: jnp.swapaxes(a, 1, 2)
    line = lambda a: a.reshape(1, -1)
    adapters = [turn(joined_adapt_in), joined_adapt_out, turn(dense_adapt_in), dense_adapt_out, turn(up_adapt_in),
                up_adapt_out, turn(down_adapt_in), down_adapt_out]
    xs, x1_all, pk, bias, qa, ka, va, w_joined, low_q = joined_call(
        adapter_ids, tokens, line(first_gain), line(first_shift), adapters, line(joined_bias), line(up_bias),
        joined_weight)
    qb, context, go_all, gos, w_dense, w_down, low_g = attend_call(qa, ka, va, pk, grad_out, dense_weight, down_weight)
    mid, x2_all, act, grad_pre, w_up, low_u, sum_d = middle_call(
        context, xs, pk, bias, low_g, line(second_gain), line(second_shift), line(dense_bias), w_dense, go_all, w_down,
        up_weight)
    grad_mid, ga_all, grad_context, mlp, low_n, low_d, sum_u = back_call(
        grad_pre, act, mid, gos, pk, line(second_gain), w_up, w_down, w_dense)
    grad_joined, layer, sum_n = attend_back_call(qb, ka, va, context, grad_context, mlp, low_n, mid, line(down_bias), pk)
    grad_tokens, layer_out, sum_q = last_call(grad_joined, grad_mid, xs, layer, line(first_gain), pk, w_joined)

    cols = [lax.dynamic_slice_in_dim(a, group * 256, 256, 1) for a in (x1_all, ga_all, x2_all, go_all)]
    halves = [dot(low, col) for low, col in zip((sum_q, sum_d, sum_u, sum_n), cols)]
    wide = [dot(low_q, grad_joined), dot(low_d, context), dot(low_u, grad_pre), dot(low_g, act)]
    mine = jnp.concatenate(wide + halves, axis=1).astype(BF16)
    first, n = PICKS["hot"]
    return (layer_out, grad_tokens, *finish(mine, pk[:8, first:first + n]))


def solution(mesh):
    fine = Mesh(mesh.devices.reshape(2, 4, 2, 2, 4), AXES)
    rows, cols = P(FSDP, TP), P(TP, FSDP)
    tok = P((*FSDP, *TP), None)
    last, middle, one = P(None, None, TP), P(None, TP, None), P(TP)
    return jax.shard_map(
        local, mesh=fine,
        in_specs=(tok, tok, P(FSDP), P(), P(), rows, one, cols, P(), P(), P(), rows, one, cols, P(), P(), last,
                  middle, P(), P(), last, middle, P()),
        out_specs=(tok, tok, P(), last, middle, P(), P(), last, middle, P()), check_vma=False)
```

time: 596 us -> 463 us (0.78)
  matrix products: 127 us -> 16.6 us
  Pallas kernels: 248 us -> 280 us
  waiting for transfers between devices: 79.1 us -> 57.9 us
  starting transfers between devices: 32.1 us -> 13.3 us
  other arithmetic: 15.9 us -> 2.23 us
  local copies, waits for them, and re-layouts: 33.2 us -> 43.9 us
  blocking collectives: 38 us -> 29.1 us
    dot_general x56 -> x8, matrix products: 123 us -> 12.6 us  [dot(): return lax.dot_general(a, b, (dims, ((), ())), preferred_element_type=F32)]
    pallas_call x8 -> x6, Pallas kernels: 248 us -> 280 us  [the longest x1 60.4 us: back_call(): pl.pallas_call(back_kernel, out_shape=outs, in_specs=specs(*[VMEM] * 6, *...]
    all_gather x0 -> x1, blocking collectives: none -> 29.1 us  [finish(): onehot = lax.all_gather(hot[:, 0], PLANE, axis=1, tiled=False)]
    psum x1 -> x0, blocking collectives: 26.5 us -> none  [local(): lows = lax.psum(lows.astype(F32), ('c', 'z')).astype(BF16)]
    ppermute x8 -> x1, starting transfers between devices: 32 us -> 13.2 us  [finish(): lax.ppermute(sums[:, :, :3072].astype(BF16), ('c', 'xh'), SWAP).astype(F32)]
    unnamed x113 -> x100, local copies, waits for them, and re-layouts: 18.3 us -> 31.8 us
    ppermute x8 -> x1, waiting for transfers between devices: 22 us -> 9.41 us  [finish(): lax.ppermute(sums[:, :, :3072].astype(BF16), ('c', 'xh'), SWAP).astype(F32)]
    unnamed x1 -> x0, blocking collectives: 11.5 us -> none
  transfers between devices with their start and end apart: 10 -> 3, of which waited for: 3 -> 3; matrix products, arithmetic and copies ran while one was open for 8% -> 1% of each run, Pallas kernels for 12% -> 0%
where the time goes in v2:
time: 463 us; the launch traced here: 459 us
  Pallas kernels  280 us (60%)
  waiting for transfers between devices  57.9 us (13%)
  local copies, waits for them, and re-layouts  43.9 us (9%)
  blocking collectives  29.1 us (6%)
  matrix products  16.6 us (4%)
  between operations  15.3 us (3%)
  starting transfers between devices  13.3 us (3%)
    pallas_call x1, Pallas kernels, back_call(): pl.pallas_call(back_kernel, out_shape=outs, in_specs=specs(*[VMEM] * 6, *...  60.4 us
    pallas_call x1, Pallas kernels, middle_call(): pl.pallas_call(middle_kernel, out_shape=outs, in_specs=specs(*[VMEM] * 8,...  59.7 us
    pallas_call x1, Pallas kernels, attend_call(): pl.pallas_call(attend_kernel, out_shape=outs, in_specs=specs(*[VMEM] * 4,...  48.6 us
    pallas_call x1, Pallas kernels, joined_call(): pl.pallas_call(joined_kernel, out_shape=outs, in_specs=specs(pltpu.SMEM,...  47.2 us
    all_gather x1, waiting for transfers between devices, finish(): every = lax.all_gather(mine, PLANE, axis=0, tiled=False)  40.1 us
    pallas_call x1, Pallas kernels, last_call(): pl.pallas_call(last_kernel, out_shape=outs, in_specs=specs(*[VMEM] * 6, A...  37.4 us
    unnamed x100, local copies, waits for them, and re-layouts  31.8 us
    all_gather x1, blocking collectives, finish(): onehot = lax.all_gather(hot[:, 0], PLANE, axis=1, tiled=False)  29.1 us
  transfers between devices with their start and end apart: 3, of which 3 were waited for; matrix products, arithmetic and copies ran while one was open for 1% of the time, Pallas kernels for 0%

profile of v2, /device:TPU:1, one launch (start us, length us, event | category | flops | bytes accessed | tf_op | source)
XLA Modules:
  0.0 458.6 jit_solution(17165748178766056588)
XLA Ops:
  8.6 1.0 copy-done.13
  9.6 1.0 copy-done.14
  10.7 1.0 copy-done.15
  11.7 1.0 copy-done.16
  12.7 1.0 copy-done.17
  13.8 0.9 copy-done.25
  14.7 0.9 copy-done.26
  15.7 0.9 copy-done.28
  16.6 0.9 copy-done.29
  17.5 0.8 copy-done.32
  20.5 47.2 %joined.1 = (bf16[128,2048]{1,0:T(8,128)(2,1)S(1)}, bf16[1024,2048]{1,0:T(8,128)(2,1)}, bf16[16,11392]{1,0:T(8,128)(2,1)S(1)}, f32[1,1792]{1,0:T(1,128)S(1)}, bf...) custom-call(s32[1]{0:T(128)S(6)} %copy.74.refs_0_, ...), custom_call_target="tpu_custom_call" | custom-call | tf_op jit(solution)/shard_map/joined/pallas_call | solution.py:584
  67.7 1.6 copy-done.8
  70.2 48.6 %attend.1 = (bf16[4,1024,128]{2,1,0:T(8,128)(2,1)S(1)}, bf16[1024,256]{1,0:T(8,128)(2,1)S(1)}, bf16[1024,2048]{1,0:T(8,128)(2,1)S(1)}, bf16[128,2048]{1,0:T(8,12...) custom-call(bf16[4,1024,128]{2,1,0:T(8,128)(2,1)S(1)} %get-tuple-element.46.ref, ...), custom_call_target="tpu_custom_call" | custom-call | tf_op jit(solution)/shard_map/attend/pallas_call | solution.py:678
  118.8 2.0 copy-done.3
  121.6 1.0 copy-done.6
  124.0 59.7 %middle.1 = (f32[128,2048]{1,0:T(8,128)}, bf16[1024,2048]{1,0:T(8,128)(2,1)}, bf16[1024,1024]{1,0:T(8,128)(2,1)}, bf16[1024,1024]{1,0:T(8,128)(2,1)}, bf16[2048,...) custom-call(bf16[1024,256]{1,0:T(8,128)(2,1)} %copy-done.4, bf16[128,2048]{1,0:T(8,128)(2,1)} %copy-done.10, ...), custom_call_target="tpu_custom_call" | custom-call | tf_op jit(solution)/shard_map/middle/pallas_call | solution.py:795
  183.7 60.4 %back.1 = (f32[128,2048]{1,0:T(8,128)}, bf16[1024,2048]{1,0:T(8,128)(2,1)}, bf16[1024,256]{1,0:T(8,128)(2,1)}, bf16[1024,2048]{1,0:T(8,128)(2,1)}, bf16[16,1024]...) custom-call(bf16[1024,1024]{1,0:T(8,128)(2,1)} %get-tuple-element.58.refs_0_, ...), custom_call_target="tpu_custom_call" | custom-call | tf_op jit(solution)/shard_map/back/pallas_call | solution.py:892
  244.2 1.0 copy-done.24
  246.0 27.0 %attend_back.1 = (bf16[1024,768]{1,0:T(8,128)(2,1)}, bf16[128,2048]{1,0:T(8,128)(2,1)S(1)}, bf16[16,1024]{1,0:T(8,128)(2,1)S(1)}) custom-call(bf16[4,1024,128]{2,1,0:T(8,128)(2,1)S(1)} %get-tuple-element.50.refs_0_, bf16[4,1024,128]{2,1,0:T(8,128)(2,1)S(1)} %get-tuple-element.47.refs_1_, bf16[4,1024,128]{2,1,0:T(8,128)(2,1)S(1)} %get-tuple-element.48.refs_2_, ...), custom_call_target="tpu_custom_call" | custom-call | tf_op jit(solution)/shard_map/attend_back/pallas_call | solution.py:984
  273.0 2.5 fusion.6
  276.4 1.0 fusion.2
  277.4 1.0 fusion.4
  278.4 1.9 copy-done.9
  280.3 1.2 copy-done.12
  281.5 1.0 copy-done.23
  282.6 37.4 %last.1 = (f32[128,2048]{1,0:T(8,128)S(1)}, bf16[128,2048]{1,0:T(8,128)(2,1)S(1)}, bf16[16,1024]{1,0:T(8,128)(2,1)S(1)}) custom-call(bf16[1024,768]{1,0:T(8,128)(2,1)S(1)} %copy-done.2, f32[128,2048]{1,0:T(8,128)S(1)} %copy-done.12, bf16[128,2048]{1,0:T(8,128)(2,1)S(1)} %copy-done.11, bf16[128,2048]{1,0:T(8,128)(2,1)S(1)} %copy-done.23, ...), custom_call_target="tpu_custom_call" | custom-call | tf_op jit(solution)/shard_map/last/pallas_call | solution.py:1048
  320.8 1.8 fusion.10
  322.6 1.8 fusion.12
  324.4 1.8 fusion.14
  326.3 1.8 fusion.16
  328.3 29.1 %all-gather.1 = bf16[16,1,8]{2,1,0:T(2,128)(2,1)S(1)} all-gather(bf16[1,1,8]{2,1,0:T(2,128)(2,1)S(1)} %bitcast.108), channel_id=1, replica_groups=mesh['xl'=2,'y'=4,'c'=2,'xh'=2,'z'=4] {'xl','y','xh'}, dimensions={0}, use_global_device_ids=true | all-gather | bytes 272 | tf_op jit(solution)/shard_map/all_gather | solution.py:1062
  357.4 40.1 %all-gather.5.cloned.1.call-done = bf16[16,16,4096]{2,1,0:T(8,128)(2,1)} async-done(((bf16[1,16,4096]{2,1,0:T(8,128)(2,1)}), bf16[16,16,4096]{2,1,0:T(8,128)(2,1)}) %all-gather.5.cloned.1.call-update) | async-done | bytes 2097168 | tf_op jit(solution)/shard_map/all_gather | solution.py:1061
  397.5 3.9 convolution_convert_fusion
  402.3 13.2 %collective-permute-start = (bf16[8,16,3072]{2,0,1:T(8,128)(2,1)S(1)}, bf16[8,16,3072]{2,0,1:T(8,128)(2,1)S(1)}, u32[]{:S(2)}, u32[]{:S(2)}) collective-permute-start(bf16[8,16,3072]{2,0,1:T(8,128)(2,1)S(1)} %slice.50), channel_id=1, source_target_pairs={{0,0},{4,8},{8,4},{12,12},{1,1},{5,9},{9,5},{13,13},{2,2},{6,10},{... | collective-permute-start | bytes 2359304 | tf_op jit(solution)/shard_map/ppermute | solution.py:1064
  415.5 9.4 %collective-permute-done = bf16[8,16,3072]{2,0,1:T(8,128)(2,1)S(1)} collective-permute-done((bf16[8,16,3072]{2,0,1:T(8,128)(2,1)S(1)}, bf16[8,16,3072]{2,0,1:T(8,128)(2,1)S(1)}, u32[]{:S(2)}, u32[]{:S(2)}) %collective-permute-start) | collective-permute-done | bytes 786464 | tf_op jit(solution)/shard_map/ppermute | solution.py:1064
  425.0 0.9 copy.59
  426.7 1.1 copy.61
  427.9 1.1 copy.62
  429.0 8.3 %all-gather.7.cloned.1.call-done = bf16[64,16,1024]{2,0,1:T(8,128)(2,1)} async-done(((bf16[8,16,1024]{2,0,1:T(8,128)(2,1)}), bf16[64,16,1024]{2,0,1:T(8,128)(2,1)}) %all-gather.7.cloned.1.call-update) | async-done | bytes 2097168 | tf_op jit(solution)/shard_map/all_gather | solution.py:1065
  437.3 2.1 convert.46
  439.4 1.9 slice_bitcast_fusion
  441.7 1.1 reshape.189
  442.8 1.6 copy.56
  444.4 1.1 reshape.190
  445.9 1.1 reshape.191
  447.0 1.6 copy.58
  448.6 1.1 reshape.192
  450.5 1.0 copy.76
  (96 shorter events, 11.7 us)
Async XLA Ops:
  7.2 390.4 %all-gather.5.cloned.1.call-start = ((), (), s32[]{:S(2)}) async-start(), calls=%async_computation | async-start | bytes 2228224 | tf_op jit(solution)/shard_map/all_gather | solution.py:1061
  8.6 1.0 copy-start.13
  9.6 1.0 copy-start.14
  10.6 1.0 copy-start.15
  11.7 1.0 copy-start.16
  12.7 1.0 copy-start.17
  13.8 0.9 copy-start.25
  14.7 0.9 copy-start.26
  15.7 0.9 copy-start.28
  16.6 0.9 copy-start.29
  17.5 0.8 copy-start.32
  18.4 0.7 copy-start.35
  19.1 0.7 copy-start.37
  20.5 49.7 %copy-start.18 = (bf16[128,2048]{1,0:T(8,128)(2,1)S(1)}, bf16[128,2048]{1,0:T(8,128)(2,1)}, u32[]{:S(2)}) copy-start(bf16[128,2048]{1,0:T(8,128)(2,1)} %refs_4_.1) | copy-start | bytes 1572868
  20.5 49.7 %copy-start.27 = (bf16[1024,128]{1,0:T(8,128)(2,1)S(1)}, bf16[1024,128]{1,0:T(8,128)(2,1)}, u32[]{:S(2)}) copy-start(bf16[1024,128]{1,0:T(8,128)(2,1)} %refs_6_.1) | copy-start | bytes 786436
  20.5 49.7 %copy-start.33 = (bf16[256,128]{1,0:T(8,128)(2,1)S(1)}, bf16[256,128]{1,0:T(8,128)(2,1)}, u32[]{:S(2)}) copy-start(bf16[256,128]{1,0:T(8,128)(2,1)} %refs_5_.3) | copy-start | bytes 196612
  67.7 1.6 copy-start.8
  69.4 0.8 copy-start.10
  70.1 48.6 %copy-start = (bf16[16,11392]{1,0:T(8,128)(2,1)}, bf16[16,11392]{1,0:T(8,128)(2,1)S(1)}, u32[]{:S(2)}) copy-start(bf16[16,11392]{1,0:T(8,128)(2,1)S(1)} %get-tuple-element.49.refs_3_.refs_2_.refs_4_.refs_9_.refs_5_) | copy-start | bytes 1093636
  70.1 48.6 %copy-start.39 = (f32[1,1792]{1,0:T(1,128)}, f32[1,1792]{1,0:T(1,128)S(1)}, u32[]{:S(2)}) copy-start(f32[1,1792]{1,0:T(1,128)S(1)} %get-tuple-element.53.refs_3_) | copy-start | bytes 21508
  118.8 2.0 copy-start.3
  120.8 0.8 copy-start.4
  121.6 1.0 copy-start.6
  122.6 0.8 copy-start.19
  183.7 60.4 %copy-start.1 = (bf16[16,11392]{1,0:T(8,128)(2,1)S(1)}, bf16[16,11392]{1,0:T(8,128)(2,1)}, u32[]{:S(2)}) copy-start(bf16[16,11392]{1,0:T(8,128)(2,1)} %copy-done) | copy-start | bytes 1093636
  183.7 60.4 %copy-start.5 = (bf16[1024,256]{1,0:T(8,128)(2,1)S(1)}, bf16[1024,256]{1,0:T(8,128)(2,1)}, u32[]{:S(2)}) copy-start(bf16[1024,256]{1,0:T(8,128)(2,1)} %copy-done.4) | copy-start | bytes 1572868
  183.7 60.4 %copy-start.7 = (f32[128,2048]{1,0:T(8,128)S(1)}, f32[128,2048]{1,0:T(8,128)}, u32[]{:S(2)}) copy-start(f32[128,2048]{1,0:T(8,128)} %get-tuple-element.60.refs_2_.refs_7_) | copy-start | bytes 3145732
  183.7 60.4 %copy-start.38 = (f32[2048]{0:T(1024)S(1)}, f32[2048]{0:T(1024)}, u32[]{:S(2)}) copy-start(f32[2048]{0:T(1024)} %param.37) | copy-start | bytes 24580
  244.2 1.0 copy-start.24
  245.2 0.8 copy-start.34
  246.0 29.6 %copy-start.46 = (bf16[16,1024]{1,0:T(8,128)(2,1)S(1)}, bf16[16,1024]{1,0:T(8,128)(2,1)}, u32[]{:S(2)}) copy-start(bf16[16,1024]{1,0:T(8,128)(2,1)} %get-tuple-element.73) | copy-start | bytes 98308
  273.0 4.4 copy-start.22
  273.0 3.4 copy-start.42
  273.0 3.4 copy-start.43
  273.0 4.4 copy-start.31
  273.0 4.4 copy-start.41
  276.4 2.0 copy-start.2
  276.4 2.0 copy-start.11
  276.4 2.0 copy-start.36
  278.4 1.9 copy-start.9
  280.3 1.2 copy-start.12
  281.5 1.0 copy-start.23
  282.6 40.0 %copy-start.44 = (bf16[16,1024]{1,0:T(8,128)(2,1)S(1)}, bf16[16,1024]{1,0:T(8,128)(2,1)}, u32[]{:S(2)}) copy-start(bf16[16,1024]{1,0:T(8,128)(2,1)} %get-tuple-element.77) | copy-start | bytes 98308
  282.6 41.8 %copy-start.45 = (bf16[16,1024]{1,0:T(8,128)(2,1)S(1)}, bf16[16,1024]{1,0:T(8,128)(2,1)}, u32[]{:S(2)}) copy-start(bf16[16,1024]{1,0:T(8,128)(2,1)} %get-tuple-element.79) | copy-start | bytes 98308
  320.0 0.8 copy-start.20
  328.1 109.2 %all-gather.7.cloned.1.call-start = ((), (), s32[]{:S(2)}) async-start(), calls=%async_computation.1 | async-start | bytes 2359296 | tf_op jit(solution)/shard_map/all_gather | solution.py:1065
  402.3 22.6 %collective-permute-start = (bf16[8,16,3072]{2,0,1:T(8,128)(2,1)S(1)}, bf16[8,16,3072]{2,0,1:T(8,128)(2,1)S(1)}, u32[]{:S(2)}, u32[]{:S(2)}) collective-permute-start(bf16[8,16,3072]{2,0,1:T(8,128)(2,1)S(1)} %slice.50), channel_id=1, source_target_pairs={{0,0},{4,8},{8,4},{12,12},{1,1},{5,9},{9,5},{13,13},{2,2},{6,10},{... | collective-permute-start | bytes 2359304 | tf_op jit(solution)/shard_map/ppermute | solution.py:1064
  447.0 2.8 copy-start.21
  (2 other events, 1.3 us)
Sparse Core Ops, SparseCore 0:
  328.2 69.2 all-gather.4
  402.3 34.9 all-gather.6

commit v3 on v2

v3 whole, which is shorter than its diff:
```python
import functools

import jax
import jax.numpy as jnp
from jax import lax
from jax.experimental import pallas as pl
from jax.experimental.pallas import tpu as pltpu
from jax.sharding import Mesh
from jax.sharding import PartitionSpec as P

HEADS = 32
EPSILON = 1e-05
MASKED = -1e30
AXES = ("xl", "y", "c", "xh", "z")
FSDP = ("xl", "y", "c")
TP = ("xh", "z")
PLANE = ("xl", "y", "xh")
MESH_ID = pl.DeviceIdType.MESH
ANY = pl.ANY
VMEM = pltpu.VMEM
DMA = pltpu.SemaphoreType.DMA
F32 = jnp.float32
BF16 = jnp.bfloat16
ORDER = (0, 3, 1, 2)
PICKS = dict(joined_in=(0, 2048), joined_out=(2048, 768), hot=(2816, 128), up_in=(2944, 2048), up_out=(4992, 1024),
             dense_in=(6016, 256), dense_out=(6272, 2048), down_in=(8320, 1024), down_out=(9344, 2048))
PICKED = 11392


def remote(src, dst, sems, index, device):
    send, recv = sems
    return pltpu.make_async_remote_copy(
        src_ref=src, dst_ref=dst, send_sem=send.at[index], recv_sem=recv.at[index],
        device_id=device, device_id_type=MESH_ID)


def places():
    return tuple(lax.axis_index(a) for a in AXES)


def at_home():
    _, _, c, xh, _ = places()
    return 1 - (xh - c) * (xh - c)


def meet(peers):
    barrier = pltpu.get_barrier_semaphore()
    for p in peers:
        pl.semaphore_signal(barrier, inc=1, device_id=p, device_id_type=MESH_ID)
    pl.semaphore_wait(barrier, len(peers))


def group_peer(n):
    _, _, c, _, z = places()
    return {"c": lax.rem(c + n // 4, 2), "z": lax.rem(z + n % 4, 4)}


def group_peers():
    return [group_peer(n) for n in range(1, 8)]


def diagonal():
    _, _, c, xh, _ = places()
    return {"c": 1 - c, "xh": 1 - xh}


def plane_peers():
    xl, y, c, xh, _ = places()
    peers = []
    for d in range(1, 4):
        for core in (0, 1):
            peers.append({"y": lax.rem(y + d, 4), "c": core})
            x = lax.rem(xh * 2 + xl + d, 4)
            peers.append({"xh": x // 2, "xl": lax.rem(x, 2), "c": core})
    return peers


def block(ref, n, size=128):
    return ref.at[pl.ds(pl.multiple_of(n * size, size), size)]


class GroupGather:
    SEMS = [DMA((8, 4)), DMA((8, 4))]

    def __init__(self, dst, send, recv):
        self.dst, self.sems = dst, (send, recv)
        _, _, self.c, _, self.z = places()
        self.up, self.down, self.other = group_peer(1), group_peer(3), group_peer(4)

    def at(self, core, z, j):
        return self.dst.at[pl.ds(pl.multiple_of((core * 4 + z) * 128 + j * 32, 32), 32)]

    def copy(self, z, j, kind, device):
        ref = self.at(self.c, z, j)
        return remote(ref, ref, self.sems, (kind, j), device)

    def put(self, j):
        self.copy(self.z, j, 0, self.up).start()
        self.copy(self.z, j, 1, self.down).start()
        self.copy(self.z, j, 2, self.other).start()

    def near(self, j):
        below, above = lax.rem(self.z + 3, 4), lax.rem(self.z + 1, 4)
        self.copy(below, j, 0, self.up).wait_recv()
        if j < 2:
            self.copy(below, j, 3, self.up).start()
        self.copy(below, j, 5, self.other).start()
        self.copy(above, j, 1, self.down).wait_recv()
        if j >= 2:
            self.copy(above, j, 4, self.down).start()
        self.copy(above, j, 6, self.other).start()

    def far(self, j):
        opposite = lax.rem(self.z + 2, 4)
        self.copy(opposite, j, 3 if j < 2 else 4, self.up).wait_recv()
        self.copy(opposite, j, 7, self.other).start()

    def shared(self, kind):
        for j in ORDER:
            self.copy(self.z, j, kind, self.other).wait_recv()

    def finish(self):
        for j in ORDER:
            for kind in (0, 1, 2, 3 if j < 2 else 4, 5, 6, 7):
                self.copy(self.z, j, kind, self.other).wait_send()


class LowGather:
    SEMS = [DMA((8,)), DMA((8,))]

    def __init__(self, dst, send, recv):
        self.dst, self.sems = dst, (send, recv)
        _, _, c, _, z = places()
        self.own = pl.ds(pl.multiple_of((c * 4 + z) * 128, 128), 128)

    def copies(self):
        ref = self.dst.at[:, self.own]
        return [remote(ref, ref, self.sems, (n,), group_peer(n)) for n in range(1, 8)]

    def start(self, value):
        self.dst[:, self.own] = value
        for copy in self.copies():
            copy.start()

    def wait(self):
        for copy in self.copies():
            copy.wait()


class LowSum:
    SEMS = [DMA((8,)), DMA((8,))]

    def __init__(self, src, got, send, recv):
        self.src, self.got, self.sems = src, got, (send, recv)
        _, _, self.c, _, self.z = places()

    def copies(self):
        out = []
        for n in range(1, 8):
            p = group_peer(n)
            cols = pl.ds(pl.multiple_of((p["c"] * 4 + p["z"]) * 128, 128), 128)
            out.append(remote(self.src.at[:, cols], self.got.at[n], self.sems, (n,), p))
        return out

    def start(self):
        for copy in self.copies():
            copy.start()

    def total(self):
        for copy in self.copies():
            copy.wait()
        own = pl.ds(pl.multiple_of((self.c * 4 + self.z) * 128, 128), 128)
        out = self.src[:, own].astype(F32)
        for n in range(1, 8):
            out = out + self.got[n].astype(F32)
        return out.astype(BF16)


class PlaneGather:
    SEMS = [DMA((1,)), DMA((22,)), DMA((16,))]

    def __init__(self, src, dst, by_rows, local_sem, send, recv):
        self.src, self.dst, self.by_rows, self.local_sem, self.sems = src, dst, by_rows, local_sem, (send, recv)
        self.xl, self.y, self.c, self.xh, _ = places()
        self.x = self.xh * 2 + self.xl
        self.home = at_home()

    def slot(self, xl, y, core):
        k = (xl * 4 + y) * 2 + core
        if self.by_rows:
            return k, block(self.dst, k)
        return k, self.dst.at[:, pl.ds(pl.multiple_of(k * 128, 128), 128)]

    def send(self, src, where, n, device):
        k, dst = where
        send, recv = self.sems
        return pltpu.make_async_remote_copy(
            src_ref=src, dst_ref=dst, send_sem=send.at[n], recv_sem=recv.at[k],
            device_id=device, device_id_type=MESH_ID)

    def arrived(self, where):
        self.send(where[1], where, 0, {"c": 1 - self.c}).wait_recv()

    def chip_x(self, d, core):
        x = lax.rem(self.x + d, 4)
        return {"xh": x // 2, "xl": lax.rem(x, 2), "c": core}

    def chip_y(self, d, core):
        return {"y": lax.rem(self.y + d, 4), "c": core}

    def first(self, act):
        own = self.slot(self.xl, self.y, self.c)

        @pl.when(self.c == 0)
        def _():
            for d in (1, 3, 2):
                act(self.send(self.src, own, d, self.chip_x(d, self.xh)))

        @pl.when(self.c == 1)
        def _():
            for d in (1, 3, 2):
                act(self.send(self.src, own, d, self.chip_y(d, self.xh)))

        @pl.when(self.home == 0)
        def _():
            act(self.send(self.src, own, 0, {"c": 1 - self.c}))

    def start(self):
        @pl.when(self.home == 1)
        def _():
            pltpu.make_async_copy(self.src, self.slot(self.xl, self.y, self.c)[1], self.local_sem.at[0]).start()

        self.first(lambda copy: copy.start())

    def columns(self):
        one = self.home * self.xl
        return one, 1 - one

    def rows_step(self, n, act):
        where = self.slot(self.columns()[n], self.y, 0)
        for d in (1, 3, 2):
            act(self.send(where[1], where, 4 + n * 3 + d - 1, self.chip_y(d, self.c)))

    def columns_step(self, n, act):
        where = self.slot(self.xl, lax.rem(self.y + n, 4), 1)

        @pl.when(self.home == 1)
        def _():
            for d in (1, 3, 2):
                act(self.send(where[1], where, 10 + n * 3 + d - 1, self.chip_x(d, self.c)))

    def step(self, n):
        if n == 0:
            @pl.when(self.home == 1)
            def _():
                pltpu.make_async_copy(self.src, self.slot(self.xl, self.y, self.c)[1], self.local_sem.at[0]).wait()
        if n < 2:
            where = self.slot(self.columns()[n], self.y, 0)
            if n == 0:
                @pl.when(self.home * (1 - self.c) == 0)
                def _():
                    self.arrived(where)
            else:
                self.arrived(where)
            self.rows_step(n, lambda copy: copy.start())
        else:
            where = self.slot(self.xl, lax.rem(self.y + n - 2, 4), 1)
            here = self.home * (1 - self.c) if n == 2 else self.home

            @pl.when(here == 1)
            def _():
                self.arrived(where)

            self.columns_step(n - 2, lambda copy: copy.start())

    def wait(self):
        for xl in (0, 1):
            for d in (1, 2, 3):
                self.arrived(self.slot(xl, lax.rem(self.y + d, 4), 0))
        one, two = self.columns()
        for y in range(4):
            self.arrived(self.slot(two, y, 1))

        @pl.when(self.home == 0)
        def _():
            for y in range(4):
                self.arrived(self.slot(one, y, 1))

    def finish(self):
        self.first(lambda copy: copy.wait_send())
        for n in (0, 1):
            self.rows_step(n, lambda copy: copy.wait_send())
        for n in range(4):
            self.columns_step(n, lambda copy: copy.wait_send())


class GroupSum:
    NAMES = ("far_up", "far_down", "up_high", "down_low", "up_low", "down_high")
    SCRATCH = [VMEM((1024, 2048), BF16), VMEM((4, 128, 2048), BF16), VMEM((3, 128, 2048), BF16),
               VMEM((2, 64, 2048), BF16), VMEM((2, 128, 2048), BF16), DMA((10,)), DMA((10,))]

    def __init__(self, parts, near, sent, half, full, send, recv):
        self.parts, self.near, self.sent, self.half, self.full, self.sems = parts, near, sent, half, full, (send, recv)
        _, _, self.c, _, self.z = places()
        self.up, self.down, self.other = group_peer(1), group_peer(3), group_peer(4)
        self.order = [lax.rem(self.z + d, 4) for d in (2, 1, 3, 0)]

    def part(self, core, i):
        return block(self.parts, core * 4 + self.order[i])

    def given(self, i):
        return remote(self.part(1 - self.c, i), self.near.at[i], self.sems, (i,), self.other)

    def give(self, i):
        self.given(i).start()

    def pair(self, i, rows=slice(None)):
        return self.part(self.c, i)[rows].astype(F32) + self.near[i, rows].astype(F32)

    def piece(self, name):
        low, high = pl.ds(0, 64), pl.ds(64, 64)
        n = self.NAMES.index(name)
        src = (self.sent.at[0, low], self.sent.at[0, high], self.sent.at[1, high], self.sent.at[2, low],
               self.sent.at[1, low], self.sent.at[2, high])[n]
        dst = (self.half.at[0], self.half.at[1], self.full.at[0, high], self.full.at[1, low],
               self.full.at[0, low], self.full.at[1, high])[n]
        return remote(src, dst, self.sems, (4 + n,), (self.up, self.down)[n % 2])

    def far(self):
        self.given(0).wait_recv()
        self.sent[0] = self.pair(0).astype(BF16)
        self.piece("far_up").start()
        self.piece("far_down").start()

    def near_up(self):
        self.given(1).wait_recv()
        self.sent[1, pl.ds(64, 64)] = self.pair(1, pl.ds(64, 64)).astype(BF16)
        self.piece("up_high").start()

    def near_down(self):
        self.given(2).wait_recv()
        self.sent[2, pl.ds(0, 64)] = self.pair(2, pl.ds(0, 64)).astype(BF16)
        self.piece("down_low").start()

    def pass_on(self):
        low, high = pl.ds(0, 64), pl.ds(64, 64)
        self.piece("far_up").wait_recv()
        self.sent[1, low] = (self.pair(1, low) + self.half[0].astype(F32)).astype(BF16)
        self.piece("up_low").start()
        self.piece("far_down").wait_recv()
        self.sent[2, high] = (self.pair(2, high) + self.half[1].astype(F32)).astype(BF16)
        self.piece("down_high").start()

    def arrive(self):
        self.given(3).wait_recv()
        for name in ("up_high", "down_low", "up_low", "down_high"):
            self.piece(name).wait_recv()

    def total(self, rows=slice(None)):
        return self.pair(3, rows) + self.full[0, rows].astype(F32) + self.full[1, rows].astype(F32)

    def finish(self):
        for name in self.NAMES:
            self.piece(name).wait_send()
        for i in range(4):
            self.given(i).wait_send()


def params(cid, mib):
    return pltpu.CompilerParams(collective_id=cid, has_side_effects=True, vmem_limit_bytes=mib << 20)


def plain(mib):
    return pltpu.CompilerParams(vmem_limit_bytes=mib << 20)


def shape(*dims, dtype=BF16):
    return jax.ShapeDtypeStruct(dims, dtype)


def specs(*spaces):
    return [pl.BlockSpec(memory_space=s) for s in spaces]


def layer_norm(rows_in, gain, shift):
    row_mean = jnp.mean(rows_in, axis=-1, keepdims=True)
    centered = rows_in - row_mean
    variance = jnp.mean(centered * centered, axis=-1, keepdims=True)
    return centered * lax.rsqrt(variance + EPSILON) * gain + shift


def norm_back(rows_in, gain, grad):
    row_mean = jnp.mean(rows_in, axis=-1, keepdims=True)
    centered = rows_in - row_mean
    inverse = lax.rsqrt(jnp.mean(centered * centered, axis=-1, keepdims=True) + EPSILON)
    n = centered * inverse
    e = gain * grad
    return (e - jnp.mean(e, axis=-1, keepdims=True) - n * jnp.mean(e * n, axis=-1, keepdims=True)) * inverse


def dot(a, b, dims=((1,), (0,))):
    return lax.dot_general(a, b, (dims, ((), ())), preferred_element_type=F32)


def dot_t(a, b):
    return dot(a, b, ((1,), (1,)))


def dot_o(a, b):
    return dot(a, b, ((0,), (0,)))


def tiles(count, size, body):
    def run(i, carry):
        body(pl.ds(pl.multiple_of(i * size, size), size))
        return carry

    lax.fori_loop(0, count, run, 0)


def split_refs(refs, *counts):
    refs, out = list(refs), []
    for n in counts:
        out.append(refs[:n])
        refs = refs[n:]
    return (*out, refs)


def pick(ref, name):
    first, n = PICKS[name]
    return ref[:, pl.ds(first, n)]


def row_pair(z):
    return (pl.ds(pl.multiple_of(z * 128, 128), 128), pl.ds(pl.multiple_of(512 + z * 128, 128), 128))


def take_pair(ref, z, cols=slice(None)):
    a, b = row_pair(z)
    return jnp.concatenate([ref[a, cols], ref[b, cols]], axis=0)


def put_pair(ref, z, value, cols=slice(None)):
    a, b = row_pair(z)
    ref[a, cols] = value[:128]
    ref[b, cols] = value[128:]


class Swap:
    def __init__(self, pairs, local, send, recv):
        self.pairs, self.local, self.sems, self.home = pairs, local, (send, recv), at_home()

    def near_copy(self, n):
        src, _, dst = self.pairs[n]
        return pltpu.make_async_copy(src, dst, self.local.at[n])

    def far_copy(self, n):
        src, dst, _ = self.pairs[n]
        return remote(src, dst, self.sems, (n,), diagonal())

    def start(self, n):
        @pl.when(self.home == 1)
        def _():
            self.near_copy(n).start()

        @pl.when(self.home == 0)
        def _():
            self.far_copy(n).start()

    def wait(self, n):
        @pl.when(self.home == 1)
        def _():
            self.near_copy(n).wait()

        @pl.when(self.home == 0)
        def _():
            self.far_copy(n).wait_recv()

    def finish(self):
        @pl.when(self.home == 0)
        def _():
            for n in range(len(self.pairs)):
                self.far_copy(n).wait_send()

    @staticmethod
    def sems(n):
        return [DMA((n,)), DMA((n,)), DMA((n,))]


class Spread:
    SCRATCH = [VMEM((16, 5, 8, 128), BF16), VMEM((16, 5, 8, 128), BF16), VMEM((8, 3, 8, 128), BF16),
               VMEM((8, 8, 128), BF16), DMA((16,)), DMA((16,)), DMA((9,)), DMA((16,)), DMA((20,)), DMA((20,)), DMA((2,))]

    def __init__(self, split, whole, send, got, part, full, one_send, one_recv, two_send, two_recv, send3, recv3, local):
        self.split, self.whole, self.send, self.got, self.part, self.full = split, whole, send, got, part, full
        self.one, self.two, self.three, self.local = (one_send, one_recv), (two_send, two_recv), (send3, recv3), local
        self.xl, self.y, self.c, self.xh, self.z = places()
        self.q = (self.xh * 2 + self.xl) * 4 + self.y
        self.home = at_home()

    def put(self, n, value):
        for m in range(4):
            k = 2 * n + m
            where = (k // 3, k % 3) if k < 48 else (k - 48, 3)
            row, col = m % 2 * 8, m // 2 * 128
            self.send[where] = value[row:row + 8, col:col + 128].astype(BF16)

    def mark(self, hot):
        for j in range(16):
            self.send[j, 4] = hot

    def chip(self, n):
        q = lax.rem(self.q + n, 16)
        x = q // 4
        return q, {"xh": x // 2, "xl": lax.rem(x, 2), "y": lax.rem(q, 4)}

    def to_owners(self):
        out = []
        for n in range(1, 16):
            q, device = self.chip(n)
            out.append(remote(self.send.at[q], self.got.at[n], self.one, (n,), device))
        return out

    def start(self):
        for copy in self.to_owners():
            copy.start()

    def add(self):
        self.got[0] = self.send[self.q]
        for copy in self.to_owners():
            copy.wait_recv()
        for b in range(8):
            total = jnp.zeros((4, 8, 128), F32)
            for n in range(16):
                hot = self.got[n, 4].astype(F32)[b:b + 1]
                total = total + self.got[n, 0:4].astype(F32) * hot
            total = total.astype(BF16)
            self.part[b] = total[:3]
            self.full[b] = total[3]

    def split_copies(self):
        out = []
        for e in (0, 1):
            for d in range(4):
                device = {"xh": self.c, "xl": lax.rem(self.xl + e, 2), "y": lax.rem(self.y + d, 4)}
                send, recv = self.two
                out.append(pltpu.make_async_remote_copy(
                    src_ref=self.part, dst_ref=self.split.at[self.q], send_sem=send.at[e * 4 + d],
                    recv_sem=recv.at[self.q], device_id=device, device_id_type=MESH_ID))
        return out

    def split_own(self):
        return pltpu.make_async_copy(self.part, self.split.at[self.q], self.local.at[0])

    def whole_own(self):
        return pltpu.make_async_copy(self.full, self.whole.at[self.c * 4 + self.z, self.q], self.local.at[1])

    def line_copies(self):
        where = self.whole.at[self.c * 4 + self.z, self.q]
        return [remote(self.full, where, self.three, (d,), {"z": lax.rem(self.z + d, 4)}) for d in (1, 2, 3)]

    def plane_copies(self):
        where = self.whole.at[pl.ds(self.c * 4, 4), self.q]
        return [remote(where, where, self.three, (4 + n,), self.chip(n)[1]) for n in range(1, 16)]

    def shared_whole(self):
        where = self.whole.at[pl.ds(self.c * 4, 4)]
        return remote(where, where, self.three, (0,), {"c": 1 - self.c})

    def shared_split(self):
        send, recv = self.two
        return pltpu.make_async_remote_copy(
            src_ref=self.split, dst_ref=self.split, send_sem=send.at[8], recv_sem=recv.at[0],
            device_id={"c": 1 - self.c}, device_id_type=MESH_ID)

    def deal(self):
        self.whole_own().start()
        for copy in self.line_copies():
            copy.start()
        copies = self.split_copies()

        @pl.when(self.home == 1)
        def _():
            self.split_own().start()

        @pl.when(self.home == 0)
        def _():
            copies[0].start()

        for copy in copies[1:]:
            copy.start()

    def deal_plane(self):
        self.whole_own().wait()
        for copy in self.line_copies():
            copy.wait_recv()
        for copy in self.plane_copies():
            copy.start()

    def share(self):
        @pl.when(self.home == 1)
        def _():
            self.split_own().wait()
            send, recv = self.two
            for q in range(16):
                @pl.when(self.q != q)
                def _(q=q):
                    pltpu.make_async_remote_copy(
                        src_ref=self.part, dst_ref=self.split.at[q], send_sem=send.at[0], recv_sem=recv.at[q],
                        device_id={"c": 1 - self.c}, device_id_type=MESH_ID).wait_recv()

            self.shared_split().start()

        for copy in self.plane_copies():
            copy.wait_recv()
        self.shared_whole().start()

    def finish(self):
        self.shared_whole().wait()

        @pl.when(self.home == 1)
        def _():
            self.shared_split().wait_send()

        @pl.when(self.home == 0)
        def _():
            self.shared_split().wait_recv()
            self.split_copies()[0].wait_send()

        for copy in self.split_copies()[1:] + self.line_copies() + self.plane_copies() + self.to_owners():
            copy.wait_send()


def far_peers():
    xl, y, _, xh, _ = places()
    peers = []
    for d in range(1, 4):
        x = lax.rem(xh * 2 + xl + d, 4)
        for e in range(1, 4):
            peers.append({"xh": x // 2, "xl": lax.rem(x, 2), "y": lax.rem(y + e, 4)})
    return peers


ROOT_HALF = 0.7071067811865476
ROOT_TAU = 0.3989422804014327
SETS = dict(joined_in=(0, 0), up_in=(128, 0), dense_out=(256, 0), down_out=(384, 0), up_out=(512, 0),
            down_in=(512, 1024), joined_out=(640, 0), dense_in=(640, 768))


def cast_parts(value):
    high = value.astype(BF16).astype(F32)
    middle = (value - high).astype(BF16).astype(F32)
    return high, middle, value - high - middle


def block_kernel(*refs):
    (ids, tokens, go, *vectors), adapters, shards, outs, scratch = split_refs(refs, 11, 8, 4, 4)
    back, out, split, whole = outs
    names = list(SCRATCH)
    v = dict(zip(names, scratch))
    rest = list(scratch[len(names):])

    def sems(n):
        taken = rest[:n]
        del rest[:n]
        return taken

    load_sem, vector_sem, copy_sem = sems(3)
    xl, y, c, xh, z = places()
    own = c * 4 + z
    mine_rows = pl.ds(pl.multiple_of(own * 128, 128), 128)
    there_rows = (1 - c) * 4 + z
    gain1, shift1, gain2, shift2, bias_d, bias_n = (v["lines"].at[n:n + 1] for n in range(6))
    pk, xs, xbuf, gbuf = v["pk"], v["xs"], v["xbuf"], v["gbuf"]
    sets = v["parts"]
    loads = {}
    for n, (name, ref) in enumerate(zip(SETS, adapters)):
        row, col = SETS[name]
        loads[name] = pltpu.make_async_copy(ref, sets.at[pl.ds(row, 128), pl.ds(col, ref.shape[1])], load_sem.at[n])
        loads[name].start()
    lines = [pltpu.make_async_copy(ref, v["lines"].at[n:n + 1], vector_sem.at[n]) for n, ref in enumerate(vectors[:6])]
    for line in lines:
        line.start()
    meet(plane_peers() + group_peers() + far_peers())

    bias = v["bias"]
    mine = v["mine"]
    piece = lambda who, j: gbuf.at[pl.ds(pl.multiple_of(who * 128 + j * 32, 32), 32)]
    sub = lambda ref, j: ref.at[pl.ds(j * 32, 32)]
    cut = 2944
    pairs = [(sub(tokens, j), sub(xs, j), sub(xs, j)) for j in range(4)]
    pairs += [(m, p, p) for m, p in ((mine.at[:, :cut], pk.at[:, :cut]), (mine.at[:, cut:], pk.at[:, cut:]),
                                     (vectors[6], bias.at[:, :1024]), (vectors[7], bias.at[:, 1024:]))]
    pairs += [(sub(go, j), piece(there_rows, j), piece(own, j)) for j in range(4)]
    sw = Swap(pairs, *sems(3))
    for j in ORDER:
        sw.start(j)
    joined = PlaneGather(shards[0], v["wj"], True, *sems(3))
    dense = PlaneGather(shards[1], v["wd"], False, *sems(3))
    down = PlaneGather(shards[2], v["wn"], False, *sems(3))
    up = PlaneGather(shards[3], v["wu"], True, *sems(3))
    joined.start()
    set_id = ids[0]
    for name, (row, col) in SETS.items():
        first, n = PICKS[name]
        loads[name].wait()
        chosen = sets[row:row + 16, col:col + n]
        for k in range(1, 8):
            chosen = jnp.where(set_id == k, sets[row + k * 16:row + k * 16 + 16, col:col + n], chosen)
        mine[:, first:first + n] = chosen
    first, n = PICKS["hot"]
    mine[:, first:first + n] = jnp.where(lax.broadcasted_iota(jnp.int32, (16, 128), 0) == set_id, 1.0, 0.0).astype(BF16)
    for n in range(4, 8):
        sw.start(n)
    for line in lines:
        line.wait()
    g1 = GroupGather(xbuf, *sems(2))
    low_q = LowGather(v["low_q"], *sems(2))
    for j in ORDER:
        sw.wait(j)
        x1 = layer_norm(xs[j * 32:(j + 1) * 32].astype(F32), gain1[...], shift1[...])
        xbuf[pl.ds(pl.multiple_of(own * 128 + j * 32, 32), 32)] = x1.astype(BF16)
        g1.put(j)
    sw.wait(4)
    low_q.start(dot_t(pick(pk, "joined_in"), xbuf[mine_rows]).astype(BF16))
    for j in ORDER:
        sw.start(8 + j)
    g1.near(0)
    joined.step(0)
    joined.step(1)
    g1.near(3)
    joined.step(2)
    joined.step(3)
    g1.near(1)
    joined.step(4)
    joined.step(5)
    g1.near(2)
    for n in range(5, 8):
        sw.wait(n)
    for j in ORDER:
        g1.far(j)
    g2 = GroupGather(gbuf, *sems(2))
    for j in ORDER:
        sw.wait(8 + j)
        g2.put(j)
    low_g = LowGather(v["low_g"], *sems(2))
    low_g.start(dot_t(pick(pk, "down_out"), gbuf[mine_rows]).astype(BF16))
    v["gos"][...] = gbuf[mine_rows]
    dense.start()
    for kind in (2, 5, 6, 7):
        g1.shared(kind)
    joined.wait()
    down.start()
    low_q.wait()

    lane = lax.broadcasted_iota(jnp.int32, (256, 128), 1)
    row = lax.broadcasted_iota(jnp.int32, (256, 128), 0)
    qa, ka, va = v["qa"], v["ka"], v["va"]

    def project(i, carry):
        rows = pl.ds(pl.multiple_of(i * 256, 256), 256)
        acc = dot(xbuf[rows], v["wj"][...]) + dot_o(v["low_q"][:, rows], pick(pk, "joined_out")) + bias[:, :768]
        b = acc.astype(BF16).astype(F32)
        position = (i * 256 + row).astype(F32) * 0.125
        ones = jnp.where(lane < 67, 1.0, 0.0)
        for h in range(4):
            slope = jnp.exp2((own * 4 + h + 1).astype(F32) * (-8.0 / HEADS) + jnp.zeros((1, 128), F32))
            high, middle, lowest = cast_parts(position * slope)
            tail = jnp.where(lane == 64, high, jnp.where(lane == 65, middle, jnp.where(lane == 66, lowest, jnp.where(
                lane < 70, 1.0, 0.0))))
            at = h * 192
            qa[h, rows] = jnp.where(lane < 64, b[:, at:at + 128] * 0.125, ones).astype(BF16)
            ka[h, rows] = jnp.where(lane < 64, b[:, at + 64:at + 192], tail).astype(BF16)
            value = jnp.concatenate([b[:, at + 128:at + 192], b[:, at:at + 64]], axis=1)
            va[h, rows] = jnp.where(lane < 64, value, ones).astype(BF16)
        return carry

    lax.fori_loop(0, 4, project, 0)
    own_cols = pl.ds(pl.multiple_of(own * 256, 256), 256)
    keep = lambda n, ref: pltpu.make_async_copy(ref.at[:, own_cols], v["cols"].at[n], copy_sem.at[n])
    keep(0, xbuf).start()
    dense.step(0)
    dense.step(1)

    hooks = [lambda: g2.near(0), lambda: down.step(0), lambda: g2.near(3), lambda: down.step(1), lambda: g2.near(1),
             lambda: (dense.step(2), dense.step(3)), lambda: g2.near(2), lambda: (dense.step(4), dense.step(5)),
             lambda: down.step(2), lambda: (g2.far(0), g2.far(3)), lambda: down.step(3), lambda: (g2.far(1), g2.far(2)),
             lambda: down.step(4), lambda: None, lambda: down.step(5), lambda: up.start()]
    mask = lax.broadcasted_iota(jnp.int32, (256, 256), 0) <= lax.broadcasted_iota(jnp.int32, (256, 256), 1)
    line = lax.broadcasted_iota(jnp.int32, (128, 256), 0)
    c4 = v["c4"]

    def head(h, carry):
        for i in range(4):
            rows = pl.ds(i * 256, 256)
            q = qa[h, rows]
            last = jnp.where(mask, dot_t(ka[h, rows], q), MASKED)
            top = jnp.max(last, axis=0, keepdims=True)
            if i:
                before = dot_t(ka[h, pl.ds(0, i * 256)], q)
                top = jnp.maximum(top, jnp.max(before, axis=0, keepdims=True))
            mix = dot_o(va[h, rows], jnp.exp(last - top).astype(BF16))
            if i:
                mix = mix + dot_o(va[h, pl.ds(0, i * 256)], jnp.exp(before - top).astype(BF16))
            total = mix[64:65]
            high, middle, lowest = cast_parts(-(top + jnp.log(total)))
            mix = jnp.where(line == 67, high, jnp.where(line == 68, middle, jnp.where(
                line == 69, lowest, mix / total)))
            turned = mix.T
            c4[h, rows] = turned.astype(BF16)
            qa[h, rows] = jnp.where(lane < 67, q.astype(F32), jnp.where(lane < 70, turned, 0.0)).astype(BF16)
            for k in range(4):
                @pl.when(h == k)
                def _(k=k, i=i):
                    hooks[k * 4 + i]()
        return carry

    lax.fori_loop(0, 4, head, 0)
    ctx = v["ctx"]
    for h in (0, 2):
        ctx[:, h * 64:h * 64 + 128] = jnp.concatenate([c4[h, :, :64], c4[h + 1, :, :64]], axis=1)

    src, got = v["low_src"], v["low_got"]
    src[0] = dot_t(pick(pk, "dense_in"), ctx[...]).astype(BF16)
    sum_d = LowSum(src.at[0], got.at[0], *sems(2))
    sum_d.start()
    s1 = GroupSum(*[v[n] for n in ("parts", "near", "sent", "half", "full")], *sems(2))
    dense.wait()
    keep(0, xbuf).wait()
    g1.finish()

    def dense_part(i):
        put_pair(s1.parts, s1.order[i], dot(take_pair(ctx, s1.order[i]), v["wd"][...]).astype(BF16))
        s1.give(i)

    dense_part(0)
    dense_part(1)
    s1.far()
    up.step(0)
    up.step(1)
    dense_part(2)
    s1.near_up()
    dense_part(3)
    s1.near_down()
    up.step(2)
    up.step(3)
    for kind in (2, 5, 6, 7):
        g2.shared(kind)
    keep(3, gbuf).start()
    s1.pass_on()
    mid, dmid, dact = v["mid"], v["dmid"], v["dact"]
    total_d = sum_d.total()
    mid[...] = dot_o(total_d, pick(pk, "dense_out")) + bias_d[...] + xs[...].astype(F32)
    low_g.wait()
    down.wait()

    def grad_act(rows):
        dact[rows] = dot_t(gbuf[rows], v["wn"][...]) + dot_o(v["low_g"][:, rows], pick(pk, "down_in"))

    tiles(2, 256, grad_act)
    up.step(4)
    up.step(5)
    tiles(2, 256, lambda rows: grad_act(pl.ds(pl.multiple_of(rows.start + 512, 256), 256)))
    s1.arrive()
    g3 = GroupGather(xbuf, *sems(2))
    for j in ORDER:
        rows = slice(j * 32, (j + 1) * 32)
        mid[rows] = mid[rows] + s1.total(rows)
        xbuf[pl.ds(pl.multiple_of(own * 128 + j * 32, 32), 32)] = layer_norm(mid[rows], gain2[...], shift2[...]).astype(BF16)
        g3.put(j)
    low_u = LowGather(v["low_u"], *sems(2))
    low_u.start(dot_t(pick(pk, "up_in"), xbuf[mine_rows]).astype(BF16))
    all_d = LowGather(v["sum_d"], *sems(2))
    all_d.start(total_d)
    up.wait()
    low_u.wait()
    act, dpre = v["act"], v["dpre"]

    def forward(at):
        x = take_pair(xbuf, at)
        lu = jnp.concatenate([v["low_u"][:, rows] for rows in row_pair(at)], axis=1)

        def run(n, carry):
            cols = pl.ds(pl.multiple_of(n * 256, 256), 256)
            w = pk[:, pl.ds(pl.multiple_of(PICKS["up_out"][0] + n * 256, 128), 256)]
            b = bias[:, pl.ds(pl.multiple_of(1024 + n * 256, 256), 256)]
            pre = dot(x, v["wu"][:, cols]) + dot_o(lu, w) + b
            cdf = 0.5 * (1.0 + lax.erf(pre * ROOT_HALF))
            put_pair(act, at, (pre * cdf).astype(BF16), cols)
            slope = cdf + pre * (jnp.exp(-0.5 * pre * pre) * ROOT_TAU)
            put_pair(dpre, at, (take_pair(dact, at, cols) * slope).astype(BF16), cols)
            return carry

        lax.fori_loop(0, 4, run, 0)

    def by_pairs(g, work):
        g.shared(2)
        work(z)
        for j in ORDER:
            g.near(j)
        g.shared(5)
        work(lax.rem(z + 3, 4))
        g.shared(6)
        work(lax.rem(z + 1, 4))
        for j in ORDER:
            g.far(j)
        g.shared(7)
        work(lax.rem(z + 2, 4))

    by_pairs(g3, forward)
    keep(2, xbuf).start()

    src[1] = dot_t(pick(pk, "up_out"), dpre[...]).astype(BF16)
    sum_u = LowSum(src.at[1], got.at[1], *sems(2))
    sum_u.start()
    s2 = GroupSum(*[v[n] for n in ("parts", "near", "sent", "half", "full")], *sems(2))
    s1.finish()

    def wide_part(s, ref, weight):
        def part(i):
            x = take_pair(ref, s.order[i])

            def run(n, carry):
                cols = pl.ds(pl.multiple_of(n * 512, 512), 512)
                put_pair(s.parts, s.order[i], dot_t(x, weight[cols]).astype(BF16), cols)
                return carry

            lax.fori_loop(0, 4, run, 0)
            s.give(i)

        part(0)
        part(1)
        s.far()
        part(2)
        s.near_up()
        part(3)
        s.near_down()
        s.pass_on()

    keep(2, xbuf).wait()
    g3.finish()
    wide_part(s2, dpre, v["wu"])
    total_u = sum_u.total()
    keep(3, gbuf).wait()
    g2.finish()
    mlp = gbuf

    def forward_down(rows):
        mlp[rows] = dot(act[rows], v["wn"][...]).astype(BF16)

    tiles(4, 256, forward_down)
    src[2] = dot_t(pick(pk, "down_in"), act[...]).astype(BF16)
    dmid[...] = dot_o(total_u, pick(pk, "up_in"))
    s2.arrive()
    g4 = GroupGather(xbuf, *sems(2))
    for j in ORDER:
        rows = slice(j * 32, (j + 1) * 32)
        dmid[rows] = v["gos"][rows].astype(F32) + norm_back(mid[rows], gain2[...], dmid[rows] + s2.total(rows))
        xbuf[pl.ds(pl.multiple_of(own * 128 + j * 32, 32), 32)] = dmid[rows].astype(BF16)
        g4.put(j)
    low_d = LowGather(v["low_d"], *sems(2))
    low_d.start(dot_t(pick(pk, "dense_out"), xbuf[mine_rows]).astype(BF16))
    all_u = LowGather(v["sum_u"], *sems(2))
    all_u.start(total_u)
    sum_n = LowSum(src.at[2], got.at[2], *sems(2))
    sum_n.start()
    low_d.wait()
    dctx = v["dctx"]

    def context(at):
        ld = jnp.concatenate([v["low_d"][:, rows] for rows in row_pair(at)], axis=1)
        value = dot_t(take_pair(xbuf, at), v["wd"][...]) + dot_o(ld, pick(pk, "dense_in"))
        put_pair(dctx, at, value.astype(BF16))

    by_pairs(g4, context)
    keep(1, xbuf).start()

    s3 = GroupSum(mlp, *[v[n] for n in ("near2", "sent2", "half2", "full2")], *sems(2))
    for i in range(4):
        s3.give(i)
    wide_lane = lax.broadcasted_iota(jnp.int32, (1024, 128), 1)
    grads = c4
    for h in range(4):
        first = h // 2 * 128
        g = dctx[:, first:first + 128].astype(F32)
        f = ctx[:, first:first + 128].astype(F32)
        here = (wide_lane // 64) == h % 2
        high, middle, lowest = cast_parts(-jnp.sum(jnp.where(here, g * f, 0.0), axis=-1, keepdims=True))
        if h % 2:
            g = jnp.concatenate([g[:, 64:], g[:, :64]], axis=1)
        grads[h] = jnp.where(wide_lane < 64, g, jnp.where(wide_lane == 64, high, jnp.where(
            wide_lane == 65, middle, jnp.where(wide_lane == 66, lowest, 0.0)))).astype(BF16)
    all_n = LowGather(v["sum_n"], *sems(2))

    def low_step():
        all_n.start(sum_n.total())

    hooks_back = {0: s3.far, 1: s3.near_up, 2: s3.near_down, 5: low_step, 6: s3.pass_on}
    dk, dv = v["dk"], v["dv"]

    def head_back(h, carry):
        dk[...] = jnp.zeros_like(dk)
        dv[...] = jnp.zeros_like(dv)
        for i in range(4):
            rows = pl.ds(i * 256, 256)
            q, g = qa[h, rows], grads[h, rows]

            def span(keys, masked):
                k = ka[h, keys]
                score = dot_t(k, q)
                if masked:
                    score = jnp.where(mask, score, MASKED)
                p = jnp.exp(score)
                ds = (p * dot_t(va[h, keys], g)).astype(BF16)
                dk[keys] += dot(ds, q)
                dv[keys] += dot(p.astype(BF16), g)
                return dot_o(k, ds)

            dq = span(rows, True)
            if i:
                dq = dq + span(pl.ds(0, i * 256), False)
            grads[h, rows] = (dq * 0.125).T.astype(BF16)
            for n, hook in hooks_back.items():
                if n % 4 == i:
                    @pl.when(h == n // 4)
                    def _(hook=hook):
                        hook()
        ka[h] = dk[...].astype(BF16)
        va[h] = dv[...].astype(BF16)
        return carry

    lax.fori_loop(0, 4, head_back, 0)
    dfused = v["dfused"]
    for h in (0, 2):
        dfused[:, h * 192:h * 192 + 384] = jnp.concatenate(
            [ref[k, :, :64] for k in (h, h + 1) for ref in (grads, ka, va)], axis=1)

    src[3] = dot_t(pick(pk, "joined_out"), dfused[...]).astype(BF16)
    sum_q = LowSum(src.at[3], got.at[3], *sems(2))
    sum_q.start()
    s4 = GroupSum(*[v[n] for n in ("parts", "near", "sent", "half", "full")], *sems(2))
    s2.finish()
    wide_part(s4, dfused, v["wj"])
    total_q = sum_q.total()
    all_q = LowGather(v["sum_q"], *sems(2))
    all_q.start(total_q)
    sw2_sems = sems(3)
    layer, mine_grad = v["layer"], v["gos"]
    pairs = [(sub(mine_grad, j), sub(back, j), sub(back, j)) for j in range(4)] + [(layer, out, out)]
    sw2 = Swap(pairs, *sw2_sems)
    s3.arrive()
    all_n.wait()
    layer[...] = (mid[...] + bias_n[...] + dot_o(v["sum_n"][:, mine_rows], pick(pk, "down_out")) + s3.total()).astype(BF16)
    sw2.start(4)

    spread = Spread(split, whole, *rest)

    def product(first, count, low, ref):
        for n in range(0, count, 2):
            spread.put(first + n, dot(low[...], ref[:, n * 128:n * 128 + 256]))

    all_d.wait()
    all_u.wait()
    keep(1, xbuf).wait()
    spread.mark(pk[:8, PICKS["hot"][0]:PICKS["hot"][0] + 128])
    product(0, 6, v["low_q"], dfused)
    product(6, 2, v["low_d"], ctx)
    product(8, 8, v["low_u"], dpre)
    product(16, 8, v["low_g"], act)
    product(26, 2, v["sum_d"], v["cols"].at[1])
    product(28, 2, v["sum_u"], v["cols"].at[2])
    product(30, 2, v["sum_n"], v["cols"].at[3])
    all_q.wait()
    product(24, 2, v["sum_q"], v["cols"].at[0])
    spread.start()
    correction = dot_o(total_q, pick(pk, "joined_in"))
    spread.add()
    spread.deal()
    s4.arrive()
    for j in ORDER:
        rows = slice(j * 32, (j + 1) * 32)
        value = dmid[rows] + norm_back(xs[rows].astype(F32), gain1[...], correction[rows] + s4.total(rows))
        mine_grad[rows] = value.astype(BF16)
        sw2.start(j)
    spread.deal_plane()
    for n in range(5):
        sw2.wait(n)
    spread.share()
    spread.finish()
    for thing in (g4, joined, dense, down, up, s3, s4, sw, sw2):
        thing.finish()


SCRATCH = dict(
    lines=((8, 2048), F32), bias=((1, 2048), F32), mine=((16, PICKED), BF16), pk=((16, PICKED), BF16),
    xs=((128, 2048), BF16), xbuf=((1024, 2048), BF16), gbuf=((1024, 2048), BF16), gos=((128, 2048), BF16),
    wj=((2048, 768), BF16), wd=((256, 2048), BF16), wn=((1024, 2048), BF16), wu=((2048, 1024), BF16),
    qa=((4, 1024, 128), BF16), ka=((4, 1024, 128), BF16), va=((4, 1024, 128), BF16), c4=((4, 1024, 128), BF16),
    ctx=((1024, 256), BF16), dctx=((1024, 256), BF16), dfused=((1024, 768), BF16), act=((1024, 1024), BF16),
    dpre=((1024, 1024), BF16), dact=((1024, 1024), F32), mid=((128, 2048), F32), dmid=((128, 2048), F32),
    layer=((128, 2048), BF16), cols=((4, 1024, 256), BF16),
    dk=((1024, 128), F32), dv=((1024, 128), F32), low_src=((4, 16, 1024), BF16), low_got=((4, 8, 16, 128), BF16),
    low_q=((16, 1024), BF16), low_g=((16, 1024), BF16), low_u=((16, 1024), BF16), low_d=((16, 1024), BF16),
    sum_d=((16, 1024), BF16), sum_u=((16, 1024), BF16), sum_n=((16, 1024), BF16), sum_q=((16, 1024), BF16),
    parts=((1024, 2048), BF16), near=((4, 128, 2048), BF16), sent=((3, 128, 2048), BF16), half=((2, 64, 2048), BF16),
    full=((2, 128, 2048), BF16), near2=((4, 128, 2048), BF16), sent2=((3, 128, 2048), BF16),
    half2=((2, 64, 2048), BF16), full2=((2, 128, 2048), BF16))


def block_call(*args):
    outs = [shape(128, 2048), shape(128, 2048), shape(16, 8, 3, 8, 128), shape(8, 16, 8, 8, 128)]
    low = [DMA((8,)), DMA((8,))]
    sums = [DMA((10,)), DMA((10,))]
    gather = GroupGather.SEMS
    kinds = [DMA((8,)), DMA((8,)), DMA((4,)), *Swap.sems(12), *PlaneGather.SEMS * 4, *gather, *low, *gather, *low, *low, *sums,
             *gather, *low, *low, *low, *sums, *gather, *low, *low, *low, *sums, *low, *low, *sums, *low, *Swap.sems(5),
             *Spread.SCRATCH]
    return pl.pallas_call(
        block_kernel, out_shape=outs, in_specs=specs(pltpu.SMEM, *[ANY] * 22), out_specs=specs(*[ANY] * 4),
        scratch_shapes=[VMEM(*s) for s in SCRATCH.values()] + kinds,
        compiler_params=params(1, 60), name="block")(*args)


WIDE = ((6, 0), (2, 6), (8, 8), (8, 16))


def write_kernel(split, whole, back, layer, *outs):
    for ref, (count, first) in zip(outs[:4], WIDE):
        for n in range(count):
            for half in (0, 1):
                k = 2 * (first + n) + half
                ref[0, half * 8:half * 8 + 8, n * 128:n * 128 + 128] = split[k // 3, 0, k % 3].astype(F32)
    for i, ref in enumerate(outs[4:8]):
        for t in range(8):
            for n in range(2):
                for half in (0, 1):
                    at = t * 256 + n * 128
                    ref[0, half * 8:half * 8 + 8, at:at + 128] = whole[t, i * 4 + n * 2 + half, 0].astype(F32)
    outs[8][...] = back[...].astype(F32)
    outs[9][...] = layer[...]


def write_call(split, whole, back, layer):
    widths = [count * 128 for count, _ in WIDE] + [2048] * 4
    rows = pl.BlockSpec((16, 2048), lambda b: (b, 0))
    return pl.pallas_call(
        write_kernel, grid=(8,),
        out_shape=[shape(8, 16, n, dtype=F32) for n in widths] + [shape(128, 2048, dtype=F32), shape(128, 2048)],
        in_specs=[pl.BlockSpec((16, 1, 3, 8, 128), lambda b: (0, b, 0, 0, 0)),
                  pl.BlockSpec((8, 16, 1, 8, 128), lambda b: (0, 0, b, 0, 0)), rows, rows],
        out_specs=[pl.BlockSpec((1, 16, n), lambda b: (b, 0, 0)) for n in widths] + [rows, rows],
        compiler_params=plain(16), name="write")(split, whole, back, layer)


def local(tokens, grad_out, adapter_ids, first_gain, first_shift, joined_weight, joined_bias, dense_weight,
          dense_bias, second_gain, second_shift, up_weight, up_bias, down_weight, down_bias, joined_adapt_in,
          joined_adapt_out, dense_adapt_in, dense_adapt_out, up_adapt_in, up_adapt_out, down_adapt_in,
          down_adapt_out):
    turn = lambda a: jnp.swapaxes(a, 1, 2)
    flat = lambda a: a.reshape(128, a.shape[2])
    vectors = [a.reshape(1, -1) for a in (first_gain, first_shift, second_gain, second_shift, dense_bias, down_bias,
                                          jnp.pad(joined_bias, (0, 256)), up_bias)]
    adapters = dict(joined_in=turn(joined_adapt_in), joined_out=joined_adapt_out, dense_in=turn(dense_adapt_in),
                    dense_out=dense_adapt_out, up_in=turn(up_adapt_in), up_out=up_adapt_out,
                    down_in=turn(down_adapt_in), down_out=down_adapt_out)
    back, layer, split, whole = block_call(
        adapter_ids, tokens, grad_out, *vectors, *[flat(adapters[n]) for n in SETS], joined_weight, dense_weight,
        down_weight, up_weight)
    joined_out, dense_in, up_out, down_in, joined_in, dense_out, up_in, down_out, grad_tokens, layer_out = write_call(
        split, whole, back, layer)
    return (layer_out, grad_tokens, turn(joined_in), joined_out, turn(dense_in), dense_out, turn(up_in), up_out,
            turn(down_in), down_out)


def solution(mesh):
    fine = Mesh(mesh.devices.reshape(2, 4, 2, 2, 4), AXES)
    rows, cols = P(FSDP, TP), P(TP, FSDP)
    tok = P((*FSDP, *TP), None)
    last, middle, one = P(None, None, TP), P(None, TP, None), P(TP)
    return jax.shard_map(
        local, mesh=fine,
        in_specs=(tok, tok, P(FSDP), P(), P(), rows, one, cols, P(), P(), P(), rows, one, cols, P(), P(), last,
                  middle, P(), P(), last, middle, P()),
        out_specs=(tok, tok, P(), last, middle, P(), P(), last, middle, P()), check_vma=False)
```

time: 463 us -> 281 us (0.61)
  waiting for transfers between devices: 57.9 us -> 0 us
  local copies, waits for them, and re-layouts: 43.9 us -> 6.08 us
  blocking collectives: 29.1 us -> 0 us
  matrix products: 16.6 us -> 0 us
  between operations: 15.3 us -> 1.44 us
  starting transfers between devices: 13.3 us -> 0 us
  Pallas kernels: 280 us -> 274 us
    all_gather x2 -> x0, waiting for transfers between devices: 48.5 us -> none  [the longest x1 40.1 us: finish(): every = lax.all_gather(mine, PLANE, axis=0, tiled=False)]
    all_gather x1 -> x0, blocking collectives: 29.1 us -> none  [finish(): onehot = lax.all_gather(hot[:, 0], PLANE, axis=1, tiled=False)]
    unnamed x100 -> x8, local copies, waits for them, and re-layouts: 31.8 us -> 4.8 us
    dot_general x9 -> x0, matrix products: 16.6 us -> none  [the longest x8 12.6 us: dot(): return lax.dot_general(a, b, (dims, ((), ())), preferred_element_type=F32)]
    ppermute x1 -> x0, starting transfers between devices: 13.2 us -> none  [finish(): lax.ppermute(sums[:, :, :3072].astype(BF16), ('c', 'xh'), SWAP).astype(F32)]
    ppermute x1 -> x0, waiting for transfers between devices: 9.41 us -> none  [finish(): lax.ppermute(sums[:, :, :3072].astype(BF16), ('c', 'xh'), SWAP).astype(F32)]
    pallas_call x6 -> x2, Pallas kernels: 280 us -> 274 us  [the longest x1 269 us: block_call(): pl.pallas_call(block_kernel, out_shape=outs, in_specs=specs(pltpu.SMEM, *...]
    transpose x7 -> x0, local copies, waits for them, and re-layouts: 5.84 us -> none  [the longest x5 5.8 us: finish(): whole[:, :, :, i].transpose(1, 2, 0, 3).reshape(8, 16, 2048)]
  transfers between devices with their start and end apart: 3 -> 0, of which waited for: 3 -> 0; matrix products, arithmetic and copies ran while one was open for 1% -> 0% of each run, Pallas kernels for 0% -> 0%
where the time goes in v3:
time: 281 us
  Pallas kernels  274 us (98%)
  local copies, waits for them, and re-layouts  6.08 us (2%)
    pallas_call x1, Pallas kernels, block_call(): pl.pallas_call(block_kernel, out_shape=outs, in_specs=specs(pltpu.SMEM, *...  269 us

profile of v3, /device:TPU:1, one launch (start us, length us, event | category | flops | bytes accessed | tf_op | source)
XLA Modules:
  0.0 281.1 jit_solution(15405081340015030068)
XLA Ops:
  1.3 1.3 pad.4
  2.6 269.1 %block.1 = (bf16[128,2048]{1,0:T(8,128)(2,1)}, bf16[128,2048]{1,0:T(8,128)(2,1)}, bf16[16,8,3,8,128]{4,3,2,1,0:T(8,128)(2,1)}, bf16[8,16,8,8,128]{4,3,2,1,0:T(8,128)(2,1)}) custom-call(s32[1]{0:T(128)S(6)} %copy.33.refs_0_, bf16[128,2048]{1,0:T(8,128)(2,1)} %refs_1_.1, bf16[128,2048]{1,0:T(8,128)(2,1)} %refs_2_.1, f32[1,2048]{1,0:T(1,128)} %bitcast.37, ...), custom_call_target="tpu_custom_call" | custom-call | tf_op jit(solution)/shard_map/block/pallas_call | solution.py:1118
  271.6 0.0 copy-start
  271.7 1.6 copy-done
  273.2 0.0 copy-start.1
  273.2 1.1 copy-done.1
  274.4 0.0 copy-start.2
  274.4 1.0 copy-done.2
  275.4 0.0 copy-start.3
  275.4 1.0 copy-done.3
  276.5 4.5 %write.1 = (f32[8,16,768]{2,1,0:T(8,128)}, f32[8,16,256]{2,1,0:T(8,128)}, f32[8,16,1024]{2,1,0:T(8,128)}, f32[8,16,1024]{2,1,0:T(8,128)}, f32[8,16,2048]{2,1,0:T...) custom-call(bf16[16,8,3,8,128]{4,3,2,1,0:T(8,128)(2,1)S(1)} %copy-do, ...), custom_call_target="tpu_custom_call" | custom-call | tf_op jit(solution)/shard_map/write/pallas_call | solution.py:1146
Async XLA Ops:
  271.6 1.6 copy-start
  273.2 1.1 copy-start.1
  274.4 1.0 copy-start.2
  275.4 1.0 copy-start.3
